TPU v7x, 256 devices: a whole 4x4x8 slice. The times are simulated.
256 devices in a mesh: src: 4 (over y), tgt: 64 (over x, z, core).
Axes of the slice: x: 4, y: 4, z: 8, core: 2. Of those that a mesh axis runs over, the one named last changes fastest.
Arguments:
- source_cells: bfloat16 [32768, 256], P(('src', 'tgt')), may hold values from -16 to 16
- target_cells: bfloat16 [65536, 256], P('tgt'), may hold values from -6 to 6
- mapping: bfloat16 [256, 256], replicated, may hold values from -2 to 2
- source_logmass: bfloat16 [32768], P(('src', 'tgt')), may hold values from -1 to 1
- target_logmass: bfloat16 [65536], P('tgt'), may hold values from -1 to 1
- group_blocks: int32 [4], replicated, may hold values from 16 to 64, as said below
- tile_source: int32 [256, 64], P(('src', 'tgt')), may hold values from -1 to 63, as said below
- tile_target: int32 [256, 64], P(('src', 'tgt')), may hold values from -1 to 7, as said below
Outputs:
- source_potential: float32 [32768], P(('src', 'tgt'))
- target_potential: float32 [65536], P('tgt')
- map_gradient: float32 [256, 256], replicated
Inputs may be any that keep to these rules, and one draw needn't show every extreme that they name: `group_blocks`: one group has all 64 blocks live. `tile_source`: -1 marks an empty slot and empty slots follow the used ones. Only live source blocks appear. No (source block, target block) pair appears twice in a group. Every live source block of a group appears on some device of that group, every target block of a device appears in its used slots, and some device uses all 64 slots. `tile_target`: -1 exactly where tile_source is -1.
All inputs are finite; a program needn't handle non-finite values.
Results may differ from a plain program's by a relative error of at most 0.0003.
The roundings to bfloat16 on the way count: a program that leaves them out, or rounds other values in their place, can miss the bound.
Values may be sent and summed in bfloat16 or wider, within the bound.
No kernel may reach another device: no remote copies, remote signals or barrier semaphores. Data moves between devices by JAX's collectives and lax.ppermute only.
A program may use at most 128 MiB of HBM per device.

v0:
```python
import math

import jax
import jax.numpy as jnp
from jax import lax
from jax.sharding import PartitionSpec as P

TILE = 128
TB_DEV = 8
SINK = 4
ADJ = 4


entropy = 0.5
damping = 0.8
lowest_score = -1e30


def combined_all(value, axis, join):
    pieces = jax.tree.map(lambda part: lax.all_gather(part, axis), value)
    head = jax.tree.map(lambda part: part[0], pieces)
    tail = jax.tree.map(lambda part: part[1:], pieces)
    so_far, _ = lax.scan(lambda so_far, share: (join(so_far, share), None), head, tail)
    return so_far


def merge_pairs(left_pair, right_pair):
    largest = jnp.maximum(left_pair[0], right_pair[0])
    total = left_pair[1] * jnp.exp(left_pair[0] - largest) + right_pair[1] * jnp.exp(
        right_pair[0] - largest
    )
    return (largest, total)


def tile_cost(source_tiles, target_tiles):
    inverse_root = 1.0 / math.sqrt(source_tiles.shape[2])
    product = jnp.einsum(
        "kid,kjd->kij", source_tiles, target_tiles, preferred_element_type=jnp.float32
    )
    return product * -inverse_root


def shards(
    source_cells,
    target_cells,
    mapping,
    source_logmass,
    target_logmass,
    group_blocks,
    tile_source,
    tile_target,
):
    highest = lax.Precision.HIGHEST
    group_index = lax.axis_index("src")
    column_index = lax.axis_index("tgt")
    group_width = lax.axis_size("tgt")
    width = source_cells.shape[1]
    inverse_root = 1.0 / math.sqrt(width)
    mapped = jnp.dot(source_cells, mapping, preferred_element_type=jnp.float32).astype(jnp.bfloat16)
    group_mapped, group_logmass = (
        lax.all_gather(mapped, "tgt", axis=0, tiled=True),
        lax.all_gather(source_logmass, "tgt", axis=0, tiled=True),
    )
    live_slot = tile_source[0] >= 0
    source_index = jnp.where(live_slot, tile_source[0], 0)
    target_index = jnp.where(live_slot, tile_target[0], 0)
    source_tiles = group_mapped.reshape(group_width, TILE, width)[source_index]
    target_tiles = target_cells.reshape(TB_DEV, TILE, width)[target_index]
    source_onehot = (
        (source_index[:, None] == jnp.arange(group_width)[None, :]) & live_slot[:, None]
    ).astype(jnp.float32)
    target_onehot = (
        (target_index[:, None] == jnp.arange(TB_DEV)[None, :]) & live_slot[:, None]
    ).astype(jnp.float32)
    block_live = jnp.arange(group_width) < group_blocks[group_index]
    row_live = jnp.repeat(block_live, TILE)
    logmass_rows = group_logmass.astype(jnp.float32)
    target_logs = target_logmass.astype(jnp.float32)

    def costs():
        return tile_cost(source_tiles, target_tiles)

    target_field = jnp.zeros((target_cells.shape[0],), jnp.float32)
    source_field = jnp.zeros((group_width * TILE,), jnp.float32)
    for sweep_index in range(SINK):
        source_current = costs()
        source_scores = (
            target_field.reshape(TB_DEV, TILE)[target_index][:, None, :] - source_current
        ) / entropy
        source_scores = jnp.where(live_slot[:, None, None], source_scores, lowest_score)
        source_tile_max = jnp.max(source_scores, axis=2)
        source_block_max = jnp.max(
            jnp.where(source_onehot[:, :, None] > 0, source_tile_max[:, None, :], lowest_score),
            axis=0,
        )
        source_tile_total = jnp.sum(
            jnp.exp(source_scores - source_block_max[source_index][:, :, None]), axis=2
        )
        source_block_total = jnp.einsum(
            "kb,ki->bi", source_onehot, source_tile_total, precision=highest
        )
        source_merged_max, source_merged_total = combined_all(
            (source_block_max.reshape(-1), source_block_total.reshape(-1)), "tgt", merge_pairs
        )
        safe_total = jnp.where(row_live, source_merged_total, 1.0)
        safe_max = jnp.where(row_live, source_merged_max, 0.0)
        source_field = jnp.where(
            row_live, entropy * logmass_rows - entropy * (safe_max + jnp.log(safe_total)), 0.0
        )
        target_current = costs()
        scores = (
            source_field.reshape(group_width, TILE)[source_index][:, :, None] - target_current
        ) / entropy
        scores = jnp.where(live_slot[:, None, None], scores, lowest_score)
        tile_max = jnp.max(scores, axis=1)
        block_max = jnp.max(
            jnp.where(target_onehot[:, :, None] > 0, tile_max[:, None, :], lowest_score), axis=0
        )
        tile_total = jnp.sum(jnp.exp(scores - block_max[target_index][:, None, :]), axis=1)
        block_total = jnp.einsum("kb,kj->bj", target_onehot, tile_total, precision=highest)
        merged_max, merged_total = combined_all(
            (block_max.reshape(-1), block_total.reshape(-1)), "src", merge_pairs
        )
        target_field = entropy * target_logs - entropy * (merged_max + jnp.log(merged_total))
    current = costs()
    exponent = (
        source_field.reshape(group_width, TILE)[source_index][:, :, None]
        + target_field.reshape(TB_DEV, TILE)[target_index][:, None, :]
        - current
    ) / entropy
    transport = jnp.where(
        live_slot[:, None, None], jnp.exp(jnp.where(live_slot[:, None, None], exponent, 0.0)), 0.0
    )
    row_partial = jnp.einsum(
        "kb,ki->bi", source_onehot, jnp.sum(transport, axis=2), precision=highest
    ).reshape(-1)
    row_weighted = jnp.einsum(
        "kb,ki->bi", source_onehot, jnp.sum(transport * current, axis=2), precision=highest
    ).reshape(-1)
    row_mass, row_cost = lax.psum((row_partial, row_weighted), "tgt")
    row_cost = row_cost / entropy
    column_partial = jnp.einsum(
        "kb,kj->bj", target_onehot, jnp.sum(transport, axis=1), precision=highest
    ).reshape(-1)
    column_weighted = jnp.einsum(
        "kb,kj->bj", target_onehot, jnp.sum(transport * current, axis=1), precision=highest
    ).reshape(-1)
    column_mass, column_cost = lax.psum((column_partial, column_weighted), "src")
    column_cost = column_cost / entropy
    safe_mass = jnp.where(row_live, row_mass, 1.0)
    target_ratio = jnp.zeros_like(target_field)
    source_ratio = jnp.zeros_like(source_field)
    for adjoint_index in range(ADJ):
        pulled = jnp.einsum(
            "kij,kj->ki",
            transport,
            target_ratio.reshape(TB_DEV, TILE)[target_index],
            precision=highest,
        )
        row_term = lax.psum(
            jnp.einsum("kb,ki->bi", source_onehot, pulled, precision=highest).reshape(-1), "tgt"
        )
        source_ratio = jnp.where(row_live, (row_cost - damping * row_term) / safe_mass, 0.0)
        pushed = jnp.einsum(
            "kij,ki->kj",
            transport,
            source_ratio.reshape(group_width, TILE)[source_index],
            precision=highest,
        )
        column_term = lax.psum(
            jnp.einsum("kb,kj->bj", target_onehot, pushed, precision=highest).reshape(-1), "src"
        )
        target_ratio = (column_cost - damping * column_term) / column_mass
    weights = transport * (
        1.0
        - current / entropy
        + source_ratio.reshape(group_width, TILE)[source_index][:, :, None]
        + target_ratio.reshape(TB_DEV, TILE)[target_index][:, None, :]
    )
    weights = weights.astype(jnp.bfloat16)
    tile_products = jnp.einsum(
        "kij,kjd->kid", weights, target_tiles, preferred_element_type=jnp.float32
    )
    group_cells = lax.all_gather(source_cells, "tgt", axis=0, tiled=True)
    cell_tiles = group_cells.reshape(group_width, TILE, width)[source_index].astype(jnp.float32)
    partial_value = jnp.einsum("kid,kie->de", cell_tiles, tile_products, precision=highest)
    map_gradient = lax.psum(partial_value, ("src", "tgt")) * -inverse_root
    own_potential = lax.dynamic_slice_in_dim(source_field, column_index * TILE, TILE, 0)
    return (own_potential, target_field, map_gradient)


def solution(mesh):
    in_specs = (
        P(("src", "tgt"), None),
        P("tgt", None),
        P(),
        P(("src", "tgt")),
        P("tgt"),
        P(),
        P(("src", "tgt"), None),
        P(("src", "tgt"), None),
    )
    out_specs = (P(("src", "tgt")), P("tgt"), P())
    return jax.shard_map(shards, mesh=mesh, in_specs=in_specs, out_specs=out_specs, check_vma=False)
```

profile of v0, /device:TPU:1, one launch (start us, length us, event | category | flops | bytes accessed | tf_op | source)
XLA Modules:
  0.0 2481.6 jit_solution(11259688128898936272)
XLA Ops:
  13.3 81.3 %all-gather.28.cloned.1.call-done = bf16[8192,256]{1,0:T(8,128)(2,1)} async-done(((bf16[128,256]{1,0:T(8,128)(2,1)}), bf16[8192,256]{1,0:T(8,128)(2,1)}) %all-gather.28.cloned.1.call-update) | async-done | bytes 4194320 | tf_op jit(solution)/shard_map/all_gather | solution.py:61
  114.7 37.7 %all-gather = bf16[64,1,128]{2,1,0:T(2,128)(2,1)S(1)} all-gather(bf16[1,1,128]{2,1,0:T(2,128)(2,1)S(1)} %bitcast.472), channel_id=1, replica_groups=mesh['src'=4,'tgt'=64] {'tgt'}, dimensions={0}, use_global_device_ids=true | all-gather | bytes 16640 | tf_op jit(solution)/shard_map/all_gather | solution.py:62
  153.3 34.7 %all-gather.34.cloned.1.call-done = f32[64,1,8192]{2,1,0:T(1,128)} async-done(((f32[1,1,8192]{2,1,0:T(1,128)}), f32[64,1,8192]{2,1,0:T(1,128)}) %all-gather.34.cloned.1.call-update) | async-done | bytes 2097168 | tf_op jit(solution)/shard_map/all_gather | solution.py:20
  192.0 74.3 %all-gather.32.cloned.1.call-done = f32[64,1,8192]{2,1,0:T(1,128)} async-done(((f32[1,1,8192]{2,1,0:T(1,128)}), f32[64,1,8192]{2,1,0:T(1,128)}) %all-gather.32.cloned.1.call-update) | async-done | bytes 2097168 | tf_op jit(solution)/shard_map/all_gather | solution.py:20
  270.4 71.8 %while.96 = (s32[]{:T(128)}, f32[8192]{0:T(1024)S(1)}, f32[8192]{0:T(1024)S(1)}, f32[63,8192]{1,0:T(8,128)}, f32[63,8192]{1,0:T(8,128)}, /*index=5*/s32[]{:T(128)}) while((s32[]{:T(128)}, f32[8192]{0:T(1024)S(1)}, f32[8192]{0:T(1024)S(1)}, f32[63,8192]{1,0:T(8,128)}, f32[63,8192]{1,0:T(8,128)}, /*index=5*/s32[]{:T(128)}) %tuple.229), condition=%wide.region_4.5_spmd, body=%wide.region_3.4_spmd.sunk | while | flops 49154 | bytes 327753 | solution.py:23
  352.0 9.4 all-gather.4
  382.6 79.6 %all-gather.38.cloned.1.call-done = f32[64,1,8192]{2,1,0:T(1,128)} async-done(((f32[1,1,8192]{2,1,0:T(1,128)}), f32[64,1,8192]{2,1,0:T(1,128)}) %all-gather.38.cloned.1.call-update) | async-done | bytes 2097168 | tf_op jit(solution)/shard_map/all_gather | solution.py:20
  466.3 74.1 %all-gather.36.cloned.1.call-done = f32[64,1,8192]{2,1,0:T(1,128)} async-done(((f32[1,1,8192]{2,1,0:T(1,128)}), f32[64,1,8192]{2,1,0:T(1,128)}) %all-gather.36.cloned.1.call-update) | async-done | bytes 2097168 | tf_op jit(solution)/shard_map/all_gather | solution.py:20
  544.5 71.8 %while.98 = (s32[]{:T(128)}, f32[8192]{0:T(1024)S(1)}, f32[8192]{0:T(1024)S(1)}, f32[63,8192]{1,0:T(8,128)}, f32[63,8192]{1,0:T(8,128)}, /*index=5*/s32[]{:T(128)}) while((s32[]{:T(128)}, f32[8192]{0:T(1024)S(1)}, f32[8192]{0:T(1024)S(1)}, f32[63,8192]{1,0:T(8,128)}, f32[63,8192]{1,0:T(8,128)}, /*index=5*/s32[]{:T(128)}) %tuple.230), condition=%wide.region_14.15_spmd, body=%wide.region_13.14_spmd.sunk | while | flops 49154 | bytes 327753 | solution.py:23
  626.1 9.4 all-gather.8
  657.7 78.3 %all-gather.42.cloned.1.call-done = f32[64,1,8192]{2,1,0:T(1,128)} async-done(((f32[1,1,8192]{2,1,0:T(1,128)}), f32[64,1,8192]{2,1,0:T(1,128)}) %all-gather.42.cloned.1.call-update) | async-done | bytes 2097168 | tf_op jit(solution)/shard_map/all_gather | solution.py:20
  740.1 74.3 %all-gather.40.cloned.1.call-done = f32[64,1,8192]{2,1,0:T(1,128)} async-done(((f32[1,1,8192]{2,1,0:T(1,128)}), f32[64,1,8192]{2,1,0:T(1,128)}) %all-gather.40.cloned.1.call-update) | async-done | bytes 2097168 | tf_op jit(solution)/shard_map/all_gather | solution.py:20
  818.4 72.0 %while.100 = (s32[]{:T(128)}, f32[8192]{0:T(1024)S(1)}, f32[8192]{0:T(1024)S(1)}, f32[63,8192]{1,0:T(8,128)}, f32[63,8192]{1,0:T(8,128)}, /*index=5*/s32[]{:T(128)}) while((s32[]{:T(128)}, f32[8192]{0:T(1024)S(1)}, f32[8192]{0:T(1024)S(1)}, f32[63,8192]{1,0:T(8,128)}, f32[63,8192]{1,0:T(8,128)}, /*index=5*/s32[]{:T(128)}) %tuple.231), condition=%wide.region_24.25_spmd, body=%wide.region_23.24_spmd.sunk | while | flops 49154 | bytes 327753 | solution.py:23
  900.3 9.3 all-gather.12
  935.7 74.6 %all-gather.46.cloned.1.call-done = f32[64,1,8192]{2,1,0:T(1,128)} async-done(((f32[1,1,8192]{2,1,0:T(1,128)}), f32[64,1,8192]{2,1,0:T(1,128)}) %all-gather.46.cloned.1.call-update) | async-done | bytes 2097168 | tf_op jit(solution)/shard_map/all_gather | solution.py:20
  1014.3 74.1 %all-gather.44.cloned.1.call-done = f32[64,1,8192]{2,1,0:T(1,128)} async-done(((f32[1,1,8192]{2,1,0:T(1,128)}), f32[64,1,8192]{2,1,0:T(1,128)}) %all-gather.44.cloned.1.call-update) | async-done | bytes 2097168 | tf_op jit(solution)/shard_map/all_gather | solution.py:20
  1092.5 71.8 %while.102 = (s32[]{:T(128)}, f32[8192]{0:T(1024)S(1)}, f32[8192]{0:T(1024)S(1)}, f32[63,8192]{1,0:T(8,128)}, f32[63,8192]{1,0:T(8,128)}, /*index=5*/s32[]{:T(128)}) while((s32[]{:T(128)}, f32[8192]{0:T(1024)S(1)}, f32[8192]{0:T(1024)S(1)}, f32[63,8192]{1,0:T(8,128)}, f32[63,8192]{1,0:T(8,128)}, /*index=5*/s32[]{:T(128)}) %tuple.232), condition=%wide.region_34.35_spmd, body=%wide.region_33.34_spmd.sunk | while | flops 49154 | bytes 327753 | solution.py:23
  1174.1 9.4 all-gather.16
  1211.3 171.4 %all-reduce.7.cloned.1.call-done = (f32[8192]{0:T(1024)}, f32[8192]{0:T(1024)}, f32[8192]{0:T(1024)}) async-done(((f32[8192]{0:T(1024)}, f32[8192]{0:T(1024)}, f32[8192]{0:T(1024)}), (f32[8192]{0:T(1024)}, f32[8192]{0:T(1024)}, f32[8192]{0:T(1024)})) %all-reduce.7.cloned.1.call-update) | async-done | bytes 98320 | tf_op jit(solution)/shard_map/psum | solution.py:160
  1389.8 13.2 all-reduce.1
  1412.2 245.9 %psum.97 = f32[8192]{0:T(1024)S(1)} all-reduce(f32[8192]{0:T(1024)S(1)} %convolution_bitcast_fusion.3), channel_id=1, replica_groups=mesh['src'=4,'tgt'=64] {'tgt'}, use_global_device_ids=true, to_apply=%region_50.51 | all-reduce | flops 8192 | bytes 65536 | tf_op jit(solution)/shard_map/psum | solution.py:160
  1679.7 247.9 %psum.99 = f32[8192]{0:T(1024)S(1)} all-reduce(f32[8192]{0:T(1024)S(1)} %convolution_bitcast_fusion.2), channel_id=1, replica_groups=mesh['src'=4,'tgt'=64] {'tgt'}, use_global_device_ids=true, to_apply=%region_52.53 | all-reduce | flops 8192 | bytes 65536 | tf_op jit(solution)/shard_map/psum | solution.py:160
  1951.0 248.2 %psum.101 = f32[8192]{0:T(1024)S(1)} all-reduce(f32[8192]{0:T(1024)S(1)} %convolution_bitcast_fusion.1), channel_id=1, replica_groups=mesh['src'=4,'tgt'=64] {'tgt'}, use_global_device_ids=true, to_apply=%region_54.55 | all-reduce | flops 8192 | bytes 65536 | tf_op jit(solution)/shard_map/psum | solution.py:160
  2224.8 247.8 %all-reduce.5.cloned.1.call-done = f32[256,256]{1,0:T(8,128)} async-done(((f32[256,256]{1,0:T(8,128)}), f32[256,256]{1,0:T(8,128)}) %all-reduce.5.cloned.1.call-update) | async-done | bytes 262160 | tf_op jit(solution)/shard_map/psum | solution.py:187
  (773 shorter events, 566.6 us)
Async XLA Ops:
  7.2 87.4 %all-gather.28.cloned.1.call-start = ((), (), s32[]{:S(2)}) async-start(), calls=%async_computation | async-start | bytes 4259840 | tf_op jit(solution)/shard_map/all_gather | solution.py:61
  9.0 178.9 %all-gather.34.cloned.1.call-start = ((), (), s32[]{:S(2)}) async-start(), calls=%async_computation.4 | async-start | bytes 2129920 | tf_op jit(solution)/shard_map/all_gather | solution.py:20
  106.3 7.8 copy-start.15
  106.3 8.4 copy-start.14
  107.0 6.3 copy-start.5
  113.3 153.0 %all-gather.32.cloned.1.call-start = ((), (), s32[]{:S(2)}) async-start(), calls=%async_computation.3 | async-start | bytes 2129920 | tf_op jit(solution)/shard_map/all_gather | solution.py:20
  114.0 348.2 %all-gather.38.cloned.1.call-start = ((), (), s32[]{:S(2)}) async-start(), calls=%async_computation.6 | async-start | bytes 2129920 | tf_op jit(solution)/shard_map/all_gather | solution.py:20
  192.0 78.4 %slice-start.1 = ((f32[64,1,8192]{2,1,0:T(1,128)}), f32[1,1,8192]{2,1,0:T(1,128)S(1)}, s32[]{:S(2)}) async-start(f32[64,1,8192]{2,1,0:T(1,128)} %all-gather.34.cloned.1.call-done), calls=%async_computation.13 | async-start | bytes 65536 | tf_op jit(solution)/shard_map/slice | solution.py:21
  342.9 28.0 %copy-start.11 = (bf16[1024]{0:T(1024)(128)(2,1)S(1)}, bf16[1024]{0:T(1024)(128)(2,1)}, u32[]{:S(2)}) copy-start(bf16[1024]{0:T(1024)(128)(2,1)} %param.28) | copy-start | bytes 6148
  381.9 158.4 %all-gather.36.cloned.1.call-start = ((), (), s32[]{:S(2)}) async-start(), calls=%async_computation.5 | async-start | bytes 2129920 | tf_op jit(solution)/shard_map/all_gather | solution.py:20
  382.5 353.5 %all-gather.42.cloned.1.call-start = ((), (), s32[]{:S(2)}) async-start(), calls=%async_computation.8 | async-start | bytes 2129920 | tf_op jit(solution)/shard_map/all_gather | solution.py:20
  466.2 78.2 %slice-start.5 = ((f32[64,1,8192]{2,1,0:T(1,128)}), f32[1,1,8192]{2,1,0:T(1,128)S(1)}, s32[]{:S(2)}) async-start(f32[64,1,8192]{2,1,0:T(1,128)} %all-gather.38.cloned.1.call-done), calls=%async_computation.17 | async-start | bytes 65536 | tf_op jit(solution)/shard_map/slice | solution.py:21
  655.8 158.6 %all-gather.40.cloned.1.call-start = ((), (), s32[]{:S(2)}) async-start(), calls=%async_computation.7 | async-start | bytes 2129920 | tf_op jit(solution)/shard_map/all_gather | solution.py:20
  656.5 274.2 %all-gather.30.cloned.1.call-start = ((), (), s32[]{:S(2)}) async-start(), calls=%async_computation.1 | async-start | bytes 4259840 | tf_op jit(solution)/shard_map/all_gather | solution.py:184
  657.3 353.0 %all-gather.46.cloned.1.call-start = ((), (), s32[]{:S(2)}) async-start(), calls=%async_computation.10 | async-start | bytes 2129920 | tf_op jit(solution)/shard_map/all_gather | solution.py:20
  740.1 78.4 %slice-start.9 = ((f32[64,1,8192]{2,1,0:T(1,128)}), f32[1,1,8192]{2,1,0:T(1,128)S(1)}, s32[]{:S(2)}) async-start(f32[64,1,8192]{2,1,0:T(1,128)} %all-gather.42.cloned.1.call-done), calls=%async_computation.21 | async-start | bytes 65536 | tf_op jit(solution)/shard_map/slice | solution.py:21
  929.9 158.5 %all-gather.44.cloned.1.call-start = ((), (), s32[]{:S(2)}) async-start(), calls=%async_computation.9 | async-start | bytes 2129920 | tf_op jit(solution)/shard_map/all_gather | solution.py:20
  930.5 452.2 %all-reduce.7.cloned.1.call-start = ((), (), s32[]{:S(2)}) async-start(), calls=%async_computation.11 | async-start | bytes 196608 | tf_op jit(solution)/shard_map/psum | solution.py:160
  1014.3 78.2 %slice-start.13 = ((f32[64,1,8192]{2,1,0:T(1,128)}), f32[1,1,8192]{2,1,0:T(1,128)S(1)}, s32[]{:S(2)}) async-start(f32[64,1,8192]{2,1,0:T(1,128)} %all-gather.46.cloned.1.call-done), calls=%async_computation.25 | async-start | bytes 65536 | tf_op jit(solution)/shard_map/slice | solution.py:21
  1192.8 6.5 copy-start.3
  1210.8 1261.9 %all-reduce.5.cloned.1.call-start = ((), (), s32[]{:S(2)}) async-start(), calls=%async_computation.2 | async-start | bytes 524288 | tf_op jit(solution)/shard_map/psum | solution.py:187
  1384.2 274.0 %copy-start.9 = (f32[8192]{0:T(1024)S(1)}, f32[8192]{0:T(1024)}, u32[]{:S(2)}) copy-start(f32[8192]{0:T(1024)} %get-tuple-element.328) | copy-start | bytes 98308
  1384.2 274.0 %copy-start.10 = (f32[8192]{0:T(1024)S(1)}, f32[8192]{0:T(1024)}, u32[]{:S(2)}) copy-start(f32[8192]{0:T(1024)} %get-tuple-element.329) | copy-start | bytes 98308
  2212.0 262.3 %copy-start.1 = (bf16[1024,256]{1,0:T(8,128)(2,1)S(1)}, bf16[1024,256]{1,0:T(8,128)(2,1)}, u32[]{:S(2)}) copy-start(bf16[1024,256]{1,0:T(8,128)(2,1)} %param.25) | copy-start | bytes 1572868
  (20 other events, 64.6 us)
Sparse Core Ops, SparseCore 0:
  11.4 83.1 all-gather.27
  113.4 74.4 all-gather.33
  191.3 74.9 all-gather.31
  382.0 80.0 all-gather.37
  465.4 74.9 all-gather.35
  655.9 80.0 all-gather.41
  739.4 74.9 all-gather.39
  817.1 76.7 all-gather.29
  930.0 80.1 all-gather.45
  1013.4 74.9 all-gather.43
  1210.9 171.7 all-reduce.6
  2224.4 248.2 all-reduce.4
where the time goes:
time: 2500 us; the launch traced here: 2480 us
  waiting for transfers between devices  1070 us (43%)
  blocking collectives  887 us (35%)
  local copies, waits for them, and re-layouts  337 us (13%)
  other arithmetic  85.4 us (3%)
  matrix products  83.1 us (3%)
    psum x3, blocking collectives, shards(): lax.psum(jnp.einsum('kb,ki->bi', source_onehot, pulled, precision=highest...  742 us
    all_gather x8, waiting for transfers between devices, combined_all(): pieces = jax.tree.map(lambda part: lax.all_gather(part, axis), value)  564 us
    dynamic_slice x264, local copies, waits for them, and re-layouts, combined_all(): lax.scan(lambda so_far, share: (join(so_far, share), None), head, tail)  273 us
    psum x1, waiting for transfers between devices, shards(): map_gradient = lax.psum(partial_value, ('src', 'tgt')) * -inverse_root  248 us
    psum x1, waiting for transfers between devices, shards(): lax.psum(jnp.einsum('kb,ki->bi', source_onehot, pulled, precision=highest...  171 us
    all_gather x1, waiting for transfers between devices, shards(): lax.all_gather(mapped, 'tgt', axis=0, tiled=True)  81.3 us
    all_gather x8, blocking collectives, combined_all(): pieces = jax.tree.map(lambda part: lax.all_gather(part, axis), value)  73.9 us
  transfers between devices with their start and end apart: 12, of which 11 were waited for; matrix products, arithmetic and copies ran while one was open for 5% of the time, Pallas kernels for 0%

commit v1 on v0

v1 whole, which is shorter than its diff:
```python
import functools
import math

import jax
import jax.numpy as jnp
from jax import lax
from jax.experimental import pallas as pl
from jax.experimental.pallas import tpu as pltpu
from jax.sharding import Mesh, PartitionSpec as P

TILE = 128
TB_DEV = 8
TILES = 64
SINK = 4
ADJ = 4
D = 256

entropy = 0.5
damping = 0.8
lowest = -1e30

AXES = ("src", "x", "zh", "zl", "core")
ROW = ("x", "zh")
COL = ("src", "zl", "core")
NA = 16
NB = 32
SLOTS = 4 * TILES
CHUNK = 8
CHUNKS = SLOTS // CHUNK
F32 = jnp.float32


VM = pl.BlockSpec(memory_space=pltpu.VMEM)
SM = pl.BlockSpec(memory_space=pltpu.SMEM)
ANY = pl.BlockSpec(memory_space=pl.ANY)
SHAPE = jax.ShapeDtypeStruct
TILE_BUF = pltpu.VMEM((SLOTS, TILE, TILE), F32)
SEMS = pltpu.SemaphoreType.DMA((CHUNKS,))


def call(kernel, name, ins, outs, scratch, flops=2 << 20, moved=4 << 20, vmem=52):
    in_specs = [spec for spec, _ in ins]
    args = [value for _, value in ins]
    return pl.pallas_call(
        kernel,
        out_shape=[shape for _, shape in outs],
        in_specs=in_specs,
        out_specs=[spec for spec, _ in outs],
        scratch_shapes=scratch,
        name=name,
        cost_estimate=pl.CostEstimate(flops=flops, bytes_accessed=moved, transcendentals=0),
        compiler_params=pltpu.CompilerParams(vmem_limit_bytes=vmem << 20),
    )(*args)


def row_form(block):
    return jnp.sum(block.T, axis=0, keepdims=True)


def column_form(row):
    return jnp.broadcast_to(row, (TILE, TILE)).T


def fold(block):
    return jnp.sum(block.reshape(16, 8, TILE), axis=0)


def fold_max(block):
    return jnp.max(block.reshape(16, 8, TILE), axis=0)


def chunks_of(list_ref):
    return lax.shift_right_logical(list_ref[SLOTS] + (CHUNK - 1), 3)


def copies(source, buffer, sems, count, act):
    def one(c, carry):
        at = pl.ds(pl.multiple_of(c * CHUNK, CHUNK), CHUNK)
        copy = pltpu.make_async_copy(source.at[at], buffer.at[at], sems.at[c])
        getattr(copy, act)()
        return carry

    lax.fori_loop(0, count, one, 0)


def wait_chunk(source, buffer, sems, c):
    at = pl.ds(pl.multiple_of(c * CHUNK, CHUNK), CHUNK)
    pltpu.make_async_copy(source.at[at], buffer.at[at], sems.at[c]).wait()


def each_tile(list_ref, count, body, before=None, after=None):
    def one(c, carry):
        if before is not None:
            before(c)
        for step in range(CHUNK):
            k = c * CHUNK + step
            code = list_ref[k]
            body(k, lax.shift_right_logical(code, 5), jnp.bitwise_and(code, NB - 1))
        if after is not None:
            after(c)
        return carry

    lax.fori_loop(0, count, one, 0)


def write_copies(out_ref, rows, value, first=0):
    for d in range(16):
        out_ref[d, first : first + rows] = value


def live_rows(meta_ref):
    block = 4 * lax.broadcasted_iota(jnp.int32, (NA, TILE), 0) + meta_ref[1]
    return block < meta_ref[0]


def total(recv_ref, first, rows):
    so_far = recv_ref[0, first : first + rows]
    for d in range(1, 16):
        so_far = so_far + recv_ref[d, first : first + rows]
    return so_far


def merged(recv_ref, rows):
    largest = recv_ref[0, 0:rows]
    for d in range(1, 16):
        largest = jnp.maximum(largest, recv_ref[d, 0:rows])
    so_far = jnp.zeros((rows, TILE), F32)
    for d in range(16):
        so_far = so_far + jnp.exp(recv_ref[d, 0:rows] - largest)
    return largest + jnp.log(so_far)


def finish_log(largest, so_far):
    good = so_far > 0
    return jnp.where(good, largest + jnp.log(jnp.where(good, so_far, 1.0)), lowest)


def scores_kernel(
    codes_ref, meta_ref, cells_ref, t0, t1, t23, mapping_ref, mass_ref,
    send_ref, list_ref, x_any,
    tbuf, mapped, xbuf, top, acc, tsem, xsems,
):
    pulls = [
        pltpu.make_async_copy(t0, tbuf.at[0], tsem.at[0]),
        pltpu.make_async_copy(t1, tbuf.at[2], tsem.at[1]),
        pltpu.make_async_copy(t23.at[0], tbuf.at[1], tsem.at[2]),
        pltpu.make_async_copy(t23.at[1], tbuf.at[3], tsem.at[3]),
    ]
    for pull in pulls:
        pull.start()
    part = meta_ref[1]

    def gather(k, n):
        code = codes_ref[k]
        source = lax.shift_right_arithmetic(code, 3)
        take = jnp.logical_and(code >= 0, jnp.bitwise_and(source, 3) == part)
        owner = jnp.bitwise_xor(lax.shift_right_logical(k, 6), part)
        target = owner * TB_DEV + jnp.bitwise_and(code, TB_DEV - 1)
        packed = lax.shift_right_arithmetic(source, 2) * NB + target
        list_ref[n] = jnp.where(take, packed, 0)
        return n + jnp.where(take, 1, 0)

    count = lax.fori_loop(0, SLOTS, gather, 0)

    def clear(k, carry):
        list_ref[k] = 0
        return carry

    lax.fori_loop(count, jnp.minimum(count + CHUNK, SLOTS), clear, 0)
    list_ref[SLOTS] = count
    chunks = chunks_of(list_ref)

    def blank(a, carry):
        top[a] = jnp.full((TILE, TILE), lowest, F32)
        acc[a] = jnp.zeros((TILE, TILE), F32)
        product = jnp.dot(cells_ref[a], mapping_ref[...], preferred_element_type=F32)
        mapped[a] = product.astype(jnp.bfloat16)
        return carry

    lax.fori_loop(0, NA, blank, 0)
    for pull in pulls:
        pull.wait()
    scale = (1.0 / entropy) / math.sqrt(D)

    def product(k, a, b):
        slot = jnp.bitwise_xor(lax.shift_right_logical(b, 3), part)
        rows = pl.ds(pl.multiple_of(jnp.bitwise_and(b, TB_DEV - 1) * TILE, TILE), TILE)
        x = lax.dot_general(
            mapped[a], tbuf[slot, rows, :], (((1,), (1,)), ((), ())), preferred_element_type=F32
        )
        x = jnp.where(k < count, x * scale, lowest)
        xbuf[k] = x
        top[a] = jnp.maximum(top[a], x)

    def push(c):
        at = pl.ds(pl.multiple_of(c * CHUNK, CHUNK), CHUNK)
        pltpu.make_async_copy(xbuf.at[at], x_any.at[at], xsems.at[c]).start()

    each_tile(list_ref, chunks, product, after=push)

    def spread(a, carry):
        top[a] = jnp.broadcast_to(jnp.max(top[a], axis=1, keepdims=True), (TILE, TILE))
        return carry

    lax.fori_loop(0, NA, spread, 0)

    def add(k, a, b):
        acc[a] += jnp.exp(xbuf[k] - top[a])

    each_tile(list_ref, chunks, add)
    for a in range(NA):
        row = finish_log(top[a].T[0:1], row_form(acc[a]))
        for d in range(16):
            send_ref[d, a : a + 1] = row
    tail = jnp.broadcast_to(mass_ref[...], (8, TILE))
    write_copies(send_ref, 8, tail, NA)
    copies(xbuf, x_any, xsems, chunks, "wait")


def first_targets_kernel(
    list_ref, meta_ref, recv_ref, x_any, mass_ref,
    send_ref, u_ref, mass_out,
    xbuf, col, top, acc, sems,
):
    chunks = chunks_of(list_ref)
    copies(x_any, xbuf, sems, chunks, "start")
    for a in range(NA):
        mass_out[a : a + 1] = recv_ref[a, NA : NA + 1]
    u = jnp.where(live_rows(meta_ref), mass_out[...] - merged(recv_ref, NA), 0.0)
    u_ref[...] = u
    for a in range(NA):
        col[a] = column_form(u[a : a + 1])
    top[...] = jnp.full((NB, 8, TILE), lowest, F32)
    acc[...] = jnp.zeros((NB, 8, TILE), F32)

    def largest(k, a, b):
        y = xbuf[k] + col[a]
        xbuf[k] = y
        top[b] = jnp.maximum(top[b], fold_max(y))

    each_tile(list_ref, chunks, largest, before=functools.partial(wait_chunk, x_any, xbuf, sems))
    for b in range(NB):
        top[b] = jnp.broadcast_to(jnp.max(top[b], axis=0, keepdims=True), (8, TILE))

    def add(k, a, b):
        acc[b] += fold(jnp.exp(xbuf[k] - top[b][0:1]))

    each_tile(list_ref, chunks, add)
    for b in range(NB):
        row = finish_log(top[b][0:1], jnp.sum(acc[b], axis=0, keepdims=True))
        for d in range(16):
            send_ref[d, b : b + 1] = row
    write_copies(send_ref, TB_DEV, mass_ref[...], NB)


def kernel_matrix_kernel(
    list_ref, recv_ref, u_ref, x_any,
    send_ref, v_ref, mass_out, k_any,
    xbuf, col, acc, sems, ksems,
):
    chunks = chunks_of(list_ref)
    copies(x_any, xbuf, sems, chunks, "start")
    for p in range(4):
        mass_out[p * TB_DEV : (p + 1) * TB_DEV] = recv_ref[p, NB : NB + TB_DEV]
    v_ref[...] = mass_out[...] - merged(recv_ref, NB)
    for a in range(NA):
        col[a] = column_form(u_ref[a : a + 1])
    acc[...] = jnp.zeros((NA, TILE, TILE), F32)

    def build(k, a, b):
        value = jnp.exp(xbuf[k] + col[a] + v_ref[pl.ds(b, 1)])
        xbuf[k] = value
        acc[a] += value

    def push(c):
        at = pl.ds(pl.multiple_of(c * CHUNK, CHUNK), CHUNK)
        pltpu.make_async_copy(xbuf.at[at], k_any.at[at], ksems.at[c]).start()

    each_tile(
        list_ref, chunks, build, before=functools.partial(wait_chunk, x_any, xbuf, sems), after=push
    )
    for a in range(NA):
        row = row_form(acc[a])
        for d in range(16):
            send_ref[d, a : a + 1] = row
    copies(xbuf, k_any, ksems, chunks, "wait")


def columns_kernel(list_ref, meta_ref, recv_ref, mass_ref, k_any, send_ref, alpha_ref, kbuf, col, acc, sems):
    chunks = chunks_of(list_ref)
    copies(k_any, kbuf, sems, chunks, "start")
    alpha = jnp.where(live_rows(meta_ref), jnp.exp(mass_ref[...]) / total(recv_ref, 0, NA), 1.0)
    alpha_ref[...] = alpha
    for a in range(NA):
        col[a] = column_form(alpha[a : a + 1])
    acc[...] = jnp.zeros((NB, 8, TILE), F32)

    def add(k, a, b):
        acc[b] += fold(kbuf[k] * col[a])

    each_tile(list_ref, chunks, add, before=functools.partial(wait_chunk, k_any, kbuf, sems))
    write_copies(send_ref, NB, jnp.sum(acc[...], axis=1))


def rows_kernel(list_ref, recv_ref, mass_ref, k_any, send_ref, beta_ref, kbuf, acc, sems):
    chunks = chunks_of(list_ref)
    copies(k_any, kbuf, sems, chunks, "start")
    beta_ref[...] = jnp.exp(mass_ref[...]) / total(recv_ref, 0, NB)
    acc[...] = jnp.zeros((NA, TILE, TILE), F32)

    def add(k, a, b):
        acc[a] += kbuf[k] * beta_ref[pl.ds(b, 1)]

    each_tile(list_ref, chunks, add, before=functools.partial(wait_chunk, k_any, kbuf, sems))
    for a in range(NA):
        row = row_form(acc[a])
        for d in range(16):
            send_ref[d, a : a + 1] = row


def masses_kernel(
    list_ref, recv_ref, mass_ref, k_any, x_any,
    send_ref, beta_ref, sum_ref, cost_ref,
    kbuf, xbuf, acc, acc_cost, sems, xsems,
):
    chunks = chunks_of(list_ref)
    copies(k_any, kbuf, sems, chunks, "start")
    copies(x_any, xbuf, xsems, chunks, "start")
    column_sum = total(recv_ref, 0, NB)
    sum_ref[...] = column_sum
    beta_ref[...] = jnp.exp(mass_ref[...]) / column_sum
    acc[...] = jnp.zeros((NA, TILE, TILE), F32)
    acc_cost[...] = jnp.zeros((NA, TILE, TILE), F32)

    def ready(c):
        wait_chunk(k_any, kbuf, sems, c)
        wait_chunk(x_any, xbuf, xsems, c)

    def add(k, a, b):
        plan = kbuf[k] * beta_ref[pl.ds(b, 1)]
        acc[a] += plan
        acc_cost[a] += plan * xbuf[k]

    each_tile(list_ref, chunks, add, before=ready)
    for a in range(NA):
        row = row_form(acc[a])
        cost = row_form(acc_cost[a])
        cost_ref[a : a + 1] = cost
        for d in range(16):
            send_ref[d, a : a + 1] = row
            send_ref[d, NA + a : NA + a + 1] = cost


def first_ratio_kernel(
    list_ref, meta_ref, recv_ref, alpha_ref, k_any, x_any,
    send_ref, sum_ref, s_ref, cost_ref,
    kbuf, xbuf, col, col2, acc, acc2, sems, xsems,
):
    chunks = chunks_of(list_ref)
    copies(k_any, kbuf, sems, chunks, "start")
    copies(x_any, xbuf, xsems, chunks, "start")
    row_sum = total(recv_ref, 0, NA)
    sum_ref[...] = row_sum
    s = jnp.where(live_rows(meta_ref), -total(recv_ref, NA, NA) / row_sum, 0.0)
    s_ref[...] = s
    for a in range(NA):
        col[a] = column_form(alpha_ref[a : a + 1])
        col2[a] = column_form(s[a : a + 1] * damping)
    acc[...] = jnp.zeros((NB, 8, TILE), F32)
    acc2[...] = jnp.zeros((NB, 8, TILE), F32)

    def ready(c):
        wait_chunk(k_any, kbuf, sems, c)
        wait_chunk(x_any, xbuf, xsems, c)

    def add(k, a, b):
        plan = kbuf[k] * col[a]
        acc[b] += fold(plan * xbuf[k])
        acc2[b] += fold(plan * (xbuf[k] + col2[a]))

    each_tile(list_ref, chunks, add, before=ready)
    cost_ref[...] = jnp.sum(acc[...], axis=1)
    write_copies(send_ref, NB, jnp.sum(acc2[...], axis=1))


def pull_kernel(
    list_ref, recv_ref, sum_ref, beta_ref, cost_ref, k_any,
    send_ref,
    kbuf, acc, weight, sems,
):
    chunks = chunks_of(list_ref)
    copies(k_any, kbuf, sems, chunks, "start")
    t = -total(recv_ref, 0, NB) / sum_ref[...]
    weight[...] = beta_ref[...] * t * damping
    acc[...] = jnp.zeros((NA, TILE, TILE), F32)

    def add(k, a, b):
        acc[a] += kbuf[k] * weight[pl.ds(b, 1)]

    each_tile(list_ref, chunks, add, before=functools.partial(wait_chunk, k_any, kbuf, sems))
    for a in range(NA):
        row = cost_ref[a : a + 1] + row_form(acc[a])
        for d in range(16):
            send_ref[d, a : a + 1] = row


def push_kernel(
    list_ref, meta_ref, recv_ref, sum_ref, alpha_ref, cost_ref, k_any,
    send_ref, s_ref,
    kbuf, col, acc, sems,
):
    chunks = chunks_of(list_ref)
    copies(k_any, kbuf, sems, chunks, "start")
    s = jnp.where(live_rows(meta_ref), -total(recv_ref, 0, NA) / sum_ref[...], 0.0)
    s_ref[...] = s
    weight = alpha_ref[...] * s * damping
    for a in range(NA):
        col[a] = column_form(weight[a : a + 1])
    acc[...] = jnp.zeros((NB, 8, TILE), F32)

    def add(k, a, b):
        acc[b] += fold(kbuf[k] * col[a])

    each_tile(list_ref, chunks, add, before=functools.partial(wait_chunk, k_any, kbuf, sems))
    write_copies(send_ref, NB, cost_ref[...] + jnp.sum(acc[...], axis=1))


def gradient_kernel(
    list_ref, meta_ref, recv_ref, sum_ref, beta_ref, alpha_ref, s_ref, cells_ref, t0, t1, t23, k_any, x_any,
    g_ref,
    tbuf, kbuf, xbuf, col, col2, trow, prod, tsem, sems, xsems,
):
    chunks = chunks_of(list_ref)
    pulls = [
        pltpu.make_async_copy(t0, tbuf.at[0], tsem.at[0]),
        pltpu.make_async_copy(t1, tbuf.at[2], tsem.at[1]),
        pltpu.make_async_copy(t23.at[0], tbuf.at[1], tsem.at[2]),
        pltpu.make_async_copy(t23.at[1], tbuf.at[3], tsem.at[3]),
    ]
    for pull in pulls:
        pull.start()
    copies(k_any, kbuf, sems, chunks, "start")
    copies(x_any, xbuf, xsems, chunks, "start")
    part = meta_ref[1]
    trow[...] = -total(recv_ref, 0, NB) / sum_ref[...]
    for a in range(NA):
        col[a] = column_form(alpha_ref[a : a + 1])
        col2[a] = column_form(1.0 + s_ref[a : a + 1])
    prod[...] = jnp.zeros((NA, TILE, D), F32)
    for pull in pulls:
        pull.wait()

    def ready(c):
        wait_chunk(k_any, kbuf, sems, c)
        wait_chunk(x_any, xbuf, xsems, c)

    def add(k, a, b):
        slot = jnp.bitwise_xor(lax.shift_right_logical(b, 3), part)
        rows = pl.ds(pl.multiple_of(jnp.bitwise_and(b, TB_DEV - 1) * TILE, TILE), TILE)
        plan = kbuf[k] * col[a] * beta_ref[pl.ds(b, 1)]
        weights = plan * (xbuf[k] + col2[a] + trow[pl.ds(b, 1)])
        prod[a] += jnp.dot(
            weights.astype(jnp.bfloat16), tbuf[slot, rows, :], preferred_element_type=F32
        )

    each_tile(list_ref, chunks, add, before=ready)
    contract = (((0,), (0,)), ((), ()))

    def outer(a, so_far):
        value = prod[a]
        high = value.astype(jnp.bfloat16)
        rest = value - high.astype(F32)
        middle = rest.astype(jnp.bfloat16)
        low = (rest - middle.astype(F32)).astype(jnp.bfloat16)
        cells = cells_ref[a]
        for piece in (low, middle, high):
            so_far = so_far + lax.dot_general(cells, piece, contract, preferred_element_type=F32)
        return so_far

    g = lax.fori_loop(0, NA, outer, jnp.zeros((D, D), F32))
    g_ref[...] = g * (-1.0 / math.sqrt(D))


def swap(value, axis):
    return lax.ppermute(value, axis, [(0, 1), (1, 0)])


def shards(
    source_cells,
    target_cells,
    mapping,
    source_logmass,
    target_logmass,
    group_blocks,
    tile_source,
    tile_target,
):
    part = lax.axis_index("zl") * 2 + lax.axis_index("core")
    owner = lax.axis_index("x") * 4 + lax.axis_index("zh")
    live = group_blocks[lax.axis_index("src")]
    meta = jnp.stack([live, part]).astype(jnp.int32)

    codes = jnp.where(tile_source >= 0, tile_source * TB_DEV + tile_target, -1)
    codes_zl = swap(codes, "zl")
    codes_core = swap(jnp.concatenate([codes, codes_zl], axis=1), "core")
    codes_all = jnp.concatenate([codes, codes_core[:, :TILES], codes_zl, codes_core[:, TILES:]], axis=1)
    t0 = target_cells
    t1 = swap(target_cells, "zl")
    t23 = swap(jnp.stack([t0, t1]), "core")
    cells = lax.all_to_all(jnp.broadcast_to(source_cells[None], (16, TILE, D)), ROW, 0, 0)

    def row_exchange(value):
        return lax.all_to_all(value, ROW, 0, 0)

    def col_exchange(value):
        return lax.all_to_all(value, COL, 0, 0)

    rows_to = (VM, SHAPE((16, NA, TILE), F32))
    cols_to = (VM, SHAPE((16, NB, TILE), F32))
    rows_state = (VM, SHAPE((NA, TILE), F32))
    cols_state = (VM, SHAPE((NB, TILE), F32))
    tiles = (ANY, SHAPE((SLOTS, TILE, TILE), F32))
    row_blocks = pltpu.VMEM((NA, TILE, TILE), F32)
    col_rows = pltpu.VMEM((NB, 8, TILE), F32)

    send, tile_list, x = call(
        scores_kernel,
        "scores",
        [
            (SM, codes_all.reshape(SLOTS)), (SM, meta), (VM, cells), (ANY, t0), (ANY, t1), (ANY, t23),
            (VM, mapping), (VM, source_logmass.astype(F32).reshape(1, TILE)),
        ],
        [(VM, SHAPE((16, NA + 8, TILE), F32)), (SM, SHAPE((SLOTS + 8,), jnp.int32)), tiles],
        [
            pltpu.VMEM((4, TB_DEV * TILE, D), jnp.bfloat16), pltpu.VMEM((NA, TILE, D), jnp.bfloat16),
            TILE_BUF, row_blocks, row_blocks, pltpu.SemaphoreType.DMA((4,)), SEMS,
        ],
        moved=8 << 20,
    )
    recv = row_exchange(send)
    send, u, source_mass = call(
        first_targets_kernel,
        "first_targets",
        [
            (SM, tile_list), (SM, meta), (VM, recv), (ANY, x),
            (VM, target_logmass.astype(F32).reshape(TB_DEV, TILE)),
        ],
        [(VM, SHAPE((16, NB + TB_DEV, TILE), F32)), rows_state, rows_state],
        [TILE_BUF, row_blocks, col_rows, col_rows, SEMS],
    )
    recv = col_exchange(send)
    send, v, target_mass, k = call(
        kernel_matrix_kernel,
        "kernel_matrix",
        [(SM, tile_list), (VM, recv), (VM, u), (ANY, x)],
        [rows_to, cols_state, cols_state, tiles],
        [TILE_BUF, row_blocks, row_blocks, SEMS, SEMS],
        moved=8 << 20,
    )
    for sweep in range(1, SINK):
        recv = row_exchange(send)
        send, alpha = call(
            columns_kernel,
            "columns",
            [(SM, tile_list), (SM, meta), (VM, recv), (VM, source_mass), (ANY, k)],
            [cols_to, rows_state],
            [TILE_BUF, row_blocks, col_rows, SEMS],
        )
        recv = col_exchange(send)
        if sweep < SINK - 1:
            send, _ = call(
                rows_kernel,
                "rows",
                [(SM, tile_list), (VM, recv), (VM, target_mass), (ANY, k)],
                [rows_to, cols_state],
                [TILE_BUF, row_blocks, SEMS],
            )
    send, beta, column_sum, row_cost = call(
        masses_kernel,
        "masses",
        [(SM, tile_list), (VM, recv), (VM, target_mass), (ANY, k), (ANY, x)],
        [(VM, SHAPE((16, 2 * NA, TILE), F32)), cols_state, cols_state, rows_state],
        [TILE_BUF, TILE_BUF, row_blocks, row_blocks, SEMS, SEMS],
        moved=8 << 20,
    )
    recv = row_exchange(send)
    send, row_sum, s, column_cost = call(
        first_ratio_kernel,
        "first_ratio",
        [(SM, tile_list), (SM, meta), (VM, recv), (VM, alpha), (ANY, k), (ANY, x)],
        [cols_to, rows_state, rows_state, cols_state],
        [TILE_BUF, TILE_BUF, row_blocks, row_blocks, col_rows, col_rows, SEMS, SEMS],
        moved=8 << 20,
    )
    recv = col_exchange(send)
    for _ in range(1, ADJ):
        (send,) = call(
            pull_kernel,
            "pull",
            [(SM, tile_list), (VM, recv), (VM, column_sum), (VM, beta), (VM, row_cost), (ANY, k)],
            [rows_to],
            [TILE_BUF, row_blocks, pltpu.VMEM((NB, TILE), F32), SEMS],
        )
        recv = row_exchange(send)
        send, s = call(
            push_kernel,
            "push",
            [
                (SM, tile_list), (SM, meta), (VM, recv), (VM, row_sum), (VM, alpha),
                (VM, column_cost), (ANY, k),
            ],
            [cols_to, rows_state],
            [TILE_BUF, row_blocks, col_rows, SEMS],
        )
        recv = col_exchange(send)
    (gradient,) = call(
        gradient_kernel,
        "gradient",
        [
            (SM, tile_list), (SM, meta), (VM, recv), (VM, column_sum), (VM, beta), (VM, alpha), (VM, s),
            (VM, cells), (ANY, t0), (ANY, t1), (ANY, t23), (ANY, k), (ANY, x),
        ],
        [(VM, SHAPE((D, D), F32))],
        [
            pltpu.VMEM((4, TB_DEV * TILE, D), jnp.bfloat16), TILE_BUF, TILE_BUF, row_blocks, row_blocks,
            pltpu.VMEM((NB, TILE), F32), pltpu.VMEM((NA, TILE, D), F32),
            pltpu.SemaphoreType.DMA((4,)), SEMS, SEMS,
        ],
        moved=10 << 20,
    )
    piece = jnp.sum(col_exchange(gradient.reshape(16, 16, D)), axis=0)
    piece = jnp.sum(row_exchange(jnp.broadcast_to(piece[None], (16, 16, D))), axis=0)
    map_gradient = col_exchange_gather(piece).reshape(D, D)

    source_field = entropy * (u + jnp.log(alpha))
    own_source = lax.dynamic_slice_in_dim(source_field, owner, 1, 0).reshape(TILE)
    target_field = entropy * (v + jnp.log(beta))
    own_target = lax.dynamic_slice_in_dim(target_field, part * TB_DEV, TB_DEV, 0)
    return (own_source, own_target.reshape(TB_DEV * TILE), map_gradient)


def col_exchange_gather(piece):
    every = lax.all_to_all(jnp.broadcast_to(piece[None], (16, 16, D)), COL, 0, 0)
    return every


def solution(mesh):
    grid = Mesh(mesh.devices.reshape(4, 4, 4, 2, 2), AXES)
    tgt = ("x", "zh", "zl", "core")
    both = ("src", *tgt)
    in_specs = (
        P(both, None),
        P(tgt, None),
        P(),
        P(both),
        P(tgt),
        P(),
        P(both, None),
        P(both, None),
    )
    out_specs = (P(both), P(tgt), P())
    return jax.shard_map(shards, mesh=grid, in_specs=in_specs, out_specs=out_specs, check_vma=False)
```

time: 2500 us -> 392 us (0.16)
  waiting for transfers between devices: 1070 us -> 50.3 us
  blocking collectives: 887 us -> 224 us
  local copies, waits for them, and re-layouts: 337 us -> 7.93 us
  matrix products: 83.1 us -> 0 us
  other arithmetic: 85.4 us -> 6.16 us
  Pallas kernels: 0 us -> 71.2 us
  starting transfers between devices: 1.27 us -> 30.7 us
    psum x7 -> x0, blocking collectives: 775 us -> none  [the longest x3 742 us: shards(): lax.psum(jnp.einsum('kb,ki->bi', source_onehot, pulled, precision=highest...]
    all_gather x10 -> x0, waiting for transfers between devices: 645 us -> none  [the longest x8 564 us: combined_all(): pieces = jax.tree.map(lambda part: lax.all_gather(part, axis), value)]
    psum x2 -> x0, waiting for transfers between devices: 419 us -> none  [the longest x1 248 us: shards(): map_gradient = lax.psum(partial_value, ('src', 'tgt')) * -inverse_root]
    dynamic_slice x266 -> x1, local copies, waits for them, and re-layouts: 274 us -> 1.24 us  [shards(): live = group_blocks[lax.axis_index('src')]]
    all_to_all x0 -> x17, blocking collectives: none -> 224 us  [the longest x9 117 us: col_exchange(): return lax.all_to_all(value, COL, 0, 0)]
    all_gather x9 -> x0, blocking collectives: 112 us -> none  [the longest x8 73.9 us: combined_all(): pieces = jax.tree.map(lambda part: lax.all_gather(part, axis), value)]
    dot_general x32 -> x0, matrix products: 83.1 us -> none  [the longest x4 31.4 us: shards(): jnp.einsum('kij,kj->ki', transport, target_ratio.reshape(TB_DEV, TILE)[ta...]
    pallas_call x0 -> x17, Pallas kernels: none -> 71.2 us  [call(): pl.pallas_call(kernel, out_shape=[shape for _, shape in outs], in_specs=i...]
  transfers between devices with their start and end apart: 12 -> 7, of which waited for: 11 -> 4; matrix products, arithmetic and copies ran while one was open for 5% -> 2% of each run, Pallas kernels for 0% -> 0%
where the time goes in v1:
time: 392 us; the launch traced here: 391 us
  blocking collectives  224 us (57%)
  Pallas kernels  71.2 us (18%)
  waiting for transfers between devices  50.3 us (13%)
  starting transfers between devices  30.7 us (8%)
  local copies, waits for them, and re-layouts  7.93 us (2%)
  other arithmetic  6.16 us (2%)
    all_to_all x9, blocking collectives, col_exchange(): return lax.all_to_all(value, COL, 0, 0)  117 us
    all_to_all x8, blocking collectives, row_exchange(): return lax.all_to_all(value, ROW, 0, 0)  106 us
    pallas_call x17, Pallas kernels, call(): pl.pallas_call(kernel, out_shape=[shape for _, shape in outs], in_specs=i...  71.2 us
    ppermute x4, waiting for transfers between devices, swap(): return lax.ppermute(value, axis, [(0, 1), (1, 0)])  34 us
    all_to_all x1, starting transfers between devices, shards(): lax.all_to_all(jnp.broadcast_to(source_cells[None], (16, TILE, D)), ROW,...  11.6 us
    all_to_all x1, waiting for transfers between devices, row_exchange(): return lax.all_to_all(value, ROW, 0, 0)  10.2 us
    all_to_all x1, starting transfers between devices, row_exchange(): return lax.all_to_all(value, ROW, 0, 0)  8.67 us
  transfers between devices with their start and end apart: 7, of which 4 were waited for; matrix products, arithmetic and copies ran while one was open for 2% of the time, Pallas kernels for 0%

profile of v1, /device:TPU:1, one launch (start us, length us, event | category | flops | bytes accessed | tf_op | source)
XLA Modules:
  0.0 390.9 jit_solution(16804267729534108111)
XLA Ops:
  2.6 11.6 %all-to-all-start = ((bf16[16,128,256]{2,1,0:T(8,128)(2,1)}), bf16[16,128,256]{2,1,0:T(8,128)(2,1)S(1)}, u32[]{:S(2)}, u32[]{:S(2)}) async-start(bf16[16,128,256]{2,1,0:T(8,128)(2,1)} %broadcast_in_dim.11), calls=%async_computation | async-start | bytes 2097152 | tf_op jit(solution)/shard_map/all_to_all | solution.py:510
  15.0 33.9 %collective-permute-done.2.t1 = bf16[1024,256]{1,0:T(8,128)(2,1)S(1)} collective-permute-done((bf16[1024,256]{1,0:T(8,128)(2,1)}, bf16[1024,256]{1,0:T(8,128)(2,1)S(1)}, u32[]{:S(2)}, u32[]{:S(2)}) %collective-permute-start.2) | collective-permute-done | bytes 524320 | tf_op jit(solution)/shard_map/ppermute | solution.py:485
  61.0 11.6 %scores.1 = (f32[16,24,128]{2,1,0:T(8,128)}, s32[264]{0:T(512)S(1)}, f32[256,128,128]{2,1,0:T(8,128)}) custom-call(s32[256]{0:T(256)S(1)} %bitcast.19, s32[2]{0:T(128)S(1)} %pad_add_fusion.2.meta_ref, bf16[16,128,256]{2,1,0:T(8,128)(2,1)} %copy-done.3, bf16[1024,256]{1,0:T(8,128)(2,1)S(1)} %copy-done, bf16[1024,256]{1,0:T(8,128)(2,1)S(1)} %collective-permute-done.2.t1, ...), custom_call_target="tpu_custom_call" | custom-call | flops 2097152 | bytes 8388608 | tf_op jit(solution)/shard_map/scores/pallas_call | solution.py:44
  72.6 8.7 %all-to-all-start.1 = ((f32[16,24,128]{2,1,0:T(8,128)}), f32[16,24,128]{2,1,0:T(8,128)S(1)}, u32[]{:S(2)}, u32[]{:S(2)}) async-start(f32[16,24,128]{2,1,0:T(8,128)} %get-tuple-element.31), calls=%async_computation.1 | async-start | bytes 393216 | tf_op jit(solution)/shard_map/all_to_all | solution.py:513
  82.0 10.2 %all-to-all-done.1.recv_ref = f32[16,24,128]{2,1,0:T(8,128)S(1)} async-done(((f32[16,24,128]{2,1,0:T(8,128)}), f32[16,24,128]{2,1,0:T(8,128)S(1)}, u32[]{:S(2)}, u32[]{:S(2)}) %all-to-all-start.1) | async-done | bytes 196640 | tf_op jit(solution)/shard_map/all_to_all | solution.py:513
  95.4 16.5 %all_to_all.100.recv_ref = f32[16,40,128]{2,1,0:T(8,128)S(1)} all-to-all(f32[16,40,128]{2,1,0:T(8,128)S(1)} %get-tuple-element.34), channel_id=1, replica_groups=mesh['src'=4,'x'=4,'zh'=4,'zl'=2,'core'=2] {'src','zl','core'}, dimensions={0} | all-to-all | bytes 655360 | tf_op jit(solution)/shard_map/all_to_all | solution.py:516
  115.7 13.1 %all_to_all.101.recv_ref = f32[16,16,128]{2,1,0:T(8,128)S(1)} all-to-all(f32[16,16,128]{2,1,0:T(8,128)S(1)} %get-tuple-element.35), channel_id=1, replica_groups=mesh['src'=4,'x'=4,'zh'=4,'zl'=2,'core'=2] {'x','zh'}, dimensions={0} | all-to-all | bytes 262144 | tf_op jit(solution)/shard_map/all_to_all | solution.py:513
  132.0 12.4 %all_to_all.102.recv_ref = f32[16,32,128]{2,1,0:T(8,128)S(1)} all-to-all(f32[16,32,128]{2,1,0:T(8,128)S(1)} %get-tuple-element.38), channel_id=1, replica_groups=mesh['src'=4,'x'=4,'zh'=4,'zl'=2,'core'=2] {'src','zl','core'}, dimensions={0} | all-to-all | bytes 524288 | tf_op jit(solution)/shard_map/all_to_all | solution.py:516
  147.7 12.9 %all_to_all.103.recv_ref = f32[16,16,128]{2,1,0:T(8,128)S(1)} all-to-all(f32[16,16,128]{2,1,0:T(8,128)S(1)} %get-tuple-element.40), channel_id=1, replica_groups=mesh['src'=4,'x'=4,'zh'=4,'zl'=2,'core'=2] {'x','zh'}, dimensions={0} | all-to-all | bytes 262144 | tf_op jit(solution)/shard_map/all_to_all | solution.py:513
  163.8 12.6 %all_to_all.104.recv_ref = f32[16,32,128]{2,1,0:T(8,128)S(1)} all-to-all(f32[16,32,128]{2,1,0:T(8,128)S(1)} %get-tuple-element.41), channel_id=1, replica_groups=mesh['src'=4,'x'=4,'zh'=4,'zl'=2,'core'=2] {'src','zl','core'}, dimensions={0} | all-to-all | bytes 524288 | tf_op jit(solution)/shard_map/all_to_all | solution.py:516
  179.6 12.9 %all_to_all.105.recv_ref = f32[16,16,128]{2,1,0:T(8,128)S(1)} all-to-all(f32[16,16,128]{2,1,0:T(8,128)S(1)} %get-tuple-element.42), channel_id=1, replica_groups=mesh['src'=4,'x'=4,'zh'=4,'zl'=2,'core'=2] {'x','zh'}, dimensions={0} | all-to-all | bytes 262144 | tf_op jit(solution)/shard_map/all_to_all | solution.py:513
  195.1 12.4 %all_to_all.106.recv_ref = f32[16,32,128]{2,1,0:T(8,128)S(1)} all-to-all(f32[16,32,128]{2,1,0:T(8,128)S(1)} %get-tuple-element.45), channel_id=1, replica_groups=mesh['src'=4,'x'=4,'zh'=4,'zl'=2,'core'=2] {'src','zl','core'}, dimensions={0} | all-to-all | bytes 524288 | tf_op jit(solution)/shard_map/all_to_all | solution.py:516
  212.0 14.3 %all_to_all.107.recv_ref = f32[16,32,128]{2,1,0:T(8,128)S(1)} all-to-all(f32[16,32,128]{2,1,0:T(8,128)S(1)} %get-tuple-element.47), channel_id=1, replica_groups=mesh['src'=4,'x'=4,'zh'=4,'zl'=2,'core'=2] {'x','zh'}, dimensions={0} | all-to-all | bytes 524288 | tf_op jit(solution)/shard_map/all_to_all | solution.py:513
  230.8 14.3 %all_to_all.108.recv_ref = f32[16,32,128]{2,1,0:T(8,128)S(1)} all-to-all(f32[16,32,128]{2,1,0:T(8,128)S(1)} %get-tuple-element.48), channel_id=1, replica_groups=mesh['src'=4,'x'=4,'zh'=4,'zl'=2,'core'=2] {'src','zl','core'}, dimensions={0} | all-to-all | bytes 524288 | tf_op jit(solution)/shard_map/all_to_all | solution.py:516
  248.0 13.4 %all_to_all.109.recv_ref = f32[16,16,128]{2,1,0:T(8,128)S(1)} all-to-all(f32[16,16,128]{2,1,0:T(8,128)S(1)} %pull.3), channel_id=1, replica_groups=mesh['src'=4,'x'=4,'zh'=4,'zl'=2,'core'=2] {'x','zh'}, dimensions={0} | all-to-all | bytes 262144 | tf_op jit(solution)/shard_map/all_to_all | solution.py:513
  264.6 12.6 %all_to_all.110.recv_ref = f32[16,32,128]{2,1,0:T(8,128)S(1)} all-to-all(f32[16,32,128]{2,1,0:T(8,128)S(1)} %get-tuple-element.53), channel_id=1, replica_groups=mesh['src'=4,'x'=4,'zh'=4,'zl'=2,'core'=2] {'src','zl','core'}, dimensions={0} | all-to-all | bytes 524288 | tf_op jit(solution)/shard_map/all_to_all | solution.py:516
  280.1 12.9 %all_to_all.111.recv_ref = f32[16,16,128]{2,1,0:T(8,128)S(1)} all-to-all(f32[16,16,128]{2,1,0:T(8,128)S(1)} %pull.4), channel_id=1, replica_groups=mesh['src'=4,'x'=4,'zh'=4,'zl'=2,'core'=2] {'x','zh'}, dimensions={0} | all-to-all | bytes 262144 | tf_op jit(solution)/shard_map/all_to_all | solution.py:513
  296.2 12.4 %all_to_all.112.recv_ref = f32[16,32,128]{2,1,0:T(8,128)S(1)} all-to-all(f32[16,32,128]{2,1,0:T(8,128)S(1)} %get-tuple-element.54), channel_id=1, replica_groups=mesh['src'=4,'x'=4,'zh'=4,'zl'=2,'core'=2] {'src','zl','core'}, dimensions={0} | all-to-all | bytes 524288 | tf_op jit(solution)/shard_map/all_to_all | solution.py:516
  311.6 12.8 %all_to_all.113.recv_ref = f32[16,16,128]{2,1,0:T(8,128)S(1)} all-to-all(f32[16,16,128]{2,1,0:T(8,128)S(1)} %pull.5), channel_id=1, replica_groups=mesh['src'=4,'x'=4,'zh'=4,'zl'=2,'core'=2] {'x','zh'}, dimensions={0} | all-to-all | bytes 262144 | tf_op jit(solution)/shard_map/all_to_all | solution.py:513
  327.1 12.6 %all_to_all.114.recv_ref = f32[16,32,128]{2,1,0:T(8,128)S(1)} all-to-all(f32[16,32,128]{2,1,0:T(8,128)S(1)} %get-tuple-element.55), channel_id=1, replica_groups=mesh['src'=4,'x'=4,'zh'=4,'zl'=2,'core'=2] {'src','zl','core'}, dimensions={0} | all-to-all | bytes 524288 | tf_op jit(solution)/shard_map/all_to_all | solution.py:516
  339.7 10.4 %gradient.1 = f32[256,256]{1,0:T(8,128)S(1)} custom-call(s32[264]{0:T(512)S(1)} %get-tuple-element.30.list_ref, s32[2]{0:T(128)S(1)} %pad_add_fusion.2.meta_ref, f32[16,32,128]{2,1,0:T(8,128)S(1)} %all_to_all.114.recv_ref, f32[32,128]{1,0:T(8,128)S(1)} %get-tuple-element.49.sum_ref, f32[32,128]{1,0:T(8,128)S(1)} %get-tuple-element.46.beta_ref, ...), custom_call_target="tpu_custom_call" | custom-call | flops 2097152 | bytes 10485760 | tf_op jit(solution)/shard_map/gradient/pallas_call | solution.py:44
  350.1 11.5 %all_to_all.115 = f32[16,16,256]{2,1,0:T(8,128)S(1)} all-to-all(f32[16,16,256]{2,1,0:T(8,128)S(1)} %bitcast.18), channel_id=1, replica_groups=mesh['src'=4,'x'=4,'zh'=4,'zl'=2,'core'=2] {'src','zl','core'}, dimensions={0} | all-to-all | bytes 524288 | tf_op jit(solution)/shard_map/all_to_all | solution.py:516
  361.7 14.1 %all_to_all.116 = f32[16,16,256]{2,1,0:T(8,128)S(1)} all-to-all(f32[16,16,256]{2,1,0:T(8,128)S(1)} %broadcast_in_dim.12), channel_id=1, replica_groups=mesh['src'=4,'x'=4,'zh'=4,'zl'=2,'core'=2] {'x','zh'}, dimensions={0} | all-to-all | bytes 524288 | tf_op jit(solution)/shard_map/all_to_all | solution.py:513
  376.5 6.5 %all-to-all-start.19 = ((f32[16,16,256]{2,1,0:T(8,128)}), f32[16,16,256]{2,1,0:T(8,128)S(1)}, u32[]{:S(2)}, u32[]{:S(2)}) async-start(f32[16,16,256]{2,1,0:T(8,128)} %broadcast_in_dim.13), calls=%async_computation.19 | async-start | bytes 524288 | tf_op jit(solution)/shard_map/all_to_all | solution.py:643
  (51 shorter events, 73.5 us)
Async XLA Ops:
  2.6 55.2 %all-to-all-start = ((bf16[16,128,256]{2,1,0:T(8,128)(2,1)}), bf16[16,128,256]{2,1,0:T(8,128)(2,1)S(1)}, u32[]{:S(2)}, u32[]{:S(2)}) async-start(bf16[16,128,256]{2,1,0:T(8,128)(2,1)} %broadcast_in_dim.11), calls=%async_computation | async-start | bytes 2097152 | tf_op jit(solution)/shard_map/all_to_all | solution.py:510
  14.2 34.7 %collective-permute-start.2 = (bf16[1024,256]{1,0:T(8,128)(2,1)}, bf16[1024,256]{1,0:T(8,128)(2,1)S(1)}, u32[]{:S(2)}, u32[]{:S(2)}) collective-permute-start(bf16[1024,256]{1,0:T(8,128)(2,1)} %t0.3), channel_id=1, source_target_pairs={{0,2},{2,0},{1,3},{3,1},{4,6},{6,4},{5,7},{7,5},{8,10},{10,8},{9,1... | collective-permute-start | bytes 1572872 | tf_op jit(solution)/shard_map/ppermute | solution.py:485
  51.0 6.8 %collective-permute-start.3 = (bf16[2,1024,256]{2,1,0:T(8,128)(2,1)}, bf16[2,1024,256]{2,1,0:T(8,128)(2,1)S(1)}, u32[]{:S(2)}, u32[]{:S(2)}) collective-permute-start(bf16[2,1024,256]{2,1,0:T(8,128)(2,1)} %pad_maximum_fusion), channel_id=1, source_target_pairs={{0,1},{1,0},{2,3},{3,2},{4,5},{5,4},{6,7},{7,6},{8,9},{9,8},{10,11... | collective-permute-start | bytes 3145736 | tf_op jit(solution)/shard_map/ppermute | solution.py:485
  53.2 2.7 collective-permute-start
  55.9 1.7 collective-permute-start.1
  57.8 1.0 copy-start.4
  57.8 1.3 copy-start.3
  59.1 1.0 copy-start
  60.1 0.9 copy-start.2
  72.6 19.5 %all-to-all-start.1 = ((f32[16,24,128]{2,1,0:T(8,128)}), f32[16,24,128]{2,1,0:T(8,128)S(1)}, u32[]{:S(2)}, u32[]{:S(2)}) async-start(f32[16,24,128]{2,1,0:T(8,128)} %get-tuple-element.31), calls=%async_computation.1 | async-start | bytes 393216 | tf_op jit(solution)/shard_map/all_to_all | solution.py:513
  308.6 31.1 %copy-start.1 = (bf16[1024,256]{1,0:T(8,128)(2,1)S(1)}, bf16[1024,256]{1,0:T(8,128)(2,1)}, u32[]{:S(2)}) copy-start(bf16[1024,256]{1,0:T(8,128)(2,1)} %t0.3) | copy-start | bytes 1572868
  376.5 13.7 %all-to-all-start.19 = ((f32[16,16,256]{2,1,0:T(8,128)}), f32[16,16,256]{2,1,0:T(8,128)S(1)}, u32[]{:S(2)}, u32[]{:S(2)}) async-start(f32[16,16,256]{2,1,0:T(8,128)} %broadcast_in_dim.13), calls=%async_computation.19 | async-start | bytes 524288 | tf_op jit(solution)/shard_map/all_to_all | solution.py:643

commit v2 on v1

v2 whole, which is shorter than its diff:
```python
import math

import jax
import jax.numpy as jnp
from jax import lax
from jax.experimental import pallas as pl
from jax.experimental.pallas import tpu as pltpu
from jax.sharding import Mesh, PartitionSpec as P

TILE = 128
TB_DEV = 8
TILES = 64
SINK = 4
ADJ = 4
D = 256

entropy = 0.5
damping = 0.8
lowest = -1e30

AXES = ("src", "x", "zh", "zl", "core")
ROW = ("x", "zh")
COL = ("src", "zl", "core")
NA = 16
NB = 32
SLOTS = 4 * TILES
CHUNK = 8
F32 = jnp.float32


VM = pl.BlockSpec(memory_space=pltpu.VMEM)
SM = pl.BlockSpec(memory_space=pltpu.SMEM)
ANY = pl.BlockSpec(memory_space=pl.ANY)
SHAPE = jax.ShapeDtypeStruct


HERE = "here"
FAR = "far"


def call(kernel, name, ins, outs, scratch, flops=2 << 20, moved=1 << 20, vmem=9):
    in_specs, args = [], []
    for spec, value in ins:
        if spec in (HERE, FAR):
            space = pltpu.VMEM if spec == HERE else pltpu.HBM
            spec, value = pl.BlockSpec(memory_space=space), pltpu.with_memory_space_constraint(value, space)
        in_specs.append(spec)
        args.append(value)
    outs = [(VM, pltpu.VMEM(shape.shape, shape.dtype)) if spec == HERE else (spec, shape) for spec, shape in outs]
    return pl.pallas_call(
        kernel,
        out_shape=[shape for _, shape in outs],
        in_specs=in_specs,
        out_specs=[spec for spec, _ in outs],
        scratch_shapes=scratch,
        name=name,
        cost_estimate=pl.CostEstimate(flops=flops, bytes_accessed=moved, transcendentals=0),
        compiler_params=pltpu.CompilerParams(vmem_limit_bytes=vmem << 20),
    )(*args)


def row_form(block):
    return jnp.sum(block.T, axis=0, keepdims=True)


def column_form(row):
    return jnp.broadcast_to(row, (TILE, TILE)).T


def fold(block):
    return jnp.sum(block.reshape(16, 8, TILE), axis=0)


def fold_max(block):
    return jnp.max(block.reshape(16, 8, TILE), axis=0)


def each_tile(list_ref, body):
    def one(c, carry):
        for step in range(CHUNK):
            k = c * CHUNK + step
            code = list_ref[k]
            body(k, lax.shift_right_logical(code, 5), jnp.bitwise_and(code, NB - 1))
        return carry

    lax.fori_loop(0, lax.shift_right_logical(list_ref[SLOTS] + (CHUNK - 1), 3), one, 0)


def part_index():
    return lax.axis_index("zl") * 2 + lax.axis_index("core")


def pulls_of(own_cells, more_cells, targets, cells, tbuf, sem):
    x, zh = lax.axis_index("x"), lax.axis_index("zh")
    pulls = [
        pltpu.make_async_copy(targets[0], tbuf.at[0], sem.at[0]),
        pltpu.make_async_copy(targets[1], tbuf.at[1], sem.at[1]),
        pltpu.make_async_copy(targets[2], tbuf.at[2], sem.at[2]),
        pltpu.make_async_copy(targets[3], tbuf.at[3], sem.at[3]),
    ]
    for m, piece in enumerate((own_cells, *more_cells)):
        for k in range(4):
            place = jnp.bitwise_and(x + (4 - m), 3) * 4 + jnp.bitwise_and(zh + (4 - k), 3)
            pulls.append(pltpu.make_async_copy(piece.at[k], cells.at[place], sem.at[4 + 4 * m + k]))
    return pulls


def write_copies(out_ref, rows, value, first=0):
    for d in range(16):
        out_ref[d, first : first + rows] = value


def live_rows(list_ref):
    block = 4 * lax.broadcasted_iota(jnp.int32, (NA, TILE), 0) + part_index()
    return block < list_ref[SLOTS + 1]


def total(recv_ref, first, rows):
    so_far = recv_ref[0, first : first + rows]
    for d in range(1, 16):
        so_far = so_far + recv_ref[d, first : first + rows]
    return so_far


def merged(recv_ref, rows):
    largest = recv_ref[0, 0:rows]
    for d in range(1, 16):
        largest = jnp.maximum(largest, recv_ref[d, 0:rows])
    so_far = jnp.zeros((rows, TILE), F32)
    for d in range(16):
        so_far = so_far + jnp.exp(recv_ref[d, 0:rows] - largest)
    return largest + jnp.log(so_far)


def finish_log(largest, so_far):
    good = so_far > 0
    return jnp.where(good, largest + jnp.log(jnp.where(good, so_far, 1.0)), lowest)


def scores_kernel(
    codes0, codes1, codes2, codes3, own_cells, c1, c2, c3, t0, t1, t2, t3, mapping_far, mass_ref,
    send_ref, list_ref, xbuf,
    tbuf, cells_ref, mapping_ref, mapped, top, acc, sem,
):
    pulls = pulls_of(own_cells, (c1, c2, c3), (t0, t1, t2, t3), cells_ref, tbuf, sem)
    pulls.append(pltpu.make_async_copy(mapping_far, mapping_ref, sem.at[20]))
    for pull in pulls:
        pull.start()
    part = part_index()
    count = 0
    for r, codes in enumerate((codes0, codes1, codes2, codes3)):
        base = jnp.bitwise_xor(part, r) * TB_DEV

        def gather(k, n, codes=codes, base=base):
            code = codes[0, k]
            source = lax.shift_right_arithmetic(code, 3)
            take = jnp.logical_and(code >= 0, jnp.bitwise_and(source, 3) == part)
            target = base + jnp.bitwise_and(code, TB_DEV - 1)
            list_ref[n] = lax.shift_right_arithmetic(source, 2) * NB + target
            return n + take.astype(jnp.int32)

        count = lax.fori_loop(0, TILES, gather, count, unroll=8)

    def clear(k, carry):
        list_ref[k] = 0
        return carry

    lax.fori_loop(count, jnp.minimum(count + CHUNK, SLOTS), clear, 0)
    list_ref[SLOTS] = count
    list_ref[SLOTS + 1] = codes0[0, TILES + lax.axis_index("src")]
    for pull in pulls:
        pull.wait()

    def blank(a, carry):
        top[a] = jnp.full((TILE, TILE), lowest, F32)
        acc[a] = jnp.zeros((TILE, TILE), F32)
        product = jnp.dot(cells_ref[a], mapping_ref[...], preferred_element_type=F32)
        mapped[a] = product.astype(jnp.bfloat16)
        return carry

    lax.fori_loop(0, NA, blank, 0)
    scale = (1.0 / entropy) / math.sqrt(D)

    def product(k, a, b):
        slot = jnp.bitwise_xor(lax.shift_right_logical(b, 3), part)
        rows = pl.ds(pl.multiple_of(jnp.bitwise_and(b, TB_DEV - 1) * TILE, TILE), TILE)
        x = lax.dot_general(
            mapped[a], tbuf[slot, rows, :], (((1,), (1,)), ((), ())), preferred_element_type=F32
        )
        x = jnp.where(k < count, x * scale, lowest)
        xbuf[k] = x
        top[a] = jnp.maximum(top[a], x)

    each_tile(list_ref, product)

    def spread(a, carry):
        top[a] = jnp.broadcast_to(jnp.max(top[a], axis=1, keepdims=True), (TILE, TILE))
        return carry

    lax.fori_loop(0, NA, spread, 0)

    def add(k, a, b):
        acc[a] += jnp.exp(xbuf[k] - top[a])

    each_tile(list_ref, add)
    for a in range(NA):
        row = finish_log(top[a].T[0:1], row_form(acc[a]))
        for d in range(16):
            send_ref[d, a : a + 1] = row
    write_copies(send_ref, 8, jnp.broadcast_to(mass_ref[...], (8, TILE)), NA)


def first_targets_kernel(
    list_ref, recv_ref, xbuf, mass_ref,
    send_ref, u_ref, mass_out,
    col, top, acc,
):
    for a in range(NA):
        mass_out[a : a + 1] = recv_ref[a, NA : NA + 1]
    u = jnp.where(live_rows(list_ref), mass_out[...] - merged(recv_ref, NA), 0.0)
    u_ref[...] = u
    for a in range(NA):
        col[a] = column_form(u[a : a + 1])
    top[...] = jnp.full((NB, 8, TILE), lowest, F32)
    acc[...] = jnp.zeros((NB, 8, TILE), F32)

    def largest(k, a, b):
        top[b] = jnp.maximum(top[b], fold_max(xbuf[k] + col[a]))

    each_tile(list_ref, largest)
    for b in range(NB):
        top[b] = jnp.broadcast_to(jnp.max(top[b], axis=0, keepdims=True), (8, TILE))

    def add(k, a, b):
        acc[b] += fold(jnp.exp(xbuf[k] + col[a] - top[b][0:1]))

    each_tile(list_ref, add)
    for b in range(NB):
        row = finish_log(top[b][0:1], jnp.sum(acc[b], axis=0, keepdims=True))
        for d in range(16):
            send_ref[d, b : b + 1] = row
    write_copies(send_ref, TB_DEV, mass_ref[...], NB)


def kernel_matrix_kernel(
    list_ref, recv_ref, u_ref, xbuf,
    send_ref, v_ref, mass_out, kbuf,
    col, acc,
):
    for p in range(4):
        mass_out[p * TB_DEV : (p + 1) * TB_DEV] = recv_ref[p, NB : NB + TB_DEV]
    v_ref[...] = mass_out[...] - merged(recv_ref, NB)
    for a in range(NA):
        col[a] = column_form(u_ref[a : a + 1])
    acc[...] = jnp.zeros((NA, TILE, TILE), F32)

    def build(k, a, b):
        value = jnp.exp(xbuf[k] + col[a] + v_ref[pl.ds(b, 1)])
        kbuf[k] = value
        acc[a] += value

    each_tile(list_ref, build)
    for a in range(NA):
        row = row_form(acc[a])
        for d in range(16):
            send_ref[d, a : a + 1] = row


def columns_kernel(list_ref, recv_ref, mass_ref, kbuf, _, send_ref, alpha_ref, col, acc):
    alpha = jnp.where(live_rows(list_ref), jnp.exp(mass_ref[...]) / total(recv_ref, 0, NA), 1.0)
    alpha_ref[...] = alpha
    for a in range(NA):
        col[a] = column_form(alpha[a : a + 1])
    acc[...] = jnp.zeros((NB, 8, TILE), F32)

    def add(k, a, b):
        acc[b] += fold(kbuf[k] * col[a])

    each_tile(list_ref, add)
    write_copies(send_ref, NB, jnp.sum(acc[...], axis=1))


def rows_kernel(list_ref, recv_ref, mass_ref, kbuf, _, send_ref, beta_ref, acc):
    beta_ref[...] = jnp.exp(mass_ref[...]) / total(recv_ref, 0, NB)
    acc[...] = jnp.zeros((NA, TILE, TILE), F32)

    def add(k, a, b):
        acc[a] += kbuf[k] * beta_ref[pl.ds(b, 1)]

    each_tile(list_ref, add)
    for a in range(NA):
        row = row_form(acc[a])
        for d in range(16):
            send_ref[d, a : a + 1] = row


def masses_kernel(
    list_ref, recv_ref, mass_ref, kbuf, xbuf,
    send_ref, beta_ref, sum_ref, cost_ref,
    acc, acc_cost,
):
    column_sum = total(recv_ref, 0, NB)
    sum_ref[...] = column_sum
    beta_ref[...] = jnp.exp(mass_ref[...]) / column_sum
    acc[...] = jnp.zeros((NA, TILE, TILE), F32)
    acc_cost[...] = jnp.zeros((NA, TILE, TILE), F32)

    def add(k, a, b):
        plan = kbuf[k] * beta_ref[pl.ds(b, 1)]
        acc[a] += plan
        acc_cost[a] += plan * xbuf[k]

    each_tile(list_ref, add)
    for a in range(NA):
        row = row_form(acc[a])
        cost = row_form(acc_cost[a])
        cost_ref[a : a + 1] = cost
        for d in range(16):
            send_ref[d, a : a + 1] = row
            send_ref[d, NA + a : NA + a + 1] = cost


def first_ratio_kernel(
    list_ref, recv_ref, alpha_ref, kbuf, xbuf,
    send_ref, sum_ref, s_ref, cost_ref,
    col, col2, acc, acc2,
):
    row_sum = total(recv_ref, 0, NA)
    sum_ref[...] = row_sum
    s = jnp.where(live_rows(list_ref), -total(recv_ref, NA, NA) / row_sum, 0.0)
    s_ref[...] = s
    for a in range(NA):
        col[a] = column_form(alpha_ref[a : a + 1])
        col2[a] = column_form(s[a : a + 1] * damping)
    acc[...] = jnp.zeros((NB, 8, TILE), F32)
    acc2[...] = jnp.zeros((NB, 8, TILE), F32)

    def add(k, a, b):
        plan = kbuf[k] * col[a]
        acc[b] += fold(plan * xbuf[k])
        acc2[b] += fold(plan * (xbuf[k] + col2[a]))

    each_tile(list_ref, add)
    cost_ref[...] = jnp.sum(acc[...], axis=1)
    write_copies(send_ref, NB, jnp.sum(acc2[...], axis=1))


def pull_kernel(
    list_ref, recv_ref, sum_ref, beta_ref, cost_ref, kbuf, _,
    send_ref,
    acc, weight,
):
    t = -total(recv_ref, 0, NB) / sum_ref[...]
    weight[...] = beta_ref[...] * t * damping
    acc[...] = jnp.zeros((NA, TILE, TILE), F32)

    def add(k, a, b):
        acc[a] += kbuf[k] * weight[pl.ds(b, 1)]

    each_tile(list_ref, add)
    for a in range(NA):
        row = cost_ref[a : a + 1] + row_form(acc[a])
        for d in range(16):
            send_ref[d, a : a + 1] = row


def push_kernel(
    list_ref, recv_ref, sum_ref, alpha_ref, cost_ref, kbuf, _,
    send_ref, s_ref,
    col, acc,
):
    s = jnp.where(live_rows(list_ref), -total(recv_ref, 0, NA) / sum_ref[...], 0.0)
    s_ref[...] = s
    weight = alpha_ref[...] * s * damping
    for a in range(NA):
        col[a] = column_form(weight[a : a + 1])
    acc[...] = jnp.zeros((NB, 8, TILE), F32)

    def add(k, a, b):
        acc[b] += fold(kbuf[k] * col[a])

    each_tile(list_ref, add)
    write_copies(send_ref, NB, cost_ref[...] + jnp.sum(acc[...], axis=1))


def gradient_kernel(
    list_ref, recv_ref, sum_ref, beta_ref, alpha_ref, s_ref, u_ref, v_ref,
    own_cells, c1, c2, c3, t0, t1, t2, t3, xbuf,
    g_ref, source_ref, target_ref,
    tbuf, cells_ref, col, col2, trow, vrow, prod, sem,
):
    pulls = pulls_of(own_cells, (c1, c2, c3), (t0, t1, t2, t3), cells_ref, tbuf, sem)
    for pull in pulls:
        pull.start()
    part = part_index()
    own = pl.ds(lax.axis_index("x") * 4 + lax.axis_index("zh"), 1)
    u = u_ref[...] + jnp.log(alpha_ref[...])
    vrow[...] = v_ref[...] + jnp.log(beta_ref[...])
    source_ref[...] = entropy * (u_ref[own] + jnp.log(alpha_ref[own]))
    own = pl.ds(pl.multiple_of(part * TB_DEV, TB_DEV), TB_DEV)
    target_ref[...] = entropy * vrow[own]
    trow[...] = -total(recv_ref, 0, NB) / sum_ref[...]
    for a in range(NA):
        col[a] = column_form(u[a : a + 1])
        col2[a] = column_form(1.0 + s_ref[a : a + 1])
    prod[...] = jnp.zeros((NA, TILE, D), F32)
    for pull in pulls:
        pull.wait()

    def add(k, a, b):
        slot = jnp.bitwise_xor(lax.shift_right_logical(b, 3), part)
        rows = pl.ds(pl.multiple_of(jnp.bitwise_and(b, TB_DEV - 1) * TILE, TILE), TILE)
        x = xbuf[k]
        weights = jnp.exp(x + col[a] + vrow[pl.ds(b, 1)]) * (x + col2[a] + trow[pl.ds(b, 1)])
        prod[a] += jnp.dot(
            weights.astype(jnp.bfloat16), tbuf[slot, rows, :], preferred_element_type=F32
        )

    each_tile(list_ref, add)
    contract = (((0,), (0,)), ((), ()))

    def outer(a, so_far):
        value = prod[a]
        high = value.astype(jnp.bfloat16)
        rest = value - high.astype(F32)
        middle = rest.astype(jnp.bfloat16)
        low = (rest - middle.astype(F32)).astype(jnp.bfloat16)
        cells = cells_ref[a]
        for piece in (low, middle, high):
            so_far = so_far + lax.dot_general(cells, piece, contract, preferred_element_type=F32)
        return so_far

    g = lax.fori_loop(0, NA, outer, jnp.zeros((D, D), F32))
    g_ref[...] = g * (-1.0 / math.sqrt(D))


def swap(value, axis):
    return lax.ppermute(value, axis, [(0, 1), (1, 0)])


def shifted(value, axis):
    return [lax.ppermute(value, axis, [(i, (i + k) % 4) for i in range(4)]) for k in (1, 2, 3)]


def row_exchange(value):
    return lax.all_to_all(value, ROW, 0, 0)


def col_exchange(value):
    return lax.all_to_all(value, COL, 0, 0)


def shards(
    source_cells,
    target_cells,
    mapping,
    source_logmass,
    target_logmass,
    group_blocks,
    tile_source,
    tile_target,
):
    codes = jnp.where(tile_source >= 0, tile_source * TB_DEV + tile_target, -1)
    codes0 = jnp.concatenate([codes, group_blocks.reshape(1, 4)], axis=1)
    first = (
        swap(codes0, "zl"),
        swap(codes0, "core"),
        *shifted(source_cells, "zh"),
        swap(target_cells, "zl"),
        swap(target_cells, "core"),
        source_logmass.astype(F32).reshape(1, TILE),
        target_logmass.astype(F32).reshape(TB_DEV, TILE),
    )
    codes2, codes1, z1, z2, z3, t2, t1, own_mass, own_target_mass = lax.optimization_barrier(first)
    codes3 = swap(codes2, "core")
    own_cells = jnp.stack([source_cells, z1, z2, z3])
    cells = (own_cells, *shifted(own_cells, "x"))
    targets = (target_cells, t1, t2, swap(t2, "core"))

    rows_to = (VM, SHAPE((16, NA, TILE), F32))
    cols_to = (VM, SHAPE((16, NB, TILE), F32))
    rows_state = (VM, SHAPE((NA, TILE), F32))
    cols_state = (VM, SHAPE((NB, TILE), F32))
    tiles = (HERE, SHAPE((SLOTS, TILE, TILE), F32))
    row_blocks = pltpu.VMEM((NA, TILE, TILE), F32)
    col_rows = pltpu.VMEM((NB, 8, TILE), F32)
    gathered = [
        pltpu.VMEM((4, TB_DEV * TILE, D), jnp.bfloat16),
        pltpu.VMEM((NA, TILE, D), jnp.bfloat16),
    ]
    gathered_sems = pltpu.SemaphoreType.DMA((21,))
    gathered_refs = [(ANY, value) for value in cells] + [(FAR, targets[0])] + [(ANY, value) for value in targets[1:]]

    send, tile_list, x = call(
        scores_kernel,
        "scores",
        [
            (SM, codes0), (SM, codes1), (SM, codes2), (SM, codes3), *gathered_refs,
            (FAR, mapping), (VM, own_mass),
        ],
        [(VM, SHAPE((16, NA + 8, TILE), F32)), (SM, SHAPE((SLOTS + 8,), jnp.int32)), tiles],
        [
            *gathered, pltpu.VMEM((D, D), jnp.bfloat16), pltpu.VMEM((NA, TILE, D), jnp.bfloat16),
            row_blocks, row_blocks, gathered_sems,
        ],
    )
    tile_list, x = (SM, tile_list), (HERE, x)
    recv = row_exchange(send)
    send, u, source_mass = call(
        first_targets_kernel,
        "first_targets",
        [tile_list, (VM, recv), x, (VM, own_target_mass)],
        [(VM, SHAPE((16, NB + TB_DEV, TILE), F32)), rows_state, rows_state],
        [row_blocks, col_rows, col_rows],
    )
    recv = col_exchange(send)
    send, v, target_mass, k = call(
        kernel_matrix_kernel,
        "kernel_matrix",
        [tile_list, (VM, recv), (VM, u), x],
        [rows_to, cols_state, cols_state, tiles],
        [row_blocks, row_blocks],
    )
    k = (HERE, k)
    for sweep in range(1, SINK):
        recv = row_exchange(send)
        send, alpha = call(
            columns_kernel,
            "columns",
            [tile_list, (VM, recv), (VM, source_mass), k, x],
            [cols_to, rows_state],
            [row_blocks, col_rows],
        )
        recv = col_exchange(send)
        if sweep < SINK - 1:
            send, _ = call(
                rows_kernel,
                "rows",
                [tile_list, (VM, recv), (VM, target_mass), k, x],
                [rows_to, cols_state],
                [row_blocks],
            )
    send, beta, column_sum, row_cost = call(
        masses_kernel,
        "masses",
        [tile_list, (VM, recv), (VM, target_mass), k, x],
        [(VM, SHAPE((16, 2 * NA, TILE), F32)), cols_state, cols_state, rows_state],
        [row_blocks, row_blocks],
    )
    recv = row_exchange(send)
    send, row_sum, s, column_cost = call(
        first_ratio_kernel,
        "first_ratio",
        [tile_list, (VM, recv), (VM, alpha), k, x],
        [cols_to, rows_state, rows_state, cols_state],
        [row_blocks, row_blocks, col_rows, col_rows],
    )
    recv = col_exchange(send)
    for _ in range(1, ADJ):
        (send,) = call(
            pull_kernel,
            "pull",
            [tile_list, (VM, recv), (VM, column_sum), (VM, beta), (VM, row_cost), k, x],
            [rows_to],
            [row_blocks, pltpu.VMEM((NB, TILE), F32)],
        )
        recv = row_exchange(send)
        send, s = call(
            push_kernel,
            "push",
            [tile_list, (VM, recv), (VM, row_sum), (VM, alpha), (VM, column_cost), k, x],
            [cols_to, rows_state],
            [row_blocks, col_rows],
        )
        recv = col_exchange(send)
    gradient, own_source, own_target = call(
        gradient_kernel,
        "gradient",
        [
            tile_list, (VM, recv), (VM, column_sum), (VM, beta), (VM, alpha), (VM, s), (VM, u), (VM, v),
            *gathered_refs, x,
        ],
        [(VM, SHAPE((D, D), F32)), (VM, SHAPE((1, TILE), F32)), (VM, SHAPE((TB_DEV, TILE), F32))],
        [
            *gathered, row_blocks, row_blocks, pltpu.VMEM((NB, TILE), F32), pltpu.VMEM((NB, TILE), F32),
            pltpu.VMEM((NA, TILE, D), F32), gathered_sems,
        ],
    )
    piece = jnp.sum(col_exchange(gradient.reshape(16, 16, D)), axis=0)
    piece = jnp.sum(row_exchange(jnp.broadcast_to(piece[None], (16, 16, D))), axis=0)
    map_gradient = col_exchange(jnp.broadcast_to(piece[None], (16, 16, D))).reshape(D, D)

    return (own_source.reshape(TILE), own_target.reshape(TB_DEV * TILE), map_gradient)


def solution(mesh):
    grid = Mesh(mesh.devices.reshape(4, 4, 4, 2, 2), AXES)
    tgt = ("x", "zh", "zl", "core")
    both = ("src", *tgt)
    in_specs = (
        P(both, None),
        P(tgt, None),
        P(),
        P(both),
        P(tgt),
        P(),
        P(both, None),
        P(both, None),
    )
    out_specs = (P(both), P(tgt), P())
    return jax.shard_map(shards, mesh=grid, in_specs=in_specs, out_specs=out_specs, check_vma=False)
```

time: 392 us -> 342 us (0.87)
  waiting for transfers between devices: 50.3 us -> 19.6 us
  Pallas kernels: 71.2 us -> 52.7 us
  blocking collectives: 224 us -> 242 us
  starting transfers between devices: 30.7 us -> 22.7 us
  local copies, waits for them, and re-layouts: 7.93 us -> 0.74 us
    ppermute x4 -> x6, waiting for transfers between devices: 34 us -> 4.22 us  [swap(): return lax.ppermute(value, axis, [(0, 1), (1, 0)])]
    all_to_all x3 -> x0, starting transfers between devices: 26.7 us -> none  [the longest x1 11.6 us: shards(): lax.all_to_all(jnp.broadcast_to(source_cells[None], (16, TILE, D)), ROW,...]
    pallas_call x17, Pallas kernels: 71.2 us -> 52.7 us  [call(): pl.pallas_call(kernel, out_shape=[shape for _, shape in outs], in_specs=i...]
    all_to_all x3 -> x0, waiting for transfers between devices: 16.3 us -> none  [the longest x1 10.2 us: row_exchange(): return lax.all_to_all(value, ROW, 0, 0)]
    ppermute x0 -> x6, starting transfers between devices: none -> 15.6 us  [shifted(): lax.ppermute(value, axis, [(i, (i + k) % 4) for i in range(4)])]
    ppermute x0 -> x6, waiting for transfers between devices: none -> 15.4 us  [shifted(): lax.ppermute(value, axis, [(i, (i + k) % 4) for i in range(4)])]
    all_to_all x8 -> x9, blocking collectives: 106 us -> 122 us  [row_exchange(): return lax.all_to_all(value, ROW, 0, 0)]
    all_to_all x9 -> x10, blocking collectives: 117 us -> 120 us  [col_exchange(): return lax.all_to_all(value, COL, 0, 0)]
  transfers between devices with their start and end apart: 7 -> 12, of which waited for: 4 -> 6; matrix products, arithmetic and copies ran while one was open for 2% -> 1% of each run, Pallas kernels for 0% -> 0%
where the time goes in v2:
time: 342 us
  blocking collectives  242 us (71%)
  Pallas kernels  52.7 us (15%)
  starting transfers between devices  22.7 us (7%)
  waiting for transfers between devices  19.6 us (6%)
  other arithmetic  3.66 us (1%)
    all_to_all x9, blocking collectives, row_exchange(): return lax.all_to_all(value, ROW, 0, 0)  122 us
    all_to_all x10, blocking collectives, col_exchange(): return lax.all_to_all(value, COL, 0, 0)  120 us
    pallas_call x17, Pallas kernels, call(): pl.pallas_call(kernel, out_shape=[shape for _, shape in outs], in_specs=i...  52.7 us
    ppermute x6, starting transfers between devices, shifted(): lax.ppermute(value, axis, [(i, (i + k) % 4) for i in range(4)])  15.6 us
    ppermute x6, waiting for transfers between devices, shifted(): lax.ppermute(value, axis, [(i, (i + k) % 4) for i in range(4)])  15.4 us
    ppermute x6, starting transfers between devices, swap(): return lax.ppermute(value, axis, [(0, 1), (1, 0)])  7.15 us
  transfers between devices with their start and end apart: 12, of which 6 were waited for; matrix products, arithmetic and copies ran while one was open for 1% of the time, Pallas kernels for 0%

profile of v2, /device:TPU:1, one launch (start us, length us, event | category | flops | bytes accessed | tf_op | source)
XLA Modules:
  0.0 342.0 jit_solution(676422447587398005)
XLA Ops:
  7.2 5.2 %collective-permute-start.3 = (bf16[128,256]{1,0:T(8,128)(2,1)}, bf16[128,256]{1,0:T(8,128)(2,1)S(1)}, u32[]{:S(2)}, u32[]{:S(2)}) collective-permute-start(bf16[128,256]{1,0:T(8,128)(2,1)} %param.8), channel_id=1, source_target_pairs={{0,8},{4,12},{8,0},{12,4},{1,9},{5,13},{9,1},{13,5},{2,10},{6,14},... | collective-permute-start | bytes 196616 | tf_op jit(solution)/shard_map/ppermute | solution.py:442
  17.7 5.5 %collective-permute-start.4 = (bf16[128,256]{1,0:T(8,128)(2,1)}, bf16[128,256]{1,0:T(8,128)(2,1)S(1)}, u32[]{:S(2)}, u32[]{:S(2)}) collective-permute-start(bf16[128,256]{1,0:T(8,128)(2,1)} %param.8), channel_id=1, source_target_pairs={{0,12},{4,0},{8,4},{12,8},{1,13},{5,1},{9,5},{13,9},{2,14},{6,2},{... | collective-permute-start | bytes 196616 | tf_op jit(solution)/shard_map/ppermute | solution.py:442
  34.1 8.4 %collective-permute-done.10.c3 = bf16[4,128,256]{2,1,0:T(8,128)(2,1)S(1)} collective-permute-done((bf16[4,128,256]{2,1,0:T(8,128)(2,1)S(1)}, bf16[4,128,256]{2,1,0:T(8,128)(2,1)S(1)}, u32[]{:S(2)}, u32[]{:S(2)}) %collective-permute-start.10) | collective-permute-done | bytes 262176 | tf_op jit(solution)/shard_map/ppermute | solution.py:442
  46.6 11.7 %scores.1 = (f32[16,24,128]{2,1,0:T(8,128)S(1)}, s32[264]{0:T(512)S(1)}, f32[256,128,128]{2,1,0:T(8,128)S(1)}) custom-call(s32[1,68]{1,0:T(1,128)S(1)} %pad_add_fusion.codes0, s32[1,68]{1,0:T(1,128)S(1)} %collective-permute-done.1.codes1, s32[1,68]{1,0:T(1,128)S(1)} %collective-permute-done.codes2, s32[1,68]{1,0:T(1,128)S(1)} %collective-permute-done.7.codes3, ...), custom_call_target="tpu_custom_call" | custom-call | flops 2097152 | bytes 1048576 | tf_op jit(solution)/shard_map/scores/pallas_call | solution.py:50
  58.3 16.3 %all_to_all.95.recv_ref = f32[16,24,128]{2,1,0:T(8,128)S(1)} all-to-all(f32[16,24,128]{2,1,0:T(8,128)S(1)} %get-tuple-element.51), channel_id=1, replica_groups=mesh['src'=4,'x'=4,'zh'=4,'zl'=2,'core'=2] {'x','zh'}, dimensions={0} | all-to-all | bytes 393216 | tf_op jit(solution)/shard_map/all_to_all | solution.py:446
  77.2 14.1 %all_to_all.96.recv_ref = f32[16,40,128]{2,1,0:T(8,128)S(1)} all-to-all(f32[16,40,128]{2,1,0:T(8,128)S(1)} %get-tuple-element.54), channel_id=1, replica_groups=mesh['src'=4,'x'=4,'zh'=4,'zl'=2,'core'=2] {'src','zl','core'}, dimensions={0} | all-to-all | bytes 655360 | tf_op jit(solution)/shard_map/all_to_all | solution.py:450
  93.5 12.9 %all_to_all.97.recv_ref = f32[16,16,128]{2,1,0:T(8,128)S(1)} all-to-all(f32[16,16,128]{2,1,0:T(8,128)S(1)} %get-tuple-element.56), channel_id=1, replica_groups=mesh['src'=4,'x'=4,'zh'=4,'zl'=2,'core'=2] {'x','zh'}, dimensions={0} | all-to-all | bytes 262144 | tf_op jit(solution)/shard_map/all_to_all | solution.py:446
  108.6 11.6 %all_to_all.98.recv_ref = f32[16,32,128]{2,1,0:T(8,128)S(1)} all-to-all(f32[16,32,128]{2,1,0:T(8,128)S(1)} %get-tuple-element.59), channel_id=1, replica_groups=mesh['src'=4,'x'=4,'zh'=4,'zl'=2,'core'=2] {'src','zl','core'}, dimensions={0} | all-to-all | bytes 524288 | tf_op jit(solution)/shard_map/all_to_all | solution.py:450
  122.1 13.0 %all_to_all.99.recv_ref = f32[16,16,128]{2,1,0:T(8,128)S(1)} all-to-all(f32[16,16,128]{2,1,0:T(8,128)S(1)} %get-tuple-element.61), channel_id=1, replica_groups=mesh['src'=4,'x'=4,'zh'=4,'zl'=2,'core'=2] {'x','zh'}, dimensions={0} | all-to-all | bytes 262144 | tf_op jit(solution)/shard_map/all_to_all | solution.py:446
  137.2 11.5 %all_to_all.100.recv_ref = f32[16,32,128]{2,1,0:T(8,128)S(1)} all-to-all(f32[16,32,128]{2,1,0:T(8,128)S(1)} %get-tuple-element.62), channel_id=1, replica_groups=mesh['src'=4,'x'=4,'zh'=4,'zl'=2,'core'=2] {'src','zl','core'}, dimensions={0} | all-to-all | bytes 524288 | tf_op jit(solution)/shard_map/all_to_all | solution.py:450
  150.5 12.8 %all_to_all.101.recv_ref = f32[16,16,128]{2,1,0:T(8,128)S(1)} all-to-all(f32[16,16,128]{2,1,0:T(8,128)S(1)} %get-tuple-element.63), channel_id=1, replica_groups=mesh['src'=4,'x'=4,'zh'=4,'zl'=2,'core'=2] {'x','zh'}, dimensions={0} | all-to-all | bytes 262144 | tf_op jit(solution)/shard_map/all_to_all | solution.py:446
  164.9 11.6 %all_to_all.102.recv_ref = f32[16,32,128]{2,1,0:T(8,128)S(1)} all-to-all(f32[16,32,128]{2,1,0:T(8,128)S(1)} %get-tuple-element.64), channel_id=1, replica_groups=mesh['src'=4,'x'=4,'zh'=4,'zl'=2,'core'=2] {'src','zl','core'}, dimensions={0} | all-to-all | bytes 524288 | tf_op jit(solution)/shard_map/all_to_all | solution.py:450
  179.0 14.0 %all_to_all.103.recv_ref = f32[16,32,128]{2,1,0:T(8,128)S(1)} all-to-all(f32[16,32,128]{2,1,0:T(8,128)S(1)} %get-tuple-element.65), channel_id=1, replica_groups=mesh['src'=4,'x'=4,'zh'=4,'zl'=2,'core'=2] {'x','zh'}, dimensions={0} | all-to-all | bytes 524288 | tf_op jit(solution)/shard_map/all_to_all | solution.py:446
  196.2 13.1 %all_to_all.104.recv_ref = f32[16,32,128]{2,1,0:T(8,128)S(1)} all-to-all(f32[16,32,128]{2,1,0:T(8,128)S(1)} %get-tuple-element.67), channel_id=1, replica_groups=mesh['src'=4,'x'=4,'zh'=4,'zl'=2,'core'=2] {'src','zl','core'}, dimensions={0} | all-to-all | bytes 524288 | tf_op jit(solution)/shard_map/all_to_all | solution.py:450
  210.9 12.7 %all_to_all.105.recv_ref = f32[16,16,128]{2,1,0:T(8,128)S(1)} all-to-all(f32[16,16,128]{2,1,0:T(8,128)S(1)} %pull.3), channel_id=1, replica_groups=mesh['src'=4,'x'=4,'zh'=4,'zl'=2,'core'=2] {'x','zh'}, dimensions={0} | all-to-all | bytes 262144 | tf_op jit(solution)/shard_map/all_to_all | solution.py:446
  225.6 11.6 %all_to_all.106.recv_ref = f32[16,32,128]{2,1,0:T(8,128)S(1)} all-to-all(f32[16,32,128]{2,1,0:T(8,128)S(1)} %get-tuple-element.73), channel_id=1, replica_groups=mesh['src'=4,'x'=4,'zh'=4,'zl'=2,'core'=2] {'src','zl','core'}, dimensions={0} | all-to-all | bytes 524288 | tf_op jit(solution)/shard_map/all_to_all | solution.py:450
  238.9 12.9 %all_to_all.107.recv_ref = f32[16,16,128]{2,1,0:T(8,128)S(1)} all-to-all(f32[16,16,128]{2,1,0:T(8,128)S(1)} %pull.4), channel_id=1, replica_groups=mesh['src'=4,'x'=4,'zh'=4,'zl'=2,'core'=2] {'x','zh'}, dimensions={0} | all-to-all | bytes 262144 | tf_op jit(solution)/shard_map/all_to_all | solution.py:446
  253.9 11.4 %all_to_all.108.recv_ref = f32[16,32,128]{2,1,0:T(8,128)S(1)} all-to-all(f32[16,32,128]{2,1,0:T(8,128)S(1)} %get-tuple-element.74), channel_id=1, replica_groups=mesh['src'=4,'x'=4,'zh'=4,'zl'=2,'core'=2] {'src','zl','core'}, dimensions={0} | all-to-all | bytes 524288 | tf_op jit(solution)/shard_map/all_to_all | solution.py:450
  266.9 12.9 %all_to_all.109.recv_ref = f32[16,16,128]{2,1,0:T(8,128)S(1)} all-to-all(f32[16,16,128]{2,1,0:T(8,128)S(1)} %pull.5), channel_id=1, replica_groups=mesh['src'=4,'x'=4,'zh'=4,'zl'=2,'core'=2] {'x','zh'}, dimensions={0} | all-to-all | bytes 262144 | tf_op jit(solution)/shard_map/all_to_all | solution.py:446
  281.4 11.5 %all_to_all.110.recv_ref = f32[16,32,128]{2,1,0:T(8,128)S(1)} all-to-all(f32[16,32,128]{2,1,0:T(8,128)S(1)} %get-tuple-element.75), channel_id=1, replica_groups=mesh['src'=4,'x'=4,'zh'=4,'zl'=2,'core'=2] {'src','zl','core'}, dimensions={0} | all-to-all | bytes 524288 | tf_op jit(solution)/shard_map/all_to_all | solution.py:450
  292.8 10.6 %gradient.1 = (f32[256,256]{1,0:T(8,128)S(1)}, f32[1,128]{1,0:T(1,128)}, f32[8,128]{1,0:T(8,128)}) custom-call(s32[264]{0:T(512)S(1)} %get-tuple-element.50.list_ref, f32[16,32,128]{2,1,0:T(8,128)S(1)} %all_to_all.110.recv_ref, f32[32,128]{1,0:T(8,128)S(1)} %get-tuple-element.68.sum_ref, f32[32,128]{1,0:T(8,128)S(1)} %get-tuple-element.69.beta_ref, ...), custom_call_target="tpu_custom_call" | custom-call | flops 2097152 | bytes 1048576 | tf_op jit(solution)/shard_map/gradient/pallas_call | solution.py:50
  303.4 10.6 %all_to_all.111 = f32[16,16,256]{2,1,0:T(8,128)S(1)} all-to-all(f32[16,16,256]{2,1,0:T(8,128)S(1)} %bitcast.15), channel_id=1, replica_groups=mesh['src'=4,'x'=4,'zh'=4,'zl'=2,'core'=2] {'src','zl','core'}, dimensions={0} | all-to-all | bytes 524288 | tf_op jit(solution)/shard_map/all_to_all | solution.py:450
  314.1 14.0 %all_to_all.112 = f32[16,16,256]{2,1,0:T(8,128)S(1)} all-to-all(f32[16,16,256]{2,1,0:T(8,128)S(1)} %broadcast_in_dim.9), channel_id=1, replica_groups=mesh['src'=4,'x'=4,'zh'=4,'zl'=2,'core'=2] {'x','zh'}, dimensions={0} | all-to-all | bytes 524288 | tf_op jit(solution)/shard_map/all_to_all | solution.py:446
  328.2 13.1 %all_to_all.113 = f32[16,16,256]{2,1,0:T(8,128)S(1)} all-to-all(f32[16,16,256]{2,1,0:T(8,128)S(1)} %broadcast_in_dim.18), channel_id=1, replica_groups=mesh['src'=4,'x'=4,'zh'=4,'zl'=2,'core'=2] {'src','zl','core'}, dimensions={0} | all-to-all | bytes 524288 | tf_op jit(solution)/shard_map/all_to_all | solution.py:450
  (46 shorter events, 58.1 us)
Async XLA Ops:
  0.6 26.1 %collective-permute-start.6 = (bf16[1024,256]{1,0:T(8,128)(2,1)}, bf16[1024,256]{1,0:T(8,128)(2,1)S(1)}, u32[]{:S(2)}, u32[]{:S(2)}) collective-permute-start(bf16[1024,256]{1,0:T(8,128)(2,1)} %t0.3), channel_id=1, source_target_pairs={{0,1},{1,0},{2,3},{3,2},{4,5},{5,4},{6,7},{7,6},{8,9},{9,8},{10,11... | collective-permute-start | bytes 1572872 | tf_op jit(solution)/shard_map/ppermute | solution.py:438
  4.0 22.7 %collective-permute-start.5 = (bf16[1024,256]{1,0:T(8,128)(2,1)}, bf16[1024,256]{1,0:T(8,128)(2,1)S(1)}, u32[]{:S(2)}, u32[]{:S(2)}) collective-permute-start(bf16[1024,256]{1,0:T(8,128)(2,1)} %t0.3), channel_id=1, source_target_pairs={{0,2},{2,0},{1,3},{3,1},{4,6},{6,4},{5,7},{7,5},{8,10},{10,8},{9,1... | collective-permute-start | bytes 1572872 | tf_op jit(solution)/shard_map/ppermute | solution.py:438
  5.4 7.7 %collective-permute-start.1 = (s32[1,68]{1,0:T(1,128)S(1)}, s32[1,68]{1,0:T(1,128)S(1)}, u32[]{:S(2)}, u32[]{:S(2)}) collective-permute-start(s32[1,68]{1,0:T(1,128)S(1)} %pad_add_fusion.codes0), channel_id=1, source_target_pairs={{0,1},{1,0},{2,3},{3,2},{4,5},{5,4},{6,7},{7,6},{8,9},{9,8},{10,11... | collective-permute-start | bytes 824 | tf_op jit(solution)/shard_map/ppermute | solution.py:438
  5.6 12.0 %collective-permute-start = (s32[1,68]{1,0:T(1,128)S(1)}, s32[1,68]{1,0:T(1,128)S(1)}, u32[]{:S(2)}, u32[]{:S(2)}) collective-permute-start(s32[1,68]{1,0:T(1,128)S(1)} %pad_add_fusion.codes0), channel_id=1, source_target_pairs={{0,2},{2,0},{1,3},{3,1},{4,6},{6,4},{5,7},{7,5},{8,10},{10,8},{9,1... | collective-permute-start | bytes 824 | tf_op jit(solution)/shard_map/ppermute | solution.py:438
  7.2 17.7 %collective-permute-start.3 = (bf16[128,256]{1,0:T(8,128)(2,1)}, bf16[128,256]{1,0:T(8,128)(2,1)S(1)}, u32[]{:S(2)}, u32[]{:S(2)}) collective-permute-start(bf16[128,256]{1,0:T(8,128)(2,1)} %param.8), channel_id=1, source_target_pairs={{0,8},{4,12},{8,0},{12,4},{1,9},{5,13},{9,1},{13,5},{2,10},{6,14},... | collective-permute-start | bytes 196616 | tf_op jit(solution)/shard_map/ppermute | solution.py:442
  13.1 13.6 %collective-permute-start.2 = (bf16[128,256]{1,0:T(8,128)(2,1)}, bf16[128,256]{1,0:T(8,128)(2,1)S(1)}, u32[]{:S(2)}, u32[]{:S(2)}) collective-permute-start(bf16[128,256]{1,0:T(8,128)(2,1)} %param.8), channel_id=1, source_target_pairs={{0,4},{4,8},{8,12},{12,0},{1,5},{5,9},{9,13},{13,1},{2,6},{6,10},{... | collective-permute-start | bytes 196616 | tf_op jit(solution)/shard_map/ppermute | solution.py:442
  17.7 9.0 %collective-permute-start.4 = (bf16[128,256]{1,0:T(8,128)(2,1)}, bf16[128,256]{1,0:T(8,128)(2,1)S(1)}, u32[]{:S(2)}, u32[]{:S(2)}) collective-permute-start(bf16[128,256]{1,0:T(8,128)(2,1)} %param.8), channel_id=1, source_target_pairs={{0,12},{4,0},{8,4},{12,8},{1,13},{5,1},{9,5},{13,9},{2,14},{6,2},{... | collective-permute-start | bytes 196616 | tf_op jit(solution)/shard_map/ppermute | solution.py:442
  26.7 19.9 %collective-permute-start.11 = (bf16[1024,256]{1,0:T(8,128)(2,1)S(1)}, bf16[1024,256]{1,0:T(8,128)(2,1)S(1)}, u32[]{:S(2)}, u32[]{:S(2)}) collective-permute-start(bf16[1024,256]{1,0:T(8,128)(2,1)S(1)} %collective-permute-done.5.t2), channel_id=1, source_target_pairs={{0,1},{1,0},{2,3},{3,2},{4,5},{5,4},{6,7},{7,6},{8,9},{9,8},{10,11... | collective-permute-start | bytes 1572872 | tf_op jit(solution)/shard_map/ppermute | solution.py:438
  28.7 13.8 %collective-permute-start.10 = (bf16[4,128,256]{2,1,0:T(8,128)(2,1)S(1)}, bf16[4,128,256]{2,1,0:T(8,128)(2,1)S(1)}, u32[]{:S(2)}, u32[]{:S(2)}) collective-permute-start(bf16[4,128,256]{2,1,0:T(8,128)(2,1)S(1)} %pad_maximum_fusion.own_cells), channel_id=1, source_target_pairs={{0,48},{16,0},{32,16},{48,32},{1,49},{17,1},{33,17},{49,33},{2,50}... | collective-permute-start | bytes 786440 | tf_op jit(solution)/shard_map/ppermute | solution.py:442
  31.2 11.2 %collective-permute-start.9 = (bf16[4,128,256]{2,1,0:T(8,128)(2,1)S(1)}, bf16[4,128,256]{2,1,0:T(8,128)(2,1)S(1)}, u32[]{:S(2)}, u32[]{:S(2)}) collective-permute-start(bf16[4,128,256]{2,1,0:T(8,128)(2,1)S(1)} %pad_maximum_fusion.own_cells), channel_id=1, source_target_pairs={{0,32},{16,48},{32,0},{48,16},{1,33},{17,49},{33,1},{49,17},{2,34}... | collective-permute-start | bytes 786440 | tf_op jit(solution)/shard_map/ppermute | solution.py:442
  31.8 14.8 %collective-permute-start.8 = (bf16[4,128,256]{2,1,0:T(8,128)(2,1)S(1)}, bf16[4,128,256]{2,1,0:T(8,128)(2,1)S(1)}, u32[]{:S(2)}, u32[]{:S(2)}) collective-permute-start(bf16[4,128,256]{2,1,0:T(8,128)(2,1)S(1)} %pad_maximum_fusion.own_cells), channel_id=1, source_target_pairs={{0,16},{16,32},{32,48},{48,0},{1,17},{17,33},{33,49},{49,1},{2,18}... | collective-permute-start | bytes 786440 | tf_op jit(solution)/shard_map/ppermute | solution.py:442
  32.4 1.7 collective-permute-start.7

commit v3 on v2

--- a/solution.py
+++ b/solution.py
@@ -38,7 +38,7 @@
 FAR = "far"
 
 
-def call(kernel, name, ins, outs, scratch, flops=2 << 20, moved=1 << 20, vmem=9):
+def call(kernel, name, ins, outs, scratch, flops=2 << 20, moved=1 << 20, vmem=9, aliases={}):
     in_specs, args = [], []
     for spec, value in ins:
         if spec in (HERE, FAR):
@@ -53,6 +53,7 @@
         in_specs=in_specs,
         out_specs=[spec for spec, _ in outs],
         scratch_shapes=scratch,
+        input_output_aliases=aliases,
         name=name,
         cost_estimate=pl.CostEstimate(flops=flops, bytes_accessed=moved, transcendentals=0),
         compiler_params=pltpu.CompilerParams(vmem_limit_bytes=vmem << 20),
@@ -86,23 +87,24 @@
     lax.fori_loop(0, lax.shift_right_logical(list_ref[SLOTS] + (CHUNK - 1), 3), one, 0)
 
 
+def each_chunk(list_ref, bodies):
+    def one(c, carry):
+        codes = [list_ref[c * CHUNK + step] for step in range(CHUNK)]
+        for body in bodies:
+            for step, code in enumerate(codes):
+                body(step, c * CHUNK + step, lax.shift_right_logical(code, 5), jnp.bitwise_and(code, NB - 1))
+        return carry
+
+    lax.fori_loop(0, lax.shift_right_logical(list_ref[SLOTS] + (CHUNK - 1), 3), one, 0)
+
+
 def part_index():
     return lax.axis_index("zl") * 2 + lax.axis_index("core")
 
 
-def pulls_of(own_cells, more_cells, targets, cells, tbuf, sem):
-    x, zh = lax.axis_index("x"), lax.axis_index("zh")
-    pulls = [
-        pltpu.make_async_copy(targets[0], tbuf.at[0], sem.at[0]),
-        pltpu.make_async_copy(targets[1], tbuf.at[1], sem.at[1]),
-        pltpu.make_async_copy(targets[2], tbuf.at[2], sem.at[2]),
-        pltpu.make_async_copy(targets[3], tbuf.at[3], sem.at[3]),
-    ]
-    for m, piece in enumerate((own_cells, *more_cells)):
-        for k in range(4):
-            place = jnp.bitwise_and(x + (4 - m), 3) * 4 + jnp.bitwise_and(zh + (4 - k), 3)
-            pulls.append(pltpu.make_async_copy(piece.at[k], cells.at[place], sem.at[4 + 4 * m + k]))
-    return pulls
+def pulls_of(cells_far, targets, cells, tbuf, sem):
+    pulls = [pltpu.make_async_copy(target, tbuf.at[r], sem.at[r]) for r, target in enumerate(targets)]
+    return [*pulls, pltpu.make_async_copy(cells_far, cells, sem.at[4])]
 
 
 def write_copies(out_ref, rows, value, first=0):
@@ -137,22 +139,14 @@
     return jnp.where(good, largest + jnp.log(jnp.where(good, so_far, 1.0)), lowest)
 
 
-def scores_kernel(
-    codes0, codes1, codes2, codes3, own_cells, c1, c2, c3, t0, t1, t2, t3, mapping_far, mass_ref,
-    send_ref, list_ref, xbuf,
-    tbuf, cells_ref, mapping_ref, mapped, top, acc, sem,
-):
-    pulls = pulls_of(own_cells, (c1, c2, c3), (t0, t1, t2, t3), cells_ref, tbuf, sem)
-    pulls.append(pltpu.make_async_copy(mapping_far, mapping_ref, sem.at[20]))
-    for pull in pulls:
-        pull.start()
+def plan_kernel(notes0, notes1, notes2, notes3, list_ref):
     part = part_index()
     count = 0
-    for r, codes in enumerate((codes0, codes1, codes2, codes3)):
+    for r, notes in enumerate((notes0, notes1, notes2, notes3)):
         base = jnp.bitwise_xor(part, r) * TB_DEV
 
-        def gather(k, n, codes=codes, base=base):
-            code = codes[0, k]
+        def gather(k, n, notes=notes, base=base):
+            code = notes[0, k].astype(jnp.int32)
             source = lax.shift_right_arithmetic(code, 3)
             take = jnp.logical_and(code >= 0, jnp.bitwise_and(source, 3) == part)
             target = base + jnp.bitwise_and(code, TB_DEV - 1)
@@ -167,7 +161,20 @@
 
     lax.fori_loop(count, jnp.minimum(count + CHUNK, SLOTS), clear, 0)
     list_ref[SLOTS] = count
-    list_ref[SLOTS + 1] = codes0[0, TILES + lax.axis_index("src")]
+    list_ref[SLOTS + 1] = notes0[0, TILES + lax.axis_index("src")].astype(jnp.int32)
+
+
+def scores_kernel(
+    list_ref, cells_far, t0, t1, t2, t3, mapping_far, mass_ref,
+    send_ref, xbuf, _,
+    tbuf, cells_ref, mapping_ref, mapped, top, acc, sem,
+):
+    pulls = pulls_of(cells_far, (t0, t1, t2, t3), cells_ref, tbuf, sem)
+    pulls.append(pltpu.make_async_copy(mapping_far, mapping_ref, sem.at[5]))
+    for pull in pulls:
+        pull.start()
+    part = part_index()
+    count = list_ref[SLOTS]
     for pull in pulls:
         pull.wait()
 
@@ -181,17 +188,18 @@
     lax.fori_loop(0, NA, blank, 0)
     scale = (1.0 / entropy) / math.sqrt(D)
 
-    def product(k, a, b):
+    def product(step, k, a, b):
         slot = jnp.bitwise_xor(lax.shift_right_logical(b, 3), part)
         rows = pl.ds(pl.multiple_of(jnp.bitwise_and(b, TB_DEV - 1) * TILE, TILE), TILE)
         x = lax.dot_general(
             mapped[a], tbuf[slot, rows, :], (((1,), (1,)), ((), ())), preferred_element_type=F32
         )
-        x = jnp.where(k < count, x * scale, lowest)
-        xbuf[k] = x
-        top[a] = jnp.maximum(top[a], x)
-
-    each_tile(list_ref, product)
+        xbuf[k] = jnp.where(k < count, x * scale, lowest)
+
+    def largest(step, k, a, b):
+        top[a] = jnp.maximum(top[a], xbuf[k])
+
+    each_chunk(list_ref, (product, largest))
 
     def spread(a, carry):
         top[a] = jnp.broadcast_to(jnp.max(top[a], axis=1, keepdims=True), (TILE, TILE))
@@ -211,7 +219,7 @@
 
 
 def first_targets_kernel(
-    list_ref, recv_ref, xbuf, mass_ref,
+    list_ref, recv_ref, xbuf, _,
     send_ref, u_ref, mass_out,
     col, top, acc,
 ):
@@ -239,16 +247,16 @@
         row = finish_log(top[b][0:1], jnp.sum(acc[b], axis=0, keepdims=True))
         for d in range(16):
             send_ref[d, b : b + 1] = row
-    write_copies(send_ref, TB_DEV, mass_ref[...], NB)
 
 
 def kernel_matrix_kernel(
-    list_ref, recv_ref, u_ref, xbuf,
+    list_ref, recv_ref, u_ref, notes0, notes1, notes2, notes3, xbuf, _,
     send_ref, v_ref, mass_out, kbuf,
     col, acc,
 ):
-    for p in range(4):
-        mass_out[p * TB_DEV : (p + 1) * TB_DEV] = recv_ref[p, NB : NB + TB_DEV]
+    for r, notes in enumerate((notes0, notes1, notes2, notes3)):
+        first = pl.multiple_of(jnp.bitwise_xor(part_index(), r) * TB_DEV, TB_DEV)
+        mass_out[pl.ds(first, TB_DEV)] = notes[TB_DEV : 2 * TB_DEV]
     v_ref[...] = mass_out[...] - merged(recv_ref, NB)
     for a in range(NA):
         col[a] = column_form(u_ref[a : a + 1])
@@ -266,9 +274,11 @@
             send_ref[d, a : a + 1] = row
 
 
-def columns_kernel(list_ref, recv_ref, mass_ref, kbuf, _, send_ref, alpha_ref, col, acc):
+def columns_kernel(list_ref, recv_ref, mass_ref, kbuf, _, send_ref, *rest):
+    *kept, col, acc = rest
     alpha = jnp.where(live_rows(list_ref), jnp.exp(mass_ref[...]) / total(recv_ref, 0, NA), 1.0)
-    alpha_ref[...] = alpha
+    for ref in kept:
+        ref[...] = alpha
     for a in range(NA):
         col[a] = column_form(alpha[a : a + 1])
     acc[...] = jnp.zeros((NB, 8, TILE), F32)
@@ -322,13 +332,12 @@
 
 def first_ratio_kernel(
     list_ref, recv_ref, alpha_ref, kbuf, xbuf,
-    send_ref, sum_ref, s_ref, cost_ref,
+    send_ref, sum_ref, cost_ref,
     col, col2, acc, acc2,
 ):
     row_sum = total(recv_ref, 0, NA)
     sum_ref[...] = row_sum
     s = jnp.where(live_rows(list_ref), -total(recv_ref, NA, NA) / row_sum, 0.0)
-    s_ref[...] = s
     for a in range(NA):
         col[a] = column_form(alpha_ref[a : a + 1])
         col2[a] = column_form(s[a : a + 1] * damping)
@@ -366,11 +375,12 @@
 
 def push_kernel(
     list_ref, recv_ref, sum_ref, alpha_ref, cost_ref, kbuf, _,
-    send_ref, s_ref,
-    col, acc,
-):
+    send_ref, *rest,
+):
+    *kept, col, acc = rest
     s = jnp.where(live_rows(list_ref), -total(recv_ref, 0, NA) / sum_ref[...], 0.0)
-    s_ref[...] = s
+    for ref in kept:
+        ref[...] = s
     weight = alpha_ref[...] * s * damping
     for a in range(NA):
         col[a] = column_form(weight[a : a + 1])
@@ -385,11 +395,11 @@
 
 def gradient_kernel(
     list_ref, recv_ref, sum_ref, beta_ref, alpha_ref, s_ref, u_ref, v_ref,
-    own_cells, c1, c2, c3, t0, t1, t2, t3, xbuf,
+    cells_far, t0, t1, t2, t3, xbuf,
     g_ref, source_ref, target_ref,
-    tbuf, cells_ref, col, col2, trow, vrow, prod, sem,
-):
-    pulls = pulls_of(own_cells, (c1, c2, c3), (t0, t1, t2, t3), cells_ref, tbuf, sem)
+    tbuf, cells_ref, col, col2, trow, vrow, prod, wbuf, pbuf, sem,
+):
+    pulls = pulls_of(cells_far, (t0, t1, t2, t3), cells_ref, tbuf, sem)
     for pull in pulls:
         pull.start()
     part = part_index()
@@ -407,16 +417,20 @@
     for pull in pulls:
         pull.wait()
 
-    def add(k, a, b):
+    def weigh(step, k, a, b):
+        x = xbuf[k]
+        weights = jnp.exp(x + col[a] + vrow[pl.ds(b, 1)]) * (x + col2[a] + trow[pl.ds(b, 1)])
+        wbuf[step] = weights.astype(jnp.bfloat16)
+
+    def multiply(step, k, a, b):
         slot = jnp.bitwise_xor(lax.shift_right_logical(b, 3), part)
         rows = pl.ds(pl.multiple_of(jnp.bitwise_and(b, TB_DEV - 1) * TILE, TILE), TILE)
-        x = xbuf[k]
-        weights = jnp.exp(x + col[a] + vrow[pl.ds(b, 1)]) * (x + col2[a] + trow[pl.ds(b, 1)])
-        prod[a] += jnp.dot(
-            weights.astype(jnp.bfloat16), tbuf[slot, rows, :], preferred_element_type=F32
-        )
-
-    each_tile(list_ref, add)
+        pbuf[step] = jnp.dot(wbuf[step], tbuf[slot, rows, :], preferred_element_type=F32)
+
+    def add(step, k, a, b):
+        prod[a] += pbuf[step]
+
+    each_chunk(list_ref, (weigh, multiply, add))
     contract = (((0,), (0,)), ((), ()))
 
     def outer(a, so_far):
@@ -438,10 +452,6 @@
     return lax.ppermute(value, axis, [(0, 1), (1, 0)])
 
 
-def shifted(value, axis):
-    return [lax.ppermute(value, axis, [(i, (i + k) % 4) for i in range(4)]) for k in (1, 2, 3)]
-
-
 def row_exchange(value):
     return lax.all_to_all(value, ROW, 0, 0)
 
@@ -461,21 +471,24 @@
     tile_target,
 ):
     codes = jnp.where(tile_source >= 0, tile_source * TB_DEV + tile_target, -1)
-    codes0 = jnp.concatenate([codes, group_blocks.reshape(1, 4)], axis=1)
+    head = jnp.concatenate([codes, group_blocks.reshape(1, 4)], axis=1).astype(F32)
+    note = jnp.concatenate(
+        [jnp.pad(head, ((0, 7), (0, TILE - TILES - 4))), target_logmass.astype(F32).reshape(TB_DEV, TILE)]
+    )
     first = (
-        swap(codes0, "zl"),
-        swap(codes0, "core"),
-        *shifted(source_cells, "zh"),
-        swap(target_cells, "zl"),
+        lax.all_to_all(jnp.broadcast_to(source_cells[None], (4, TILE, D)), "zh", 0, 0),
+        swap(note, "zl"),
+        swap(note, "core"),
         swap(target_cells, "core"),
         source_logmass.astype(F32).reshape(1, TILE),
-        target_logmass.astype(F32).reshape(TB_DEV, TILE),
-    )
-    codes2, codes1, z1, z2, z3, t2, t1, own_mass, own_target_mass = lax.optimization_barrier(first)
-    codes3 = swap(codes2, "core")
-    own_cells = jnp.stack([source_cells, z1, z2, z3])
-    cells = (own_cells, *shifted(own_cells, "x"))
+        target_cells,
+    )
+    column_cells, note2, note1, t1, own_mass, t0 = lax.optimization_barrier(first)
+    t2 = swap(t0, "zl")
+    notes = (note, note1, note2, swap(note2, "core"))
     targets = (target_cells, t1, t2, swap(t2, "core"))
+    cells = lax.all_to_all(jnp.broadcast_to(column_cells[None], (4, 4, TILE, D)), "x", 0, 0)
+    cells = cells.reshape(NA, TILE, D)
 
     rows_to = (VM, SHAPE((16, NA, TILE), F32))
     cols_to = (VM, SHAPE((16, NB, TILE), F32))
@@ -488,17 +501,24 @@
         pltpu.VMEM((4, TB_DEV * TILE, D), jnp.bfloat16),
         pltpu.VMEM((NA, TILE, D), jnp.bfloat16),
     ]
-    gathered_sems = pltpu.SemaphoreType.DMA((21,))
-    gathered_refs = [(ANY, value) for value in cells] + [(FAR, targets[0])] + [(ANY, value) for value in targets[1:]]
-
-    send, tile_list, x = call(
+    gathered_sems = pltpu.SemaphoreType.DMA((6,))
+    gathered_refs = [(ANY, cells), (FAR, targets[0]), *[(ANY, value) for value in targets[1:]]]
+
+    (tile_list,) = call(
+        plan_kernel,
+        "plan",
+        [(SM, note) for note in notes],
+        [(SM, SHAPE((SLOTS + 8,), jnp.int32))],
+        [],
+    )
+    send, x, k = call(
         scores_kernel,
         "scores",
         [
-            (SM, codes0), (SM, codes1), (SM, codes2), (SM, codes3), *gathered_refs,
+            (SM, tile_list), *gathered_refs,
             (FAR, mapping), (VM, own_mass),
         ],
-        [(VM, SHAPE((16, NA + 8, TILE), F32)), (SM, SHAPE((SLOTS + 8,), jnp.int32)), tiles],
+        [(VM, SHAPE((16, NA + 8, TILE), F32)), tiles, tiles],
         [
             *gathered, pltpu.VMEM((D, D), jnp.bfloat16), pltpu.VMEM((NA, TILE, D), jnp.bfloat16),
             row_blocks, row_blocks, gathered_sems,
@@ -509,37 +529,39 @@
     send, u, source_mass = call(
         first_targets_kernel,
         "first_targets",
-        [tile_list, (VM, recv), x, (VM, own_target_mass)],
-        [(VM, SHAPE((16, NB + TB_DEV, TILE), F32)), rows_state, rows_state],
+        [tile_list, (VM, recv), x, (HERE, k)],
+        [cols_to, rows_state, rows_state],
         [row_blocks, col_rows, col_rows],
     )
     recv = col_exchange(send)
     send, v, target_mass, k = call(
         kernel_matrix_kernel,
         "kernel_matrix",
-        [tile_list, (VM, recv), (VM, u), x],
+        [tile_list, (VM, recv), (VM, u), *[(VM, note) for note in notes], x, (HERE, k)],
         [rows_to, cols_state, cols_state, tiles],
         [row_blocks, row_blocks],
+        aliases={8: 3},
     )
     k = (HERE, k)
     for sweep in range(1, SINK):
         recv = row_exchange(send)
-        send, alpha = call(
+        send, *kept = call(
             columns_kernel,
             "columns",
             [tile_list, (VM, recv), (VM, source_mass), k, x],
-            [cols_to, rows_state],
+            [cols_to, *([rows_state] if sweep == SINK - 1 else [])],
             [row_blocks, col_rows],
         )
         recv = col_exchange(send)
         if sweep < SINK - 1:
-            send, _ = call(
+            (send,) = call(
                 rows_kernel,
                 "rows",
                 [tile_list, (VM, recv), (VM, target_mass), k, x],
-                [rows_to, cols_state],
-                [row_blocks],
+                [rows_to],
+                [pltpu.VMEM((NB, TILE), F32), row_blocks],
             )
+    (alpha,) = kept
     send, beta, column_sum, row_cost = call(
         masses_kernel,
         "masses",
@@ -548,15 +570,15 @@
         [row_blocks, row_blocks],
     )
     recv = row_exchange(send)
-    send, row_sum, s, column_cost = call(
+    send, row_sum, column_cost = call(
         first_ratio_kernel,
         "first_ratio",
         [tile_list, (VM, recv), (VM, alpha), k, x],
-        [cols_to, rows_state, rows_state, cols_state],
+        [cols_to, rows_state, cols_state],
         [row_blocks, row_blocks, col_rows, col_rows],
     )
     recv = col_exchange(send)
-    for _ in range(1, ADJ):
+    for step in range(1, ADJ):
         (send,) = call(
             pull_kernel,
             "pull",
@@ -565,14 +587,15 @@
             [row_blocks, pltpu.VMEM((NB, TILE), F32)],
         )
         recv = row_exchange(send)
-        send, s = call(
+        send, *kept = call(
             push_kernel,
             "push",
             [tile_list, (VM, recv), (VM, row_sum), (VM, alpha), (VM, column_cost), k, x],
-            [cols_to, rows_state],
+            [cols_to, *([rows_state] if step == ADJ - 1 else [])],
             [row_blocks, col_rows],
         )
         recv = col_exchange(send)
+    (s,) = kept
     gradient, own_source, own_target = call(
         gradient_kernel,
         "gradient",
@@ -583,7 +606,8 @@
         [(VM, SHAPE((D, D), F32)), (VM, SHAPE((1, TILE), F32)), (VM, SHAPE((TB_DEV, TILE), F32))],
         [
             *gathered, row_blocks, row_blocks, pltpu.VMEM((NB, TILE), F32), pltpu.VMEM((NB, TILE), F32),
-            pltpu.VMEM((NA, TILE, D), F32), gathered_sems,
+            pltpu.VMEM((NA, TILE, D), F32),
+            pltpu.VMEM((CHUNK, TILE, TILE), jnp.bfloat16), pltpu.VMEM((CHUNK, TILE, D), F32), gathered_sems,
         ],
     )
     piece = jnp.sum(col_exchange(gradient.reshape(16, 16, D)), axis=0)

time: 342 us -> 331 us (0.968)
  Pallas kernels: 52.7 us -> 36.9 us
  blocking collectives: 242 us -> 257 us
  waiting for transfers between devices: 19.6 us -> 8.67 us
    pallas_call x17 -> x18, Pallas kernels: 52.7 us -> 36.9 us  [call(): pl.pallas_call(kernel, out_shape=[shape for _, shape in outs], in_specs=i...]
    ppermute x6 -> x0, starting transfers between devices: 15.6 us -> none  [shifted(): lax.ppermute(value, axis, [(i, (i + k) % 4) for i in range(4)])]
    ppermute x6 -> x0, waiting for transfers between devices: 15.4 us -> none  [shifted(): lax.ppermute(value, axis, [(i, (i + k) % 4) for i in range(4)])]
    all_to_all x0 -> x2, starting transfers between devices: none -> 13 us  [the longest x1 9.01 us: shards(): lax.all_to_all(jnp.broadcast_to(source_cells[None], (4, TILE, D)), 'zh',...]
    all_to_all x10, blocking collectives: 120 us -> 132 us  [col_exchange(): return lax.all_to_all(value, COL, 0, 0)]
  transfers between devices with their start and end apart: 12 -> 8, of which waited for: 6 -> 4; matrix products, arithmetic and copies ran while one was open for 1% -> 1% of each run, Pallas kernels for 0% -> 1%
where the time goes in v3:
time: 331 us; the launch traced here: 330 us
  blocking collectives  257 us (78%)
  Pallas kernels  36.9 us (11%)
  starting transfers between devices  20.8 us (6%)
  waiting for transfers between devices  8.67 us (3%)
  local copies, waits for them, and re-layouts  3.38 us (1%)
    all_to_all x10, blocking collectives, col_exchange(): return lax.all_to_all(value, COL, 0, 0)  132 us
    all_to_all x9, blocking collectives, row_exchange(): return lax.all_to_all(value, ROW, 0, 0)  125 us
    pallas_call x18, Pallas kernels, call(): pl.pallas_call(kernel, out_shape=[shape for _, shape in outs], in_specs=i...  36.9 us
    all_to_all x1, starting transfers between devices, shards(): lax.all_to_all(jnp.broadcast_to(source_cells[None], (4, TILE, D)), 'zh',...  9.01 us
    ppermute x6, starting transfers between devices, swap(): return lax.ppermute(value, axis, [(0, 1), (1, 0)])  7.75 us
  transfers between devices with their start and end apart: 8, of which 4 were waited for; matrix products, arithmetic and copies ran while one was open for 1% of the time, Pallas kernels for 1%

profile of v3, /device:TPU:1, one launch (start us, length us, event | category | flops | bytes accessed | tf_op | source)
XLA Modules:
  0.0 330.0 jit_solution(1473966053405765124)
XLA Ops:
  2.2 9.0 %all-to-all-start = ((bf16[4,128,256]{2,1,0:T(8,128)(2,1)}), bf16[4,128,256]{2,1,0:T(8,128)(2,1)S(1)}, u32[]{:S(2)}, u32[]{:S(2)}) async-start(bf16[4,128,256]{2,1,0:T(8,128)(2,1)} %broadcast_in_dim.13), calls=%async_computation | async-start | bytes 524288 | tf_op jit(solution)/shard_map/all_to_all | solution.py:479
  21.2 4.0 %all-to-all-start.1 = ((bf16[4,4,128,256]{3,2,1,0:T(8,128)(2,1)}), bf16[4,4,128,256]{3,2,1,0:T(8,128)(2,1)S(1)}, u32[]{:S(2)}, u32[]{:S(2)}) async-start(bf16[4,4,128,256]{3,2,1,0:T(8,128)(2,1)} %broadcast_in_dim.14), calls=%async_computation.1 | async-start | bytes 2097152 | tf_op jit(solution)/shard_map/all_to_all | solution.py:490
  28.7 5.2 %collective-permute-start.5 = (bf16[1024,256]{1,0:T(8,128)(2,1)S(1)}, bf16[1024,256]{1,0:T(8,128)(2,1)S(1)}, u32[]{:S(2)}, u32[]{:S(2)}) collective-permute-start(bf16[1024,256]{1,0:T(8,128)(2,1)S(1)} %collective-permute-done.4.t2), channel_id=1, source_target_pairs={{0,1},{1,0},{2,3},{3,2},{4,5},{5,4},{6,7},{7,6},{8,9},{9,8},{10,11... | collective-permute-start | bytes 1572872 | tf_op jit(solution)/shard_map/ppermute | solution.py:452
  38.9 7.3 %scores.1 = (f32[16,24,128]{2,1,0:T(8,128)S(1)}, f32[256,128,128]{2,1,0:T(8,128)S(1)}, f32[256,128,128]{2,1,0:T(8,128)S(1)}) custom-call(s32[264]{0:T(512)S(1)} %plan.1.list_ref, bf16[16,128,256]{2,1,0:T(8,128)(2,1)S(1)} %bitcast.12, bf16[1024,256]{1,0:T(8,128)(2,1)} %t0.3, bf16[1024,256]{1,0:T(8,128)(2,1)S(1)} %collective-permute-done.2.t1, ...), custom_call_target="tpu_custom_call" | custom-call | flops 2097152 | bytes 1048576 | tf_op jit(solution)/shard_map/scores/pallas_call | solution.py:50
  46.2 19.4 %all_to_all.105.recv_ref = f32[16,24,128]{2,1,0:T(8,128)S(1)} all-to-all(f32[16,24,128]{2,1,0:T(8,128)S(1)} %get-tuple-element.39), channel_id=1, replica_groups=mesh['src'=4,'x'=4,'zh'=4,'zl'=2,'core'=2] {'x','zh'}, dimensions={0} | all-to-all | bytes 393216 | tf_op jit(solution)/shard_map/all_to_all | solution.py:456
  67.2 17.1 %all_to_all.106.recv_ref = f32[16,32,128]{2,1,0:T(8,128)S(1)} all-to-all(f32[16,32,128]{2,1,0:T(8,128)S(1)} %get-tuple-element.42), channel_id=1, replica_groups=mesh['src'=4,'x'=4,'zh'=4,'zl'=2,'core'=2] {'src','zl','core'}, dimensions={0} | all-to-all | bytes 524288 | tf_op jit(solution)/shard_map/all_to_all | solution.py:460
  85.8 13.0 %all_to_all.107.recv_ref = f32[16,16,128]{2,1,0:T(8,128)S(1)} all-to-all(f32[16,16,128]{2,1,0:T(8,128)S(1)} %get-tuple-element.44), channel_id=1, replica_groups=mesh['src'=4,'x'=4,'zh'=4,'zl'=2,'core'=2] {'x','zh'}, dimensions={0} | all-to-all | bytes 262144 | tf_op jit(solution)/shard_map/all_to_all | solution.py:456
  99.9 12.6 %all_to_all.108.recv_ref = f32[16,32,128]{2,1,0:T(8,128)S(1)} all-to-all(f32[16,32,128]{2,1,0:T(8,128)S(1)} %columns.3), channel_id=1, replica_groups=mesh['src'=4,'x'=4,'zh'=4,'zl'=2,'core'=2] {'src','zl','core'}, dimensions={0} | all-to-all | bytes 524288 | tf_op jit(solution)/shard_map/all_to_all | solution.py:460
  113.6 12.9 %all_to_all.109.recv_ref = f32[16,16,128]{2,1,0:T(8,128)S(1)} all-to-all(f32[16,16,128]{2,1,0:T(8,128)S(1)} %rows.2), channel_id=1, replica_groups=mesh['src'=4,'x'=4,'zh'=4,'zl'=2,'core'=2] {'x','zh'}, dimensions={0} | all-to-all | bytes 262144 | tf_op jit(solution)/shard_map/all_to_all | solution.py:456
  127.7 12.2 %all_to_all.110.recv_ref = f32[16,32,128]{2,1,0:T(8,128)S(1)} all-to-all(f32[16,32,128]{2,1,0:T(8,128)S(1)} %columns.4), channel_id=1, replica_groups=mesh['src'=4,'x'=4,'zh'=4,'zl'=2,'core'=2] {'src','zl','core'}, dimensions={0} | all-to-all | bytes 524288 | tf_op jit(solution)/shard_map/all_to_all | solution.py:460
  141.0 13.0 %all_to_all.111.recv_ref = f32[16,16,128]{2,1,0:T(8,128)S(1)} all-to-all(f32[16,16,128]{2,1,0:T(8,128)S(1)} %rows.3), channel_id=1, replica_groups=mesh['src'=4,'x'=4,'zh'=4,'zl'=2,'core'=2] {'x','zh'}, dimensions={0} | all-to-all | bytes 262144 | tf_op jit(solution)/shard_map/all_to_all | solution.py:456
  155.1 12.3 %all_to_all.112.recv_ref = f32[16,32,128]{2,1,0:T(8,128)S(1)} all-to-all(f32[16,32,128]{2,1,0:T(8,128)S(1)} %get-tuple-element.48), channel_id=1, replica_groups=mesh['src'=4,'x'=4,'zh'=4,'zl'=2,'core'=2] {'src','zl','core'}, dimensions={0} | all-to-all | bytes 524288 | tf_op jit(solution)/shard_map/all_to_all | solution.py:460
  169.0 13.9 %all_to_all.113.recv_ref = f32[16,32,128]{2,1,0:T(8,128)S(1)} all-to-all(f32[16,32,128]{2,1,0:T(8,128)S(1)} %get-tuple-element.49), channel_id=1, replica_groups=mesh['src'=4,'x'=4,'zh'=4,'zl'=2,'core'=2] {'x','zh'}, dimensions={0} | all-to-all | bytes 524288 | tf_op jit(solution)/shard_map/all_to_all | solution.py:456
  184.6 15.0 %all_to_all.114.recv_ref = f32[16,32,128]{2,1,0:T(8,128)S(1)} all-to-all(f32[16,32,128]{2,1,0:T(8,128)S(1)} %get-tuple-element.51), channel_id=1, replica_groups=mesh['src'=4,'x'=4,'zh'=4,'zl'=2,'core'=2] {'src','zl','core'}, dimensions={0} | all-to-all | bytes 524288 | tf_op jit(solution)/shard_map/all_to_all | solution.py:460
  200.7 12.7 %all_to_all.115.recv_ref = f32[16,16,128]{2,1,0:T(8,128)S(1)} all-to-all(f32[16,16,128]{2,1,0:T(8,128)S(1)} %pull.3), channel_id=1, replica_groups=mesh['src'=4,'x'=4,'zh'=4,'zl'=2,'core'=2] {'x','zh'}, dimensions={0} | all-to-all | bytes 262144 | tf_op jit(solution)/shard_map/all_to_all | solution.py:456
  214.5 12.5 %all_to_all.116.recv_ref = f32[16,32,128]{2,1,0:T(8,128)S(1)} all-to-all(f32[16,32,128]{2,1,0:T(8,128)S(1)} %push.3), channel_id=1, replica_groups=mesh['src'=4,'x'=4,'zh'=4,'zl'=2,'core'=2] {'src','zl','core'}, dimensions={0} | all-to-all | bytes 524288 | tf_op jit(solution)/shard_map/all_to_all | solution.py:460
  228.2 12.9 %all_to_all.117.recv_ref = f32[16,16,128]{2,1,0:T(8,128)S(1)} all-to-all(f32[16,16,128]{2,1,0:T(8,128)S(1)} %pull.4), channel_id=1, replica_groups=mesh['src'=4,'x'=4,'zh'=4,'zl'=2,'core'=2] {'x','zh'}, dimensions={0} | all-to-all | bytes 262144 | tf_op jit(solution)/shard_map/all_to_all | solution.py:456
  242.3 12.3 %all_to_all.118.recv_ref = f32[16,32,128]{2,1,0:T(8,128)S(1)} all-to-all(f32[16,32,128]{2,1,0:T(8,128)S(1)} %push.4), channel_id=1, replica_groups=mesh['src'=4,'x'=4,'zh'=4,'zl'=2,'core'=2] {'src','zl','core'}, dimensions={0} | all-to-all | bytes 524288 | tf_op jit(solution)/shard_map/all_to_all | solution.py:460
  255.7 12.9 %all_to_all.119.recv_ref = f32[16,16,128]{2,1,0:T(8,128)S(1)} all-to-all(f32[16,16,128]{2,1,0:T(8,128)S(1)} %pull.5), channel_id=1, replica_groups=mesh['src'=4,'x'=4,'zh'=4,'zl'=2,'core'=2] {'x','zh'}, dimensions={0} | all-to-all | bytes 262144 | tf_op jit(solution)/shard_map/all_to_all | solution.py:456
  269.7 12.5 %all_to_all.120.recv_ref = f32[16,32,128]{2,1,0:T(8,128)S(1)} all-to-all(f32[16,32,128]{2,1,0:T(8,128)S(1)} %get-tuple-element.57), channel_id=1, replica_groups=mesh['src'=4,'x'=4,'zh'=4,'zl'=2,'core'=2] {'src','zl','core'}, dimensions={0} | all-to-all | bytes 524288 | tf_op jit(solution)/shard_map/all_to_all | solution.py:460
  282.2 7.4 %gradient.1 = (f32[256,256]{1,0:T(8,128)S(1)}, f32[1,128]{1,0:T(1,128)}, f32[8,128]{1,0:T(8,128)}) custom-call(s32[264]{0:T(512)S(1)} %plan.1.list_ref, f32[16,32,128]{2,1,0:T(8,128)S(1)} %all_to_all.120.recv_ref, f32[32,128]{1,0:T(8,128)S(1)} %get-tuple-element.52.sum_ref, f32[32,128]{1,0:T(8,128)S(1)} %get-tuple-element.53.beta_ref, ...), custom_call_target="tpu_custom_call" | custom-call | flops 2097152 | bytes 1048576 | tf_op jit(solution)/shard_map/gradient/pallas_call | solution.py:50
  289.7 12.4 %all_to_all.121 = f32[16,16,256]{2,1,0:T(8,128)S(1)} all-to-all(f32[16,16,256]{2,1,0:T(8,128)S(1)} %bitcast.14), channel_id=1, replica_groups=mesh['src'=4,'x'=4,'zh'=4,'zl'=2,'core'=2] {'src','zl','core'}, dimensions={0} | all-to-all | bytes 524288 | tf_op jit(solution)/shard_map/all_to_all | solution.py:460
  302.1 14.1 %all_to_all.122 = f32[16,16,256]{2,1,0:T(8,128)S(1)} all-to-all(f32[16,16,256]{2,1,0:T(8,128)S(1)} %broadcast_in_dim.15), channel_id=1, replica_groups=mesh['src'=4,'x'=4,'zh'=4,'zl'=2,'core'=2] {'x','zh'}, dimensions={0} | all-to-all | bytes 524288 | tf_op jit(solution)/shard_map/all_to_all | solution.py:456
  316.3 13.0 %all_to_all.123 = f32[16,16,256]{2,1,0:T(8,128)S(1)} all-to-all(f32[16,16,256]{2,1,0:T(8,128)S(1)} %broadcast_in_dim.16), channel_id=1, replica_groups=mesh['src'=4,'x'=4,'zh'=4,'zl'=2,'core'=2] {'src','zl','core'}, dimensions={0} | all-to-all | bytes 524288 | tf_op jit(solution)/shard_map/all_to_all | solution.py:460
  (41 shorter events, 39.5 us)
Async XLA Ops:
  2.2 17.2 %all-to-all-start = ((bf16[4,128,256]{2,1,0:T(8,128)(2,1)}), bf16[4,128,256]{2,1,0:T(8,128)(2,1)S(1)}, u32[]{:S(2)}, u32[]{:S(2)}) async-start(bf16[4,128,256]{2,1,0:T(8,128)(2,1)} %broadcast_in_dim.13), calls=%async_computation | async-start | bytes 524288 | tf_op jit(solution)/shard_map/all_to_all | solution.py:479
  11.2 8.2 %collective-permute-start.2 = (bf16[1024,256]{1,0:T(8,128)(2,1)}, bf16[1024,256]{1,0:T(8,128)(2,1)S(1)}, u32[]{:S(2)}, u32[]{:S(2)}) collective-permute-start(bf16[1024,256]{1,0:T(8,128)(2,1)} %t0.3), channel_id=1, source_target_pairs={{0,1},{1,0},{2,3},{3,2},{4,5},{5,4},{6,7},{7,6},{8,9},{9,8},{10,11... | collective-permute-start | bytes 1572872 | tf_op jit(solution)/shard_map/ppermute | solution.py:452
  14.2 1.5 collective-permute-start.1
  14.3 2.7 collective-permute-start
  19.4 9.3 %collective-permute-start.4 = (bf16[1024,256]{1,0:T(8,128)(2,1)}, bf16[1024,256]{1,0:T(8,128)(2,1)S(1)}, u32[]{:S(2)}, u32[]{:S(2)}) collective-permute-start(bf16[1024,256]{1,0:T(8,128)(2,1)} %t0.3), channel_id=1, source_target_pairs={{0,2},{2,0},{1,3},{3,1},{4,6},{6,4},{5,7},{7,5},{8,10},{10,8},{9,1... | collective-permute-start | bytes 1572872 | tf_op jit(solution)/shard_map/ppermute | solution.py:452
  21.2 17.7 %all-to-all-start.1 = ((bf16[4,4,128,256]{3,2,1,0:T(8,128)(2,1)}), bf16[4,4,128,256]{3,2,1,0:T(8,128)(2,1)S(1)}, u32[]{:S(2)}, u32[]{:S(2)}) async-start(bf16[4,4,128,256]{3,2,1,0:T(8,128)(2,1)} %broadcast_in_dim.14), calls=%async_computation.1 | async-start | bytes 2097152 | tf_op jit(solution)/shard_map/all_to_all | solution.py:490
  28.7 10.2 %collective-permute-start.5 = (bf16[1024,256]{1,0:T(8,128)(2,1)S(1)}, bf16[1024,256]{1,0:T(8,128)(2,1)S(1)}, u32[]{:S(2)}, u32[]{:S(2)}) collective-permute-start(bf16[1024,256]{1,0:T(8,128)(2,1)S(1)} %collective-permute-done.4.t2), channel_id=1, source_target_pairs={{0,1},{1,0},{2,3},{3,2},{4,5},{5,4},{6,7},{7,6},{8,9},{9,8},{10,11... | collective-permute-start | bytes 1572872 | tf_op jit(solution)/shard_map/ppermute | solution.py:452
  33.9 1.5 collective-permute-start.3

commit v4 on v3

--- a/solution.py
+++ b/solution.py
@@ -38,7 +38,7 @@
 FAR = "far"
 
 
-def call(kernel, name, ins, outs, scratch, flops=2 << 20, moved=1 << 20, vmem=9, aliases={}):
+def call(kernel, name, ins, outs, scratch, flops=2 << 20, moved=1 << 20, vmem=10, aliases={}):
     in_specs, args = [], []
     for spec, value in ins:
         if spec in (HERE, FAR):
@@ -102,9 +102,8 @@
     return lax.axis_index("zl") * 2 + lax.axis_index("core")
 
 
-def pulls_of(cells_far, targets, cells, tbuf, sem):
-    pulls = [pltpu.make_async_copy(target, tbuf.at[r], sem.at[r]) for r, target in enumerate(targets)]
-    return [*pulls, pltpu.make_async_copy(cells_far, cells, sem.at[4])]
+def pulls_of(targets, tbuf, sem):
+    return [pltpu.make_async_copy(target, tbuf.at[r], sem.at[r]) for r, target in enumerate(targets)]
 
 
 def write_copies(out_ref, rows, value, first=0):
@@ -165,34 +164,37 @@
 
 
 def scores_kernel(
-    list_ref, cells_far, t0, t1, t2, t3, mapping_far, mass_ref,
+    list_ref, cells_ref, t0, t1, t2, t3, mapping_far, mass_ref,
     send_ref, xbuf, _,
-    tbuf, cells_ref, mapping_ref, mapped, top, acc, sem,
-):
-    pulls = pulls_of(cells_far, (t0, t1, t2, t3), cells_ref, tbuf, sem)
-    pulls.append(pltpu.make_async_copy(mapping_far, mapping_ref, sem.at[5]))
+    tbuf, mapping_ref, mapped, top, acc, sem,
+):
+    pull_mapping = pltpu.make_async_copy(mapping_far, mapping_ref, sem.at[4])
+    pull_mapping.start()
+    pulls = pulls_of((t0, t1, t2, t3), tbuf, sem)
     for pull in pulls:
         pull.start()
     part = part_index()
     count = list_ref[SLOTS]
+    top[...] = jnp.full((NA, TILE, TILE), lowest, F32)
+    acc[...] = jnp.zeros((NA, TILE, TILE), F32)
+    pull_mapping.wait()
+
+    def embed(step, carry):
+        rows = pl.ds(pl.multiple_of(step * 2 * D, 2 * D), 2 * D)
+        product = jnp.dot(cells_ref[rows], mapping_ref[...], preferred_element_type=F32)
+        mapped[rows] = product.astype(jnp.bfloat16)
+        return carry
+
+    lax.fori_loop(0, NA * TILE // (2 * D), embed, 0)
     for pull in pulls:
         pull.wait()
-
-    def blank(a, carry):
-        top[a] = jnp.full((TILE, TILE), lowest, F32)
-        acc[a] = jnp.zeros((TILE, TILE), F32)
-        product = jnp.dot(cells_ref[a], mapping_ref[...], preferred_element_type=F32)
-        mapped[a] = product.astype(jnp.bfloat16)
-        return carry
-
-    lax.fori_loop(0, NA, blank, 0)
     scale = (1.0 / entropy) / math.sqrt(D)
 
     def product(step, k, a, b):
         slot = jnp.bitwise_xor(lax.shift_right_logical(b, 3), part)
         rows = pl.ds(pl.multiple_of(jnp.bitwise_and(b, TB_DEV - 1) * TILE, TILE), TILE)
         x = lax.dot_general(
-            mapped[a], tbuf[slot, rows, :], (((1,), (1,)), ((), ())), preferred_element_type=F32
+            mapped[pl.ds(pl.multiple_of(a * TILE, TILE), TILE)], tbuf[slot, rows, :], (((1,), (1,)), ((), ())), preferred_element_type=F32
         )
         xbuf[k] = jnp.where(k < count, x * scale, lowest)
 
@@ -395,11 +397,11 @@
 
 def gradient_kernel(
     list_ref, recv_ref, sum_ref, beta_ref, alpha_ref, s_ref, u_ref, v_ref,
-    cells_far, t0, t1, t2, t3, xbuf,
+    cells_ref, t0, t1, t2, t3, xbuf,
     g_ref, source_ref, target_ref,
-    tbuf, cells_ref, col, col2, trow, vrow, prod, wbuf, pbuf, sem,
-):
-    pulls = pulls_of(cells_far, (t0, t1, t2, t3), cells_ref, tbuf, sem)
+    tbuf, col, col2, trow, vrow, prod, wbuf, pbuf, sem,
+):
+    pulls = pulls_of((t0, t1, t2, t3), tbuf, sem)
     for pull in pulls:
         pull.start()
     part = part_index()
@@ -413,7 +415,7 @@
     for a in range(NA):
         col[a] = column_form(u[a : a + 1])
         col2[a] = column_form(1.0 + s_ref[a : a + 1])
-    prod[...] = jnp.zeros((NA, TILE, D), F32)
+    prod[...] = jnp.zeros((NA * TILE, D), F32)
     for pull in pulls:
         pull.wait()
 
@@ -428,23 +430,15 @@
         pbuf[step] = jnp.dot(wbuf[step], tbuf[slot, rows, :], preferred_element_type=F32)
 
     def add(step, k, a, b):
-        prod[a] += pbuf[step]
+        prod[pl.ds(pl.multiple_of(a * TILE, TILE), TILE)] += pbuf[step]
 
     each_chunk(list_ref, (weigh, multiply, add))
-    contract = (((0,), (0,)), ((), ()))
-
-    def outer(a, so_far):
-        value = prod[a]
-        high = value.astype(jnp.bfloat16)
-        rest = value - high.astype(F32)
-        middle = rest.astype(jnp.bfloat16)
-        low = (rest - middle.astype(F32)).astype(jnp.bfloat16)
-        cells = cells_ref[a]
-        for piece in (low, middle, high):
-            so_far = so_far + lax.dot_general(cells, piece, contract, preferred_element_type=F32)
-        return so_far
-
-    g = lax.fori_loop(0, NA, outer, jnp.zeros((D, D), F32))
+    g = jnp.zeros((D, D), F32)
+    for step in range(3):
+        piece = prod[...].astype(jnp.bfloat16)
+        if step < 2:
+            prod[...] -= piece.astype(F32)
+        g += lax.dot_general(cells_ref[...], piece, (((0,), (0,)), ((), ())), preferred_element_type=F32)
     g_ref[...] = g * (-1.0 / math.sqrt(D))
 
 
@@ -488,7 +482,7 @@
     notes = (note, note1, note2, swap(note2, "core"))
     targets = (target_cells, t1, t2, swap(t2, "core"))
     cells = lax.all_to_all(jnp.broadcast_to(column_cells[None], (4, 4, TILE, D)), "x", 0, 0)
-    cells = cells.reshape(NA, TILE, D)
+    cells = cells.reshape(NA * TILE, D)
 
     rows_to = (VM, SHAPE((16, NA, TILE), F32))
     cols_to = (VM, SHAPE((16, NB, TILE), F32))
@@ -497,12 +491,9 @@
     tiles = (HERE, SHAPE((SLOTS, TILE, TILE), F32))
     row_blocks = pltpu.VMEM((NA, TILE, TILE), F32)
     col_rows = pltpu.VMEM((NB, 8, TILE), F32)
-    gathered = [
-        pltpu.VMEM((4, TB_DEV * TILE, D), jnp.bfloat16),
-        pltpu.VMEM((NA, TILE, D), jnp.bfloat16),
-    ]
-    gathered_sems = pltpu.SemaphoreType.DMA((6,))
-    gathered_refs = [(ANY, cells), (FAR, targets[0]), *[(ANY, value) for value in targets[1:]]]
+    gathered = pltpu.VMEM((4, TB_DEV * TILE, D), jnp.bfloat16)
+    gathered_sems = pltpu.SemaphoreType.DMA((5,))
+    gathered_refs = [(VM, cells), (FAR, targets[0]), *[(ANY, value) for value in targets[1:]]]
 
     (tile_list,) = call(
         plan_kernel,
@@ -520,7 +511,7 @@
         ],
         [(VM, SHAPE((16, NA + 8, TILE), F32)), tiles, tiles],
         [
-            *gathered, pltpu.VMEM((D, D), jnp.bfloat16), pltpu.VMEM((NA, TILE, D), jnp.bfloat16),
+            gathered, pltpu.VMEM((D, D), jnp.bfloat16), pltpu.VMEM((NA * TILE, D), jnp.bfloat16),
             row_blocks, row_blocks, gathered_sems,
         ],
     )
@@ -605,8 +596,8 @@
         ],
         [(VM, SHAPE((D, D), F32)), (VM, SHAPE((1, TILE), F32)), (VM, SHAPE((TB_DEV, TILE), F32))],
         [
-            *gathered, row_blocks, row_blocks, pltpu.VMEM((NB, TILE), F32), pltpu.VMEM((NB, TILE), F32),
-            pltpu.VMEM((NA, TILE, D), F32),
+            gathered, row_blocks, row_blocks, pltpu.VMEM((NB, TILE), F32), pltpu.VMEM((NB, TILE), F32),
+            pltpu.VMEM((NA * TILE, D), F32),
             pltpu.VMEM((CHUNK, TILE, TILE), jnp.bfloat16), pltpu.VMEM((CHUNK, TILE, D), F32), gathered_sems,
         ],
     )

time: 331 us -> 324 us (0.979)
  blocking collectives: 257 us -> 240 us
  Pallas kernels: 36.9 us -> 44.4 us
    all_to_all x10, blocking collectives: 132 us -> 116 us  [col_exchange(): return lax.all_to_all(value, COL, 0, 0)]
    pallas_call x18, Pallas kernels: 36.9 us -> 44.4 us  [call(): pl.pallas_call(kernel, out_shape=[shape for _, shape in outs], in_specs=i...]
where the time goes in v4:
time: 324 us; the launch traced here: 320 us
  blocking collectives  240 us (74%)
  Pallas kernels  44.4 us (14%)
  starting transfers between devices  20.8 us (6%)
  waiting for transfers between devices  8.67 us (3%)
  local copies, waits for them, and re-layouts  3.38 us (1%)
    all_to_all x9, blocking collectives, row_exchange(): return lax.all_to_all(value, ROW, 0, 0)  124 us
    all_to_all x10, blocking collectives, col_exchange(): return lax.all_to_all(value, COL, 0, 0)  116 us
    pallas_call x18, Pallas kernels, call(): pl.pallas_call(kernel, out_shape=[shape for _, shape in outs], in_specs=i...  44.4 us
    all_to_all x1, starting transfers between devices, shards(): lax.all_to_all(jnp.broadcast_to(source_cells[None], (4, TILE, D)), 'zh',...  9.01 us
    ppermute x6, starting transfers between devices, swap(): return lax.ppermute(value, axis, [(0, 1), (1, 0)])  7.75 us
  transfers between devices with their start and end apart: 8, of which 4 were waited for; matrix products, arithmetic and copies ran while one was open for 1% of the time, Pallas kernels for 1%

profile of v4, /device:TPU:1, one launch (start us, length us, event | category | flops | bytes accessed | tf_op | source)
XLA Modules:
  0.0 320.4 jit_solution(11356259353303256281)
XLA Ops:
  2.2 9.0 %all-to-all-start = ((bf16[4,128,256]{2,1,0:T(8,128)(2,1)}), bf16[4,128,256]{2,1,0:T(8,128)(2,1)S(1)}, u32[]{:S(2)}, u32[]{:S(2)}) async-start(bf16[4,128,256]{2,1,0:T(8,128)(2,1)} %broadcast_in_dim.13), calls=%async_computation | async-start | bytes 524288 | tf_op jit(solution)/shard_map/all_to_all | solution.py:473
  21.2 4.0 %all-to-all-start.1 = ((bf16[4,4,128,256]{3,2,1,0:T(8,128)(2,1)}), bf16[4,4,128,256]{3,2,1,0:T(8,128)(2,1)S(1)}, u32[]{:S(2)}, u32[]{:S(2)}) async-start(bf16[4,4,128,256]{3,2,1,0:T(8,128)(2,1)} %broadcast_in_dim.14), calls=%async_computation.1 | async-start | bytes 2097152 | tf_op jit(solution)/shard_map/all_to_all | solution.py:484
  28.7 5.2 %collective-permute-start.5 = (bf16[1024,256]{1,0:T(8,128)(2,1)S(1)}, bf16[1024,256]{1,0:T(8,128)(2,1)S(1)}, u32[]{:S(2)}, u32[]{:S(2)}) collective-permute-start(bf16[1024,256]{1,0:T(8,128)(2,1)S(1)} %collective-permute-done.4.t2), channel_id=1, source_target_pairs={{0,1},{1,0},{2,3},{3,2},{4,5},{5,4},{6,7},{7,6},{8,9},{9,8},{10,11... | collective-permute-start | bytes 1572872 | tf_op jit(solution)/shard_map/ppermute | solution.py:446
  38.9 7.9 %scores.1 = (f32[16,24,128]{2,1,0:T(8,128)S(1)}, f32[256,128,128]{2,1,0:T(8,128)S(1)}, f32[256,128,128]{2,1,0:T(8,128)S(1)}) custom-call(s32[264]{0:T(512)S(1)} %plan.1.list_ref, bf16[2048,256]{1,0:T(8,128)(2,1)S(1)} %bitcast.12, bf16[1024,256]{1,0:T(8,128)(2,1)} %t0.3, bf16[1024,256]{1,0:T(8,128)(2,1)S(1)} %collective-permute-done.2.t1, ...), custom_call_target="tpu_custom_call" | custom-call | flops 2097152 | bytes 1048576 | tf_op jit(solution)/shard_map/scores/pallas_call | solution.py:50
  46.8 19.5 %all_to_all.105.recv_ref = f32[16,24,128]{2,1,0:T(8,128)S(1)} all-to-all(f32[16,24,128]{2,1,0:T(8,128)S(1)} %get-tuple-element.39), channel_id=1, replica_groups=mesh['src'=4,'x'=4,'zh'=4,'zl'=2,'core'=2] {'x','zh'}, dimensions={0} | all-to-all | bytes 393216 | tf_op jit(solution)/shard_map/all_to_all | solution.py:450
  68.9 11.2 %all_to_all.106.recv_ref = f32[16,32,128]{2,1,0:T(8,128)S(1)} all-to-all(f32[16,32,128]{2,1,0:T(8,128)S(1)} %get-tuple-element.42), channel_id=1, replica_groups=mesh['src'=4,'x'=4,'zh'=4,'zl'=2,'core'=2] {'src','zl','core'}, dimensions={0} | all-to-all | bytes 524288 | tf_op jit(solution)/shard_map/all_to_all | solution.py:454
  82.4 13.0 %all_to_all.107.recv_ref = f32[16,16,128]{2,1,0:T(8,128)S(1)} all-to-all(f32[16,16,128]{2,1,0:T(8,128)S(1)} %get-tuple-element.44), channel_id=1, replica_groups=mesh['src'=4,'x'=4,'zh'=4,'zl'=2,'core'=2] {'x','zh'}, dimensions={0} | all-to-all | bytes 262144 | tf_op jit(solution)/shard_map/all_to_all | solution.py:450
  96.9 11.1 %all_to_all.108.recv_ref = f32[16,32,128]{2,1,0:T(8,128)S(1)} all-to-all(f32[16,32,128]{2,1,0:T(8,128)S(1)} %columns.3), channel_id=1, replica_groups=mesh['src'=4,'x'=4,'zh'=4,'zl'=2,'core'=2] {'src','zl','core'}, dimensions={0} | all-to-all | bytes 524288 | tf_op jit(solution)/shard_map/all_to_all | solution.py:454
  109.6 12.7 %all_to_all.109.recv_ref = f32[16,16,128]{2,1,0:T(8,128)S(1)} all-to-all(f32[16,16,128]{2,1,0:T(8,128)S(1)} %rows.2), channel_id=1, replica_groups=mesh['src'=4,'x'=4,'zh'=4,'zl'=2,'core'=2] {'x','zh'}, dimensions={0} | all-to-all | bytes 262144 | tf_op jit(solution)/shard_map/all_to_all | solution.py:450
  123.9 11.4 %all_to_all.110.recv_ref = f32[16,32,128]{2,1,0:T(8,128)S(1)} all-to-all(f32[16,32,128]{2,1,0:T(8,128)S(1)} %columns.4), channel_id=1, replica_groups=mesh['src'=4,'x'=4,'zh'=4,'zl'=2,'core'=2] {'src','zl','core'}, dimensions={0} | all-to-all | bytes 524288 | tf_op jit(solution)/shard_map/all_to_all | solution.py:454
  136.8 12.7 %all_to_all.111.recv_ref = f32[16,16,128]{2,1,0:T(8,128)S(1)} all-to-all(f32[16,16,128]{2,1,0:T(8,128)S(1)} %rows.3), channel_id=1, replica_groups=mesh['src'=4,'x'=4,'zh'=4,'zl'=2,'core'=2] {'x','zh'}, dimensions={0} | all-to-all | bytes 262144 | tf_op jit(solution)/shard_map/all_to_all | solution.py:450
  151.1 11.4 %all_to_all.112.recv_ref = f32[16,32,128]{2,1,0:T(8,128)S(1)} all-to-all(f32[16,32,128]{2,1,0:T(8,128)S(1)} %get-tuple-element.48), channel_id=1, replica_groups=mesh['src'=4,'x'=4,'zh'=4,'zl'=2,'core'=2] {'src','zl','core'}, dimensions={0} | all-to-all | bytes 524288 | tf_op jit(solution)/shard_map/all_to_all | solution.py:454
  164.9 13.9 %all_to_all.113.recv_ref = f32[16,32,128]{2,1,0:T(8,128)S(1)} all-to-all(f32[16,32,128]{2,1,0:T(8,128)S(1)} %get-tuple-element.49), channel_id=1, replica_groups=mesh['src'=4,'x'=4,'zh'=4,'zl'=2,'core'=2] {'x','zh'}, dimensions={0} | all-to-all | bytes 524288 | tf_op jit(solution)/shard_map/all_to_all | solution.py:450
  181.2 12.8 %all_to_all.114.recv_ref = f32[16,32,128]{2,1,0:T(8,128)S(1)} all-to-all(f32[16,32,128]{2,1,0:T(8,128)S(1)} %get-tuple-element.51), channel_id=1, replica_groups=mesh['src'=4,'x'=4,'zh'=4,'zl'=2,'core'=2] {'src','zl','core'}, dimensions={0} | all-to-all | bytes 524288 | tf_op jit(solution)/shard_map/all_to_all | solution.py:454
  195.7 12.6 %all_to_all.115.recv_ref = f32[16,16,128]{2,1,0:T(8,128)S(1)} all-to-all(f32[16,16,128]{2,1,0:T(8,128)S(1)} %pull.3), channel_id=1, replica_groups=mesh['src'=4,'x'=4,'zh'=4,'zl'=2,'core'=2] {'x','zh'}, dimensions={0} | all-to-all | bytes 262144 | tf_op jit(solution)/shard_map/all_to_all | solution.py:450
  209.8 11.6 %all_to_all.116.recv_ref = f32[16,32,128]{2,1,0:T(8,128)S(1)} all-to-all(f32[16,32,128]{2,1,0:T(8,128)S(1)} %push.3), channel_id=1, replica_groups=mesh['src'=4,'x'=4,'zh'=4,'zl'=2,'core'=2] {'src','zl','core'}, dimensions={0} | all-to-all | bytes 524288 | tf_op jit(solution)/shard_map/all_to_all | solution.py:454
  223.0 13.0 %all_to_all.117.recv_ref = f32[16,16,128]{2,1,0:T(8,128)S(1)} all-to-all(f32[16,16,128]{2,1,0:T(8,128)S(1)} %pull.4), channel_id=1, replica_groups=mesh['src'=4,'x'=4,'zh'=4,'zl'=2,'core'=2] {'x','zh'}, dimensions={0} | all-to-all | bytes 262144 | tf_op jit(solution)/shard_map/all_to_all | solution.py:450
  237.5 11.0 %all_to_all.118.recv_ref = f32[16,32,128]{2,1,0:T(8,128)S(1)} all-to-all(f32[16,32,128]{2,1,0:T(8,128)S(1)} %push.4), channel_id=1, replica_groups=mesh['src'=4,'x'=4,'zh'=4,'zl'=2,'core'=2] {'src','zl','core'}, dimensions={0} | all-to-all | bytes 524288 | tf_op jit(solution)/shard_map/all_to_all | solution.py:454
  250.2 12.7 %all_to_all.119.recv_ref = f32[16,16,128]{2,1,0:T(8,128)S(1)} all-to-all(f32[16,16,128]{2,1,0:T(8,128)S(1)} %pull.5), channel_id=1, replica_groups=mesh['src'=4,'x'=4,'zh'=4,'zl'=2,'core'=2] {'x','zh'}, dimensions={0} | all-to-all | bytes 262144 | tf_op jit(solution)/shard_map/all_to_all | solution.py:450
  264.4 11.4 %all_to_all.120.recv_ref = f32[16,32,128]{2,1,0:T(8,128)S(1)} all-to-all(f32[16,32,128]{2,1,0:T(8,128)S(1)} %get-tuple-element.57), channel_id=1, replica_groups=mesh['src'=4,'x'=4,'zh'=4,'zl'=2,'core'=2] {'src','zl','core'}, dimensions={0} | all-to-all | bytes 524288 | tf_op jit(solution)/shard_map/all_to_all | solution.py:454
  275.8 6.0 %gradient.1 = (f32[256,256]{1,0:T(8,128)S(1)}, f32[1,128]{1,0:T(1,128)}, f32[8,128]{1,0:T(8,128)}) custom-call(s32[264]{0:T(512)S(1)} %plan.1.list_ref, f32[16,32,128]{2,1,0:T(8,128)S(1)} %all_to_all.120.recv_ref, f32[32,128]{1,0:T(8,128)S(1)} %get-tuple-element.52.sum_ref, f32[32,128]{1,0:T(8,128)S(1)} %get-tuple-element.53.beta_ref, ...), custom_call_target="tpu_custom_call" | custom-call | flops 2097152 | bytes 1048576 | tf_op jit(solution)/shard_map/gradient/pallas_call | solution.py:50
  281.8 10.6 %all_to_all.121 = f32[16,16,256]{2,1,0:T(8,128)S(1)} all-to-all(f32[16,16,256]{2,1,0:T(8,128)S(1)} %bitcast.14), channel_id=1, replica_groups=mesh['src'=4,'x'=4,'zh'=4,'zl'=2,'core'=2] {'src','zl','core'}, dimensions={0} | all-to-all | bytes 524288 | tf_op jit(solution)/shard_map/all_to_all | solution.py:454
  292.5 13.9 %all_to_all.122 = f32[16,16,256]{2,1,0:T(8,128)S(1)} all-to-all(f32[16,16,256]{2,1,0:T(8,128)S(1)} %broadcast_in_dim.15), channel_id=1, replica_groups=mesh['src'=4,'x'=4,'zh'=4,'zl'=2,'core'=2] {'x','zh'}, dimensions={0} | all-to-all | bytes 524288 | tf_op jit(solution)/shard_map/all_to_all | solution.py:450
  306.5 13.3 %all_to_all.123 = f32[16,16,256]{2,1,0:T(8,128)S(1)} all-to-all(f32[16,16,256]{2,1,0:T(8,128)S(1)} %broadcast_in_dim.16), channel_id=1, replica_groups=mesh['src'=4,'x'=4,'zh'=4,'zl'=2,'core'=2] {'src','zl','core'}, dimensions={0} | all-to-all | bytes 524288 | tf_op jit(solution)/shard_map/all_to_all | solution.py:454
  (41 shorter events, 47.9 us)
Async XLA Ops:
  2.2 17.2 %all-to-all-start = ((bf16[4,128,256]{2,1,0:T(8,128)(2,1)}), bf16[4,128,256]{2,1,0:T(8,128)(2,1)S(1)}, u32[]{:S(2)}, u32[]{:S(2)}) async-start(bf16[4,128,256]{2,1,0:T(8,128)(2,1)} %broadcast_in_dim.13), calls=%async_computation | async-start | bytes 524288 | tf_op jit(solution)/shard_map/all_to_all | solution.py:473
  11.2 8.2 %collective-permute-start.2 = (bf16[1024,256]{1,0:T(8,128)(2,1)}, bf16[1024,256]{1,0:T(8,128)(2,1)S(1)}, u32[]{:S(2)}, u32[]{:S(2)}) collective-permute-start(bf16[1024,256]{1,0:T(8,128)(2,1)} %t0.3), channel_id=1, source_target_pairs={{0,1},{1,0},{2,3},{3,2},{4,5},{5,4},{6,7},{7,6},{8,9},{9,8},{10,11... | collective-permute-start | bytes 1572872 | tf_op jit(solution)/shard_map/ppermute | solution.py:446
  14.2 1.5 collective-permute-start.1
  14.3 2.7 collective-permute-start
  19.4 9.3 %collective-permute-start.4 = (bf16[1024,256]{1,0:T(8,128)(2,1)}, bf16[1024,256]{1,0:T(8,128)(2,1)S(1)}, u32[]{:S(2)}, u32[]{:S(2)}) collective-permute-start(bf16[1024,256]{1,0:T(8,128)(2,1)} %t0.3), channel_id=1, source_target_pairs={{0,2},{2,0},{1,3},{3,1},{4,6},{6,4},{5,7},{7,5},{8,10},{10,8},{9,1... | collective-permute-start | bytes 1572872 | tf_op jit(solution)/shard_map/ppermute | solution.py:446
  21.2 17.7 %all-to-all-start.1 = ((bf16[4,4,128,256]{3,2,1,0:T(8,128)(2,1)}), bf16[4,4,128,256]{3,2,1,0:T(8,128)(2,1)S(1)}, u32[]{:S(2)}, u32[]{:S(2)}) async-start(bf16[4,4,128,256]{3,2,1,0:T(8,128)(2,1)} %broadcast_in_dim.14), calls=%async_computation.1 | async-start | bytes 2097152 | tf_op jit(solution)/shard_map/all_to_all | solution.py:484
  28.7 10.2 %collective-permute-start.5 = (bf16[1024,256]{1,0:T(8,128)(2,1)S(1)}, bf16[1024,256]{1,0:T(8,128)(2,1)S(1)}, u32[]{:S(2)}, u32[]{:S(2)}) collective-permute-start(bf16[1024,256]{1,0:T(8,128)(2,1)S(1)} %collective-permute-done.4.t2), channel_id=1, source_target_pairs={{0,1},{1,0},{2,3},{3,2},{4,5},{5,4},{6,7},{7,6},{8,9},{9,8},{10,11... | collective-permute-start | bytes 1572872 | tf_op jit(solution)/shard_map/ppermute | solution.py:446
  33.9 1.5 collective-permute-start.3

commit v5 on v4

--- a/solution.py
+++ b/solution.py
@@ -35,18 +35,25 @@
 
 
 HERE = "here"
+KEPT = "kept"
 FAR = "far"
+
+
+SPACES = {HERE: pltpu.VMEM, KEPT: pltpu.SMEM, FAR: pltpu.HBM}
 
 
 def call(kernel, name, ins, outs, scratch, flops=2 << 20, moved=1 << 20, vmem=10, aliases={}):
     in_specs, args = [], []
     for spec, value in ins:
-        if spec in (HERE, FAR):
-            space = pltpu.VMEM if spec == HERE else pltpu.HBM
+        if isinstance(spec, str):
+            space = SPACES[spec]
             spec, value = pl.BlockSpec(memory_space=space), pltpu.with_memory_space_constraint(value, space)
         in_specs.append(spec)
         args.append(value)
-    outs = [(VM, pltpu.VMEM(shape.shape, shape.dtype)) if spec == HERE else (spec, shape) for spec, shape in outs]
+    outs = [
+        (pl.BlockSpec(memory_space=SPACES[spec]), SPACES[spec](shape.shape, shape.dtype)) if isinstance(spec, str) else (spec, shape)
+        for spec, shape in outs
+    ]
     return pl.pallas_call(
         kernel,
         out_shape=[shape for _, shape in outs],
@@ -469,17 +476,19 @@
     note = jnp.concatenate(
         [jnp.pad(head, ((0, 7), (0, TILE - TILES - 4))), target_logmass.astype(F32).reshape(TB_DEV, TILE)]
     )
+    note2 = swap(note, "zl")
     first = (
         lax.all_to_all(jnp.broadcast_to(source_cells[None], (4, TILE, D)), "zh", 0, 0),
-        swap(note, "zl"),
+        note2,
+        swap(note2, "core"),
         swap(note, "core"),
         swap(target_cells, "core"),
         source_logmass.astype(F32).reshape(1, TILE),
         target_cells,
     )
-    column_cells, note2, note1, t1, own_mass, t0 = lax.optimization_barrier(first)
+    column_cells, note2, note3, note1, t1, own_mass, t0 = lax.optimization_barrier(first)
     t2 = swap(t0, "zl")
-    notes = (note, note1, note2, swap(note2, "core"))
+    notes = (note, note1, note2, note3)
     targets = (target_cells, t1, t2, swap(t2, "core"))
     cells = lax.all_to_all(jnp.broadcast_to(column_cells[None], (4, 4, TILE, D)), "x", 0, 0)
     cells = cells.reshape(NA * TILE, D)
@@ -499,14 +508,15 @@
         plan_kernel,
         "plan",
         [(SM, note) for note in notes],
-        [(SM, SHAPE((SLOTS + 8,), jnp.int32))],
+        [(KEPT, SHAPE((SLOTS + 8,), jnp.int32))],
         [],
+        moved=10 << 20,
     )
     send, x, k = call(
         scores_kernel,
         "scores",
         [
-            (SM, tile_list), *gathered_refs,
+            (KEPT, tile_list), *gathered_refs,
             (FAR, mapping), (VM, own_mass),
         ],
         [(VM, SHAPE((16, NA + 8, TILE), F32)), tiles, tiles],
@@ -515,7 +525,7 @@
             row_blocks, row_blocks, gathered_sems,
         ],
     )
-    tile_list, x = (SM, tile_list), (HERE, x)
+    tile_list, x = (KEPT, tile_list), (HERE, x)
     recv = row_exchange(send)
     send, u, source_mass = call(
         first_targets_kernel,

time: 324 us -> 316 us (0.975)
  Pallas kernels: 44.4 us -> 33.9 us
  blocking collectives: 240 us -> 245 us
    pallas_call x18, Pallas kernels: 44.4 us -> 33.9 us  [call(): pl.pallas_call(kernel, out_shape=[shape for _, shape in outs], in_specs=i...]
    all_to_all x10, blocking collectives: 116 us -> 119 us  [col_exchange(): return lax.all_to_all(value, COL, 0, 0)]
where the time goes in v5:
time: 316 us; the launch traced here: 314 us
  blocking collectives  245 us (78%)
  Pallas kernels  33.9 us (11%)
  starting transfers between devices  22 us (7%)
  waiting for transfers between devices  5.88 us (2%)
  local copies, waits for them, and re-layouts  3.38 us (1%)
    all_to_all x9, blocking collectives, row_exchange(): return lax.all_to_all(value, ROW, 0, 0)  126 us
    all_to_all x10, blocking collectives, col_exchange(): return lax.all_to_all(value, COL, 0, 0)  119 us
    pallas_call x18, Pallas kernels, call(): pl.pallas_call(kernel, out_shape=[shape for _, shape in outs], in_specs=i...  33.9 us
    all_to_all x1, starting transfers between devices, shards(): lax.all_to_all(jnp.broadcast_to(source_cells[None], (4, TILE, D)), 'zh',...  9.01 us
    ppermute x6, starting transfers between devices, swap(): return lax.ppermute(value, axis, [(0, 1), (1, 0)])  9 us
  transfers between devices with their start and end apart: 8, of which 4 were waited for; matrix products, arithmetic and copies ran while one was open for 1% of the time, Pallas kernels for 1%

profile of v5, /device:TPU:1, one launch (start us, length us, event | category | flops | bytes accessed | tf_op | source)
XLA Modules:
  0.0 314.0 jit_solution(15263448580335874043)
XLA Ops:
  2.2 9.0 %all-to-all-start = ((bf16[4,128,256]{2,1,0:T(8,128)(2,1)}), bf16[4,128,256]{2,1,0:T(8,128)(2,1)S(1)}, u32[]{:S(2)}, u32[]{:S(2)}) async-start(bf16[4,128,256]{2,1,0:T(8,128)(2,1)} %broadcast_in_dim.13), calls=%async_computation | async-start | bytes 524288 | tf_op jit(solution)/shard_map/all_to_all | solution.py:481
  21.2 4.0 %all-to-all-start.1 = ((bf16[4,4,128,256]{3,2,1,0:T(8,128)(2,1)}), bf16[4,4,128,256]{3,2,1,0:T(8,128)(2,1)S(1)}, u32[]{:S(2)}, u32[]{:S(2)}) async-start(bf16[4,4,128,256]{3,2,1,0:T(8,128)(2,1)} %broadcast_in_dim.14), calls=%async_computation.1 | async-start | bytes 2097152 | tf_op jit(solution)/shard_map/all_to_all | solution.py:493
  28.7 5.2 %collective-permute-start.5 = (bf16[1024,256]{1,0:T(8,128)(2,1)S(1)}, bf16[1024,256]{1,0:T(8,128)(2,1)S(1)}, u32[]{:S(2)}, u32[]{:S(2)}) collective-permute-start(bf16[1024,256]{1,0:T(8,128)(2,1)S(1)} %collective-permute-done.4.t2), channel_id=1, source_target_pairs={{0,1},{1,0},{2,3},{3,2},{4,5},{5,4},{6,7},{7,6},{8,9},{9,8},{10,11... | collective-permute-start | bytes 1572872 | tf_op jit(solution)/shard_map/ppermute | solution.py:453
  36.7 7.3 %scores.1 = (f32[16,24,128]{2,1,0:T(8,128)S(1)}, f32[256,128,128]{2,1,0:T(8,128)S(1)}, f32[256,128,128]{2,1,0:T(8,128)S(1)}) custom-call(s32[264]{0:T(512)S(4)} %plan.1.list_ref, bf16[2048,256]{1,0:T(8,128)(2,1)S(1)} %bitcast.12, bf16[1024,256]{1,0:T(8,128)(2,1)} %t0.3, bf16[1024,256]{1,0:T(8,128)(2,1)S(1)} %collective-permute-done.3.t1, ...), custom_call_target="tpu_custom_call" | custom-call | flops 2097152 | bytes 1048576 | tf_op jit(solution)/shard_map/scores/pallas_call | solution.py:57
  44.0 20.7 %all_to_all.105.recv_ref = f32[16,24,128]{2,1,0:T(8,128)S(1)} all-to-all(f32[16,24,128]{2,1,0:T(8,128)S(1)} %get-tuple-element.41), channel_id=1, replica_groups=mesh['src'=4,'x'=4,'zh'=4,'zl'=2,'core'=2] {'x','zh'}, dimensions={0} | all-to-all | bytes 393216 | tf_op jit(solution)/shard_map/all_to_all | solution.py:457
  66.6 14.9 %all_to_all.106.recv_ref = f32[16,32,128]{2,1,0:T(8,128)S(1)} all-to-all(f32[16,32,128]{2,1,0:T(8,128)S(1)} %get-tuple-element.44), channel_id=1, replica_groups=mesh['src'=4,'x'=4,'zh'=4,'zl'=2,'core'=2] {'src','zl','core'}, dimensions={0} | all-to-all | bytes 524288 | tf_op jit(solution)/shard_map/all_to_all | solution.py:461
  83.2 12.9 %all_to_all.107.recv_ref = f32[16,16,128]{2,1,0:T(8,128)S(1)} all-to-all(f32[16,16,128]{2,1,0:T(8,128)S(1)} %get-tuple-element.46), channel_id=1, replica_groups=mesh['src'=4,'x'=4,'zh'=4,'zl'=2,'core'=2] {'x','zh'}, dimensions={0} | all-to-all | bytes 262144 | tf_op jit(solution)/shard_map/all_to_all | solution.py:457
  97.1 11.2 %all_to_all.108.recv_ref = f32[16,32,128]{2,1,0:T(8,128)S(1)} all-to-all(f32[16,32,128]{2,1,0:T(8,128)S(1)} %columns.3), channel_id=1, replica_groups=mesh['src'=4,'x'=4,'zh'=4,'zl'=2,'core'=2] {'src','zl','core'}, dimensions={0} | all-to-all | bytes 524288 | tf_op jit(solution)/shard_map/all_to_all | solution.py:461
  109.4 12.9 %all_to_all.109.recv_ref = f32[16,16,128]{2,1,0:T(8,128)S(1)} all-to-all(f32[16,16,128]{2,1,0:T(8,128)S(1)} %rows.2), channel_id=1, replica_groups=mesh['src'=4,'x'=4,'zh'=4,'zl'=2,'core'=2] {'x','zh'}, dimensions={0} | all-to-all | bytes 262144 | tf_op jit(solution)/shard_map/all_to_all | solution.py:457
  123.3 11.3 %all_to_all.110.recv_ref = f32[16,32,128]{2,1,0:T(8,128)S(1)} all-to-all(f32[16,32,128]{2,1,0:T(8,128)S(1)} %columns.4), channel_id=1, replica_groups=mesh['src'=4,'x'=4,'zh'=4,'zl'=2,'core'=2] {'src','zl','core'}, dimensions={0} | all-to-all | bytes 524288 | tf_op jit(solution)/shard_map/all_to_all | solution.py:461
  135.6 12.9 %all_to_all.111.recv_ref = f32[16,16,128]{2,1,0:T(8,128)S(1)} all-to-all(f32[16,16,128]{2,1,0:T(8,128)S(1)} %rows.3), channel_id=1, replica_groups=mesh['src'=4,'x'=4,'zh'=4,'zl'=2,'core'=2] {'x','zh'}, dimensions={0} | all-to-all | bytes 262144 | tf_op jit(solution)/shard_map/all_to_all | solution.py:457
  149.5 11.3 %all_to_all.112.recv_ref = f32[16,32,128]{2,1,0:T(8,128)S(1)} all-to-all(f32[16,32,128]{2,1,0:T(8,128)S(1)} %get-tuple-element.50), channel_id=1, replica_groups=mesh['src'=4,'x'=4,'zh'=4,'zl'=2,'core'=2] {'src','zl','core'}, dimensions={0} | all-to-all | bytes 524288 | tf_op jit(solution)/shard_map/all_to_all | solution.py:461
  162.6 14.0 %all_to_all.113.recv_ref = f32[16,32,128]{2,1,0:T(8,128)S(1)} all-to-all(f32[16,32,128]{2,1,0:T(8,128)S(1)} %get-tuple-element.51), channel_id=1, replica_groups=mesh['src'=4,'x'=4,'zh'=4,'zl'=2,'core'=2] {'x','zh'}, dimensions={0} | all-to-all | bytes 524288 | tf_op jit(solution)/shard_map/all_to_all | solution.py:457
  178.6 12.8 %all_to_all.114.recv_ref = f32[16,32,128]{2,1,0:T(8,128)S(1)} all-to-all(f32[16,32,128]{2,1,0:T(8,128)S(1)} %get-tuple-element.53), channel_id=1, replica_groups=mesh['src'=4,'x'=4,'zh'=4,'zl'=2,'core'=2] {'src','zl','core'}, dimensions={0} | all-to-all | bytes 524288 | tf_op jit(solution)/shard_map/all_to_all | solution.py:461
  192.4 12.7 %all_to_all.115.recv_ref = f32[16,16,128]{2,1,0:T(8,128)S(1)} all-to-all(f32[16,16,128]{2,1,0:T(8,128)S(1)} %pull.3), channel_id=1, replica_groups=mesh['src'=4,'x'=4,'zh'=4,'zl'=2,'core'=2] {'x','zh'}, dimensions={0} | all-to-all | bytes 262144 | tf_op jit(solution)/shard_map/all_to_all | solution.py:457
  206.1 11.5 %all_to_all.116.recv_ref = f32[16,32,128]{2,1,0:T(8,128)S(1)} all-to-all(f32[16,32,128]{2,1,0:T(8,128)S(1)} %push.3), channel_id=1, replica_groups=mesh['src'=4,'x'=4,'zh'=4,'zl'=2,'core'=2] {'src','zl','core'}, dimensions={0} | all-to-all | bytes 524288 | tf_op jit(solution)/shard_map/all_to_all | solution.py:461
  218.7 13.0 %all_to_all.117.recv_ref = f32[16,16,128]{2,1,0:T(8,128)S(1)} all-to-all(f32[16,16,128]{2,1,0:T(8,128)S(1)} %pull.4), channel_id=1, replica_groups=mesh['src'=4,'x'=4,'zh'=4,'zl'=2,'core'=2] {'x','zh'}, dimensions={0} | all-to-all | bytes 262144 | tf_op jit(solution)/shard_map/all_to_all | solution.py:457
  232.7 11.2 %all_to_all.118.recv_ref = f32[16,32,128]{2,1,0:T(8,128)S(1)} all-to-all(f32[16,32,128]{2,1,0:T(8,128)S(1)} %push.4), channel_id=1, replica_groups=mesh['src'=4,'x'=4,'zh'=4,'zl'=2,'core'=2] {'src','zl','core'}, dimensions={0} | all-to-all | bytes 524288 | tf_op jit(solution)/shard_map/all_to_all | solution.py:461
  244.9 12.9 %all_to_all.119.recv_ref = f32[16,16,128]{2,1,0:T(8,128)S(1)} all-to-all(f32[16,16,128]{2,1,0:T(8,128)S(1)} %pull.5), channel_id=1, replica_groups=mesh['src'=4,'x'=4,'zh'=4,'zl'=2,'core'=2] {'x','zh'}, dimensions={0} | all-to-all | bytes 262144 | tf_op jit(solution)/shard_map/all_to_all | solution.py:457
  258.8 11.2 %all_to_all.120.recv_ref = f32[16,32,128]{2,1,0:T(8,128)S(1)} all-to-all(f32[16,32,128]{2,1,0:T(8,128)S(1)} %get-tuple-element.59), channel_id=1, replica_groups=mesh['src'=4,'x'=4,'zh'=4,'zl'=2,'core'=2] {'src','zl','core'}, dimensions={0} | all-to-all | bytes 524288 | tf_op jit(solution)/shard_map/all_to_all | solution.py:461
  270.0 5.4 %gradient.1 = (f32[256,256]{1,0:T(8,128)S(1)}, f32[1,128]{1,0:T(1,128)}, f32[8,128]{1,0:T(8,128)}) custom-call(s32[264]{0:T(512)S(4)} %plan.1.list_ref, f32[16,32,128]{2,1,0:T(8,128)S(1)} %all_to_all.120.recv_ref, f32[32,128]{1,0:T(8,128)S(1)} %get-tuple-element.54.sum_ref, f32[32,128]{1,0:T(8,128)S(1)} %get-tuple-element.55.beta_ref, ...), custom_call_target="tpu_custom_call" | custom-call | flops 2097152 | bytes 1048576 | tf_op jit(solution)/shard_map/gradient/pallas_call | solution.py:57
  275.4 10.6 %all_to_all.121 = f32[16,16,256]{2,1,0:T(8,128)S(1)} all-to-all(f32[16,16,256]{2,1,0:T(8,128)S(1)} %bitcast.14), channel_id=1, replica_groups=mesh['src'=4,'x'=4,'zh'=4,'zl'=2,'core'=2] {'src','zl','core'}, dimensions={0} | all-to-all | bytes 524288 | tf_op jit(solution)/shard_map/all_to_all | solution.py:461
  286.1 13.9 %all_to_all.122 = f32[16,16,256]{2,1,0:T(8,128)S(1)} all-to-all(f32[16,16,256]{2,1,0:T(8,128)S(1)} %broadcast_in_dim.15), channel_id=1, replica_groups=mesh['src'=4,'x'=4,'zh'=4,'zl'=2,'core'=2] {'x','zh'}, dimensions={0} | all-to-all | bytes 524288 | tf_op jit(solution)/shard_map/all_to_all | solution.py:457
  300.0 13.2 %all_to_all.123 = f32[16,16,256]{2,1,0:T(8,128)S(1)} all-to-all(f32[16,16,256]{2,1,0:T(8,128)S(1)} %broadcast_in_dim.16), channel_id=1, replica_groups=mesh['src'=4,'x'=4,'zh'=4,'zl'=2,'core'=2] {'src','zl','core'}, dimensions={0} | all-to-all | bytes 524288 | tf_op jit(solution)/shard_map/all_to_all | solution.py:461
  (41 shorter events, 37.0 us)
Async XLA Ops:
  2.2 17.2 %all-to-all-start = ((bf16[4,128,256]{2,1,0:T(8,128)(2,1)}), bf16[4,128,256]{2,1,0:T(8,128)(2,1)S(1)}, u32[]{:S(2)}, u32[]{:S(2)}) async-start(bf16[4,128,256]{2,1,0:T(8,128)(2,1)} %broadcast_in_dim.13), calls=%async_computation | async-start | bytes 524288 | tf_op jit(solution)/shard_map/all_to_all | solution.py:481
  11.2 8.2 %collective-permute-start.3 = (bf16[1024,256]{1,0:T(8,128)(2,1)}, bf16[1024,256]{1,0:T(8,128)(2,1)S(1)}, u32[]{:S(2)}, u32[]{:S(2)}) collective-permute-start(bf16[1024,256]{1,0:T(8,128)(2,1)} %t0.3), channel_id=1, source_target_pairs={{0,1},{1,0},{2,3},{3,2},{4,5},{5,4},{6,7},{7,6},{8,9},{9,8},{10,11... | collective-permute-start | bytes 1572872 | tf_op jit(solution)/shard_map/ppermute | solution.py:453
  14.2 2.8 collective-permute-start
  15.0 3.7 %collective-permute-start.2 = (f32[16,128]{1,0:T(8,128)S(1)}, f32[16,128]{1,0:T(8,128)S(1)}, u32[]{:S(2)}, u32[]{:S(2)}) collective-permute-start(f32[16,128]{1,0:T(8,128)S(1)} %select_maximum_fusion.notes0), channel_id=1, source_target_pairs={{0,1},{1,0},{2,3},{3,2},{4,5},{5,4},{6,7},{7,6},{8,9},{9,8},{10,11... | collective-permute-start | bytes 24584 | tf_op jit(solution)/shard_map/ppermute | solution.py:453
  17.0 1.9 collective-permute-start.1
  19.4 9.3 %collective-permute-start.4 = (bf16[1024,256]{1,0:T(8,128)(2,1)}, bf16[1024,256]{1,0:T(8,128)(2,1)S(1)}, u32[]{:S(2)}, u32[]{:S(2)}) collective-permute-start(bf16[1024,256]{1,0:T(8,128)(2,1)} %t0.3), channel_id=1, source_target_pairs={{0,2},{2,0},{1,3},{3,1},{4,6},{6,4},{5,7},{7,5},{8,10},{10,8},{9,1... | collective-permute-start | bytes 1572872 | tf_op jit(solution)/shard_map/ppermute | solution.py:453
  21.2 15.5 %all-to-all-start.1 = ((bf16[4,4,128,256]{3,2,1,0:T(8,128)(2,1)}), bf16[4,4,128,256]{3,2,1,0:T(8,128)(2,1)S(1)}, u32[]{:S(2)}, u32[]{:S(2)}) async-start(bf16[4,4,128,256]{3,2,1,0:T(8,128)(2,1)} %broadcast_in_dim.14), calls=%async_computation.1 | async-start | bytes 2097152 | tf_op jit(solution)/shard_map/all_to_all | solution.py:493
  28.7 8.0 %collective-permute-start.5 = (bf16[1024,256]{1,0:T(8,128)(2,1)S(1)}, bf16[1024,256]{1,0:T(8,128)(2,1)S(1)}, u32[]{:S(2)}, u32[]{:S(2)}) collective-permute-start(bf16[1024,256]{1,0:T(8,128)(2,1)S(1)} %collective-permute-done.4.t2), channel_id=1, source_target_pairs={{0,1},{1,0},{2,3},{3,2},{4,5},{5,4},{6,7},{7,6},{8,9},{9,8},{10,11... | collective-permute-start | bytes 1572872 | tf_op jit(solution)/shard_map/ppermute | solution.py:453

commit v6 on v5

--- a/solution.py
+++ b/solution.py
@@ -441,9 +441,9 @@
 
     each_chunk(list_ref, (weigh, multiply, add))
     g = jnp.zeros((D, D), F32)
-    for step in range(3):
+    for step in range(2):
         piece = prod[...].astype(jnp.bfloat16)
-        if step < 2:
+        if step < 1:
             prod[...] -= piece.astype(F32)
         g += lax.dot_general(cells_ref[...], piece, (((0,), (0,)), ((), ())), preferred_element_type=F32)
     g_ref[...] = g * (-1.0 / math.sqrt(D))

time: 316 us -> 315 us (level)
  no operation moved by 1% of the time
where the time goes in v6:
time: 315 us; the launch traced here: 312 us
  blocking collectives  246 us (78%)
  Pallas kernels  31.3 us (10%)
  starting transfers between devices  22 us (7%)
  waiting for transfers between devices  5.88 us (2%)
  local copies, waits for them, and re-layouts  3.38 us (1%)
    all_to_all x9, blocking collectives, row_exchange(): return lax.all_to_all(value, ROW, 0, 0)  126 us
    all_to_all x10, blocking collectives, col_exchange(): return lax.all_to_all(value, COL, 0, 0)  120 us
    pallas_call x18, Pallas kernels, call(): pl.pallas_call(kernel, out_shape=[shape for _, shape in outs], in_specs=i...  31.3 us
    all_to_all x1, starting transfers between devices, shards(): lax.all_to_all(jnp.broadcast_to(source_cells[None], (4, TILE, D)), 'zh',...  9.01 us
    ppermute x6, starting transfers between devices, swap(): return lax.ppermute(value, axis, [(0, 1), (1, 0)])  9 us
  transfers between devices with their start and end apart: 8, of which 4 were waited for; matrix products, arithmetic and copies ran while one was open for 1% of the time, Pallas kernels for 1%

profile of v6, /device:TPU:1, one launch (start us, length us, event | category | flops | bytes accessed | tf_op | source)
XLA Modules:
  0.0 312.5 jit_solution(16340623448498058527)
XLA Ops:
  2.2 9.0 %all-to-all-start = ((bf16[4,128,256]{2,1,0:T(8,128)(2,1)}), bf16[4,128,256]{2,1,0:T(8,128)(2,1)S(1)}, u32[]{:S(2)}, u32[]{:S(2)}) async-start(bf16[4,128,256]{2,1,0:T(8,128)(2,1)} %broadcast_in_dim.13), calls=%async_computation | async-start | bytes 524288 | tf_op jit(solution)/shard_map/all_to_all | solution.py:481
  21.2 4.0 %all-to-all-start.1 = ((bf16[4,4,128,256]{3,2,1,0:T(8,128)(2,1)}), bf16[4,4,128,256]{3,2,1,0:T(8,128)(2,1)S(1)}, u32[]{:S(2)}, u32[]{:S(2)}) async-start(bf16[4,4,128,256]{3,2,1,0:T(8,128)(2,1)} %broadcast_in_dim.14), calls=%async_computation.1 | async-start | bytes 2097152 | tf_op jit(solution)/shard_map/all_to_all | solution.py:493
  28.7 5.2 %collective-permute-start.5 = (bf16[1024,256]{1,0:T(8,128)(2,1)S(1)}, bf16[1024,256]{1,0:T(8,128)(2,1)S(1)}, u32[]{:S(2)}, u32[]{:S(2)}) collective-permute-start(bf16[1024,256]{1,0:T(8,128)(2,1)S(1)} %collective-permute-done.4.t2), channel_id=1, source_target_pairs={{0,1},{1,0},{2,3},{3,2},{4,5},{5,4},{6,7},{7,6},{8,9},{9,8},{10,11... | collective-permute-start | bytes 1572872 | tf_op jit(solution)/shard_map/ppermute | solution.py:453
  36.7 6.9 %scores.1 = (f32[16,24,128]{2,1,0:T(8,128)S(1)}, f32[256,128,128]{2,1,0:T(8,128)S(1)}, f32[256,128,128]{2,1,0:T(8,128)S(1)}) custom-call(s32[264]{0:T(512)S(4)} %plan.1.list_ref, bf16[2048,256]{1,0:T(8,128)(2,1)S(1)} %bitcast.12, bf16[1024,256]{1,0:T(8,128)(2,1)} %t0.3, bf16[1024,256]{1,0:T(8,128)(2,1)S(1)} %collective-permute-done.3.t1, ...), custom_call_target="tpu_custom_call" | custom-call | flops 2097152 | bytes 1048576 | tf_op jit(solution)/shard_map/scores/pallas_call | solution.py:57
  43.5 20.7 %all_to_all.105.recv_ref = f32[16,24,128]{2,1,0:T(8,128)S(1)} all-to-all(f32[16,24,128]{2,1,0:T(8,128)S(1)} %get-tuple-element.41), channel_id=1, replica_groups=mesh['src'=4,'x'=4,'zh'=4,'zl'=2,'core'=2] {'x','zh'}, dimensions={0} | all-to-all | bytes 393216 | tf_op jit(solution)/shard_map/all_to_all | solution.py:457
  66.0 15.4 %all_to_all.106.recv_ref = f32[16,32,128]{2,1,0:T(8,128)S(1)} all-to-all(f32[16,32,128]{2,1,0:T(8,128)S(1)} %get-tuple-element.44), channel_id=1, replica_groups=mesh['src'=4,'x'=4,'zh'=4,'zl'=2,'core'=2] {'src','zl','core'}, dimensions={0} | all-to-all | bytes 524288 | tf_op jit(solution)/shard_map/all_to_all | solution.py:461
  83.0 13.0 %all_to_all.107.recv_ref = f32[16,16,128]{2,1,0:T(8,128)S(1)} all-to-all(f32[16,16,128]{2,1,0:T(8,128)S(1)} %get-tuple-element.46), channel_id=1, replica_groups=mesh['src'=4,'x'=4,'zh'=4,'zl'=2,'core'=2] {'x','zh'}, dimensions={0} | all-to-all | bytes 262144 | tf_op jit(solution)/shard_map/all_to_all | solution.py:457
  96.9 11.3 %all_to_all.108.recv_ref = f32[16,32,128]{2,1,0:T(8,128)S(1)} all-to-all(f32[16,32,128]{2,1,0:T(8,128)S(1)} %columns.3), channel_id=1, replica_groups=mesh['src'=4,'x'=4,'zh'=4,'zl'=2,'core'=2] {'src','zl','core'}, dimensions={0} | all-to-all | bytes 524288 | tf_op jit(solution)/shard_map/all_to_all | solution.py:461
  109.2 12.9 %all_to_all.109.recv_ref = f32[16,16,128]{2,1,0:T(8,128)S(1)} all-to-all(f32[16,16,128]{2,1,0:T(8,128)S(1)} %rows.2), channel_id=1, replica_groups=mesh['src'=4,'x'=4,'zh'=4,'zl'=2,'core'=2] {'x','zh'}, dimensions={0} | all-to-all | bytes 262144 | tf_op jit(solution)/shard_map/all_to_all | solution.py:457
  123.0 11.3 %all_to_all.110.recv_ref = f32[16,32,128]{2,1,0:T(8,128)S(1)} all-to-all(f32[16,32,128]{2,1,0:T(8,128)S(1)} %columns.4), channel_id=1, replica_groups=mesh['src'=4,'x'=4,'zh'=4,'zl'=2,'core'=2] {'src','zl','core'}, dimensions={0} | all-to-all | bytes 524288 | tf_op jit(solution)/shard_map/all_to_all | solution.py:461
  135.3 12.9 %all_to_all.111.recv_ref = f32[16,16,128]{2,1,0:T(8,128)S(1)} all-to-all(f32[16,16,128]{2,1,0:T(8,128)S(1)} %rows.3), channel_id=1, replica_groups=mesh['src'=4,'x'=4,'zh'=4,'zl'=2,'core'=2] {'x','zh'}, dimensions={0} | all-to-all | bytes 262144 | tf_op jit(solution)/shard_map/all_to_all | solution.py:457
  149.1 11.6 %all_to_all.112.recv_ref = f32[16,32,128]{2,1,0:T(8,128)S(1)} all-to-all(f32[16,32,128]{2,1,0:T(8,128)S(1)} %get-tuple-element.50), channel_id=1, replica_groups=mesh['src'=4,'x'=4,'zh'=4,'zl'=2,'core'=2] {'src','zl','core'}, dimensions={0} | all-to-all | bytes 524288 | tf_op jit(solution)/shard_map/all_to_all | solution.py:461
  162.3 13.9 %all_to_all.113.recv_ref = f32[16,32,128]{2,1,0:T(8,128)S(1)} all-to-all(f32[16,32,128]{2,1,0:T(8,128)S(1)} %get-tuple-element.51), channel_id=1, replica_groups=mesh['src'=4,'x'=4,'zh'=4,'zl'=2,'core'=2] {'x','zh'}, dimensions={0} | all-to-all | bytes 524288 | tf_op jit(solution)/shard_map/all_to_all | solution.py:457
  178.0 13.0 %all_to_all.114.recv_ref = f32[16,32,128]{2,1,0:T(8,128)S(1)} all-to-all(f32[16,32,128]{2,1,0:T(8,128)S(1)} %get-tuple-element.53), channel_id=1, replica_groups=mesh['src'=4,'x'=4,'zh'=4,'zl'=2,'core'=2] {'src','zl','core'}, dimensions={0} | all-to-all | bytes 524288 | tf_op jit(solution)/shard_map/all_to_all | solution.py:461
  191.9 13.0 %all_to_all.115.recv_ref = f32[16,16,128]{2,1,0:T(8,128)S(1)} all-to-all(f32[16,16,128]{2,1,0:T(8,128)S(1)} %pull.3), channel_id=1, replica_groups=mesh['src'=4,'x'=4,'zh'=4,'zl'=2,'core'=2] {'x','zh'}, dimensions={0} | all-to-all | bytes 262144 | tf_op jit(solution)/shard_map/all_to_all | solution.py:457
  205.8 11.3 %all_to_all.116.recv_ref = f32[16,32,128]{2,1,0:T(8,128)S(1)} all-to-all(f32[16,32,128]{2,1,0:T(8,128)S(1)} %push.3), channel_id=1, replica_groups=mesh['src'=4,'x'=4,'zh'=4,'zl'=2,'core'=2] {'src','zl','core'}, dimensions={0} | all-to-all | bytes 524288 | tf_op jit(solution)/shard_map/all_to_all | solution.py:461
  218.0 12.9 %all_to_all.117.recv_ref = f32[16,16,128]{2,1,0:T(8,128)S(1)} all-to-all(f32[16,16,128]{2,1,0:T(8,128)S(1)} %pull.4), channel_id=1, replica_groups=mesh['src'=4,'x'=4,'zh'=4,'zl'=2,'core'=2] {'x','zh'}, dimensions={0} | all-to-all | bytes 262144 | tf_op jit(solution)/shard_map/all_to_all | solution.py:457
  231.8 11.3 %all_to_all.118.recv_ref = f32[16,32,128]{2,1,0:T(8,128)S(1)} all-to-all(f32[16,32,128]{2,1,0:T(8,128)S(1)} %push.4), channel_id=1, replica_groups=mesh['src'=4,'x'=4,'zh'=4,'zl'=2,'core'=2] {'src','zl','core'}, dimensions={0} | all-to-all | bytes 524288 | tf_op jit(solution)/shard_map/all_to_all | solution.py:461
  244.1 13.0 %all_to_all.119.recv_ref = f32[16,16,128]{2,1,0:T(8,128)S(1)} all-to-all(f32[16,16,128]{2,1,0:T(8,128)S(1)} %pull.5), channel_id=1, replica_groups=mesh['src'=4,'x'=4,'zh'=4,'zl'=2,'core'=2] {'x','zh'}, dimensions={0} | all-to-all | bytes 262144 | tf_op jit(solution)/shard_map/all_to_all | solution.py:457
  258.0 11.2 %all_to_all.120.recv_ref = f32[16,32,128]{2,1,0:T(8,128)S(1)} all-to-all(f32[16,32,128]{2,1,0:T(8,128)S(1)} %get-tuple-element.59), channel_id=1, replica_groups=mesh['src'=4,'x'=4,'zh'=4,'zl'=2,'core'=2] {'src','zl','core'}, dimensions={0} | all-to-all | bytes 524288 | tf_op jit(solution)/shard_map/all_to_all | solution.py:461
  269.2 4.7 %gradient.1 = (f32[256,256]{1,0:T(8,128)S(1)}, f32[1,128]{1,0:T(1,128)}, f32[8,128]{1,0:T(8,128)}) custom-call(s32[264]{0:T(512)S(4)} %plan.1.list_ref, f32[16,32,128]{2,1,0:T(8,128)S(1)} %all_to_all.120.recv_ref, f32[32,128]{1,0:T(8,128)S(1)} %get-tuple-element.54.sum_ref, f32[32,128]{1,0:T(8,128)S(1)} %get-tuple-element.55.beta_ref, ...), custom_call_target="tpu_custom_call" | custom-call | flops 2097152 | bytes 1048576 | tf_op jit(solution)/shard_map/gradient/pallas_call | solution.py:57
  273.9 10.6 %all_to_all.121 = f32[16,16,256]{2,1,0:T(8,128)S(1)} all-to-all(f32[16,16,256]{2,1,0:T(8,128)S(1)} %bitcast.14), channel_id=1, replica_groups=mesh['src'=4,'x'=4,'zh'=4,'zl'=2,'core'=2] {'src','zl','core'}, dimensions={0} | all-to-all | bytes 524288 | tf_op jit(solution)/shard_map/all_to_all | solution.py:461
  284.6 13.9 %all_to_all.122 = f32[16,16,256]{2,1,0:T(8,128)S(1)} all-to-all(f32[16,16,256]{2,1,0:T(8,128)S(1)} %broadcast_in_dim.15), channel_id=1, replica_groups=mesh['src'=4,'x'=4,'zh'=4,'zl'=2,'core'=2] {'x','zh'}, dimensions={0} | all-to-all | bytes 524288 | tf_op jit(solution)/shard_map/all_to_all | solution.py:457
  298.6 13.2 %all_to_all.123 = f32[16,16,256]{2,1,0:T(8,128)S(1)} all-to-all(f32[16,16,256]{2,1,0:T(8,128)S(1)} %broadcast_in_dim.16), channel_id=1, replica_groups=mesh['src'=4,'x'=4,'zh'=4,'zl'=2,'core'=2] {'src','zl','core'}, dimensions={0} | all-to-all | bytes 524288 | tf_op jit(solution)/shard_map/all_to_all | solution.py:461
  (41 shorter events, 35.6 us)
Async XLA Ops:
  2.2 17.2 %all-to-all-start = ((bf16[4,128,256]{2,1,0:T(8,128)(2,1)}), bf16[4,128,256]{2,1,0:T(8,128)(2,1)S(1)}, u32[]{:S(2)}, u32[]{:S(2)}) async-start(bf16[4,128,256]{2,1,0:T(8,128)(2,1)} %broadcast_in_dim.13), calls=%async_computation | async-start | bytes 524288 | tf_op jit(solution)/shard_map/all_to_all | solution.py:481
  11.2 8.2 %collective-permute-start.3 = (bf16[1024,256]{1,0:T(8,128)(2,1)}, bf16[1024,256]{1,0:T(8,128)(2,1)S(1)}, u32[]{:S(2)}, u32[]{:S(2)}) collective-permute-start(bf16[1024,256]{1,0:T(8,128)(2,1)} %t0.3), channel_id=1, source_target_pairs={{0,1},{1,0},{2,3},{3,2},{4,5},{5,4},{6,7},{7,6},{8,9},{9,8},{10,11... | collective-permute-start | bytes 1572872 | tf_op jit(solution)/shard_map/ppermute | solution.py:453
  14.2 2.8 collective-permute-start
  15.0 3.7 %collective-permute-start.2 = (f32[16,128]{1,0:T(8,128)S(1)}, f32[16,128]{1,0:T(8,128)S(1)}, u32[]{:S(2)}, u32[]{:S(2)}) collective-permute-start(f32[16,128]{1,0:T(8,128)S(1)} %select_maximum_fusion.notes0), channel_id=1, source_target_pairs={{0,1},{1,0},{2,3},{3,2},{4,5},{5,4},{6,7},{7,6},{8,9},{9,8},{10,11... | collective-permute-start | bytes 24584 | tf_op jit(solution)/shard_map/ppermute | solution.py:453
  17.0 1.9 collective-permute-start.1
  19.4 9.3 %collective-permute-start.4 = (bf16[1024,256]{1,0:T(8,128)(2,1)}, bf16[1024,256]{1,0:T(8,128)(2,1)S(1)}, u32[]{:S(2)}, u32[]{:S(2)}) collective-permute-start(bf16[1024,256]{1,0:T(8,128)(2,1)} %t0.3), channel_id=1, source_target_pairs={{0,2},{2,0},{1,3},{3,1},{4,6},{6,4},{5,7},{7,5},{8,10},{10,8},{9,1... | collective-permute-start | bytes 1572872 | tf_op jit(solution)/shard_map/ppermute | solution.py:453
  21.2 15.5 %all-to-all-start.1 = ((bf16[4,4,128,256]{3,2,1,0:T(8,128)(2,1)}), bf16[4,4,128,256]{3,2,1,0:T(8,128)(2,1)S(1)}, u32[]{:S(2)}, u32[]{:S(2)}) async-start(bf16[4,4,128,256]{3,2,1,0:T(8,128)(2,1)} %broadcast_in_dim.14), calls=%async_computation.1 | async-start | bytes 2097152 | tf_op jit(solution)/shard_map/all_to_all | solution.py:493
  28.7 8.0 %collective-permute-start.5 = (bf16[1024,256]{1,0:T(8,128)(2,1)S(1)}, bf16[1024,256]{1,0:T(8,128)(2,1)S(1)}, u32[]{:S(2)}, u32[]{:S(2)}) collective-permute-start(bf16[1024,256]{1,0:T(8,128)(2,1)S(1)} %collective-permute-done.4.t2), channel_id=1, source_target_pairs={{0,1},{1,0},{2,3},{3,2},{4,5},{5,4},{6,7},{7,6},{8,9},{9,8},{10,11... | collective-permute-start | bytes 1572872 | tf_op jit(solution)/shard_map/ppermute | solution.py:453
